TPU v7x, 32 devices: a whole 2x2x4 slice. The times are simulated.
32 devices in a mesh: dp: 32 (over z, y, x, core).
Axes of the slice: x: 2, y: 2, z: 4, core: 2. Of those that a mesh axis runs over, the one named last changes fastest.
Arguments:
- patches: bfloat16 [32768, 768], P('dp'), may hold values from -6 to 6
- img_length: int32 [512], P('dp'), may hold values from 0 to 576, as said below
- img_start: int32 [512], P('dp'), may hold values from 0 to 1024, as said below
- class_count: int32 [32], P('dp'), may hold values from 1 to 63, as said below
- gain_attend: bfloat16 [2, 768], replicated, may hold values from 0.25 to 1.75
- shift_attend: bfloat16 [2, 768], replicated, may hold values from -1 to 1
- qkv_weight: bfloat16 [2, 768, 2304], replicated, may hold values from -0.21875 to 0.21875
- qv_bias: bfloat16 [2, 1536], replicated, may hold values from -1 to 1
- out_weight: bfloat16 [2, 768, 768], replicated, may hold values from -0.875 to 0.875
- out_bias: bfloat16 [2, 768], replicated, may hold values from -1 to 1
- gain_mlp: bfloat16 [2, 768], replicated, may hold values from 0.25 to 1.75
- shift_mlp: bfloat16 [2, 768], replicated, may hold values from -1 to 1
- up_weight: bfloat16 [2, 768, 3072], replicated, may hold values from -0.21875 to 0.21875
- up_bias: bfloat16 [2, 3072], replicated, may hold values from -1 to 1
- down_weight: bfloat16 [2, 3072, 768], replicated, may hold values from -0.109375 to 0.109375
- down_bias: bfloat16 [2, 768], replicated, may hold values from -1 to 1
- cls_weight: bfloat16 [768, 2048], P(None, 'dp'), may hold values from -0.21875 to 0.21875
- cls_bias: bfloat16 [2048], P('dp'), may hold values from -2.5 to 2.5
- logit_grad: bfloat16 [512, 2048], P(None, 'dp'), may hold values from -48 to 48
Outputs:
- logits: float32 [512, 2048], P(None, 'dp')
- patch_grad: float32 [32768, 768], P('dp')
- gain_attend_grad: float32 [2, 768], P(None, 'dp')
- shift_attend_grad: float32 [2, 768], P(None, 'dp')
- qkv_weight_grad: float32 [2, 768, 2304], P(None, 'dp')
- qv_bias_grad: float32 [2, 1536], P(None, 'dp')
- out_weight_grad: float32 [2, 768, 768], P(None, 'dp')
- out_bias_grad: float32 [2, 768], P(None, 'dp')
- gain_mlp_grad: float32 [2, 768], P(None, 'dp')
- shift_mlp_grad: float32 [2, 768], P(None, 'dp')
- up_weight_grad: float32 [2, 768, 3072], P(None, 'dp')
- up_bias_grad: float32 [2, 3072], P(None, 'dp')
- down_weight_grad: float32 [2, 3072, 768], P(None, 'dp')
- down_bias_grad: float32 [2, 768], P(None, 'dp')
- cls_weight_grad: float32 [768, 2048], P(None, 'dp')
- cls_bias_grad: float32 [2048], P('dp')
Inputs may be any that keep to these rules, and one draw needn't show every extreme that they name: `img_length`: each device's 16 slots hold images of 64 or 576 patches, or 0 for an empty slot; a device holds at most one image of 576 patches, in its first slot, and its images take at most 1024 rows. In every draw some device fills all 1024 rows and some device uses all 16 slots. `img_start`: A device's images lie end to end from row 0 in slot order; an empty slot starts where the device's images end. `class_count`: the live columns of a device are the first ones of its 64; the counts of all devices sum to 1024.
All inputs are finite; a program needn't handle non-finite values.
Results may differ from a plain program's by a relative error of at most 0.01.
Values may be sent and summed in bfloat16 or wider, within the bound.
A program may use at most 320 MiB of HBM per device.

v0:
```python
from functools import partial

import jax
import jax.numpy as jnp
from jax import lax
from jax.sharding import PartitionSpec as P

HD = 64
LAYERS = 2
QBLK = 512


EPSILON = 1e-06
HIGHEST = lax.Precision.HIGHEST


def layer_norm(stream, gain_vector, shift_vector):
    center = stream - jnp.mean(stream, axis=-1, keepdims=True)
    spread = jnp.mean(center * center, axis=-1, keepdims=True)
    return center * lax.rsqrt(spread + EPSILON) * gain_vector + shift_vector


def split_heads(joined, model_width):
    row_count = joined.shape[0]
    head_count = model_width // HD
    queries = joined[:, :model_width].reshape(row_count, head_count, HD)
    keys_all = joined[:, model_width : 2 * model_width].reshape(row_count, head_count, HD)
    values_all = joined[:, 2 * model_width :].reshape(row_count, head_count, HD)
    return (queries, keys_all, values_all)


def block_scores(query_piece, keys_all, mask_piece):
    score_scale = query_piece.shape[2] ** (-0.5)
    scores = (
        jnp.einsum("qhd,khd->hqk", query_piece, keys_all, preferred_element_type=jnp.float32)
        * score_scale
    )
    return jnp.where(mask_piece[None], scores, -jnp.inf)


def attend_forward(queries, keys_all, values_all, same_image, block_rows):
    row_count, head_count, head_width = queries.shape
    blocks = row_count // block_rows
    query_blocks = queries.reshape(blocks, block_rows, head_count, head_width)
    mask_blocks = same_image.reshape(blocks, block_rows, row_count)

    def one_block(pieces):
        query_piece, mask_piece = pieces
        scores = block_scores(query_piece, keys_all, mask_piece)
        largest = jnp.max(scores, axis=-1, keepdims=True)
        exponent = jnp.exp(scores - largest)
        totals = jnp.sum(exponent, axis=-1, keepdims=True)
        probabilities = (exponent / totals).astype(jnp.bfloat16)
        mixed_values = jnp.einsum(
            "hqk,khd->qhd", probabilities, values_all, preferred_element_type=jnp.float32
        )
        return (mixed_values.astype(jnp.bfloat16), (largest + jnp.log(totals))[..., 0])

    mixed_values, logsum = lax.map(one_block, (query_blocks, mask_blocks))
    return (mixed_values.reshape(row_count, head_count * head_width), logsum)


def attend_backward(queries, keys_all, values_all, same_image, logsum, grad_attended, block_rows):
    row_count, head_count, head_width = queries.shape
    score_scale = head_width ** (-0.5)
    blocks = row_count // block_rows
    query_blocks = queries.reshape(blocks, block_rows, head_count, head_width)
    mask_blocks = same_image.reshape(blocks, block_rows, row_count)
    grad_blocks = grad_attended.reshape(blocks, block_rows, head_count, head_width)

    def one_block(carry, pieces):
        grad_keys, grad_values = carry
        query_piece, mask_piece, logsum_piece, grad_piece = pieces
        scores = block_scores(query_piece, keys_all, mask_piece)
        probabilities = jnp.exp(scores - logsum_piece[..., None])
        grad_values = grad_values + jnp.einsum(
            "hqk,qhd->khd",
            probabilities.astype(jnp.bfloat16),
            grad_piece,
            preferred_element_type=jnp.float32,
        )
        grad_probs = jnp.einsum(
            "qhd,khd->hqk", grad_piece, values_all, preferred_element_type=jnp.float32
        )
        inner_sums = jnp.sum(probabilities * grad_probs, axis=-1, keepdims=True)
        grad_scores = (probabilities * (grad_probs - inner_sums)).astype(jnp.bfloat16)
        grad_query = (
            jnp.einsum("hqk,khd->qhd", grad_scores, keys_all, preferred_element_type=jnp.float32)
            * score_scale
        )
        grad_keys = (
            grad_keys
            + jnp.einsum(
                "hqk,qhd->khd", grad_scores, query_piece, preferred_element_type=jnp.float32
            )
            * score_scale
        )
        return ((grad_keys, grad_values), grad_query)

    empty = jnp.zeros((row_count, head_count, head_width), jnp.float32)
    carried, grad_queries = lax.scan(
        one_block, (empty, empty), (query_blocks, mask_blocks, logsum, grad_blocks)
    )
    grad_keys, grad_values = carried
    return (
        grad_queries.reshape(row_count, -1),
        grad_keys.reshape(row_count, -1),
        grad_values.reshape(row_count, -1),
    )


def layer_forward(stream, weights, same_image, block_rows):
    (
        gain_one,
        shift_one,
        qkv_w,
        qv_b,
        out_w,
        out_b,
        gain_two,
        shift_two,
        up_w,
        up_b,
        down_w,
        down_b,
    ) = weights
    model_width = stream.shape[1]
    normed = layer_norm(stream, gain_one.astype(jnp.float32), shift_one.astype(jnp.float32)).astype(
        jnp.bfloat16
    )
    bias_full = jnp.concatenate(
        [qv_b[:model_width], jnp.zeros((model_width,), jnp.bfloat16), qv_b[model_width:]]
    ).astype(jnp.float32)
    joined = (jnp.dot(normed, qkv_w, preferred_element_type=jnp.float32) + bias_full).astype(
        jnp.bfloat16
    )
    queries, keys_all, values_all = split_heads(joined, model_width)
    attended, logsum = attend_forward(queries, keys_all, values_all, same_image, block_rows)
    middle = (
        stream
        + jnp.dot(attended, out_w, preferred_element_type=jnp.float32)
        + out_b.astype(jnp.float32)
    )
    normed_two = layer_norm(
        middle, gain_two.astype(jnp.float32), shift_two.astype(jnp.float32)
    ).astype(jnp.bfloat16)
    hidden = jnp.dot(normed_two, up_w, preferred_element_type=jnp.float32) + up_b.astype(
        jnp.float32
    )
    activated = jax.nn.gelu(hidden, approximate=False).astype(jnp.bfloat16)
    output = (
        middle
        + jnp.dot(activated, down_w, preferred_element_type=jnp.float32)
        + down_b.astype(jnp.float32)
    )
    return (
        output,
        (stream, normed, joined, attended, logsum, middle, normed_two, hidden, activated),
    )


def mlp_backward(grad_stream, cache, weights):
    stream, normed, joined, attended, logsum, middle, normed_two, hidden, activated = cache
    (
        gain_one,
        shift_one,
        qkv_w,
        qv_b,
        out_w,
        out_b,
        gain_two,
        shift_two,
        up_w,
        up_b,
        down_w,
        down_b,
    ) = weights
    grad_low = grad_stream.astype(jnp.bfloat16)
    grad_down_w = jnp.einsum("tf,td->fd", activated, grad_low, preferred_element_type=jnp.float32)
    grad_down_b = jnp.sum(grad_low.astype(jnp.float32), axis=0)
    grad_activated = jnp.einsum("td,fd->tf", grad_low, down_w, preferred_element_type=jnp.float32)
    unused, gelu_back = jax.vjp(partial(jax.nn.gelu, approximate=False), hidden)
    grad_hidden = gelu_back(grad_activated)[0].astype(jnp.bfloat16)
    grad_up_w = jnp.einsum("td,tf->df", normed_two, grad_hidden, preferred_element_type=jnp.float32)
    grad_up_b = jnp.sum(grad_hidden.astype(jnp.float32), axis=0)
    grad_normed = jnp.einsum("tf,df->td", grad_hidden, up_w, preferred_element_type=jnp.float32)
    unused, norm_back = jax.vjp(
        layer_norm, middle, gain_two.astype(jnp.float32), shift_two.astype(jnp.float32)
    )
    grad_middle, grad_gain, grad_shift = norm_back(grad_normed)
    return (
        grad_stream + grad_middle,
        (grad_gain, grad_shift, grad_up_w, grad_up_b, grad_down_w, grad_down_b),
    )


def attention_backward(grad_middle, cache, weights, same_image, block_rows):
    stream, normed, joined, attended, logsum, middle, normed_two, hidden, activated = cache
    (
        gain_one,
        shift_one,
        qkv_w,
        qv_b,
        out_w,
        out_b,
        gain_two,
        shift_two,
        up_w,
        up_b,
        down_w,
        down_b,
    ) = weights
    model_width = stream.shape[1]
    grad_low = grad_middle.astype(jnp.bfloat16)
    grad_out_w = jnp.einsum("tc,td->cd", attended, grad_low, preferred_element_type=jnp.float32)
    grad_out_b = jnp.sum(grad_low.astype(jnp.float32), axis=0)
    grad_attended = jnp.einsum(
        "td,cd->tc", grad_low, out_w, preferred_element_type=jnp.float32
    ).astype(jnp.bfloat16)
    queries, keys_all, values_all = split_heads(joined, model_width)
    grad_heads = grad_attended.reshape(queries.shape)
    grad_queries, grad_keys, grad_values = attend_backward(
        queries, keys_all, values_all, same_image, logsum, grad_heads, block_rows
    )
    grad_joined = jnp.concatenate([grad_queries, grad_keys, grad_values], axis=1).astype(
        jnp.bfloat16
    )
    grad_qkv_w = jnp.einsum("td,te->de", normed, grad_joined, preferred_element_type=jnp.float32)
    column_sums = jnp.sum(grad_joined.astype(jnp.float32), axis=0)
    grad_qv_b = jnp.concatenate([column_sums[:model_width], column_sums[2 * model_width :]])
    grad_normed = jnp.einsum("te,de->td", grad_joined, qkv_w, preferred_element_type=jnp.float32)
    unused, norm_back = jax.vjp(
        layer_norm, stream, gain_one.astype(jnp.float32), shift_one.astype(jnp.float32)
    )
    grad_input, grad_gain, grad_shift = norm_back(grad_normed)
    return (
        grad_middle + grad_input,
        (grad_gain, grad_shift, grad_qkv_w, grad_qv_b, grad_out_w, grad_out_b),
    )


def local(
    patches,
    img_length,
    img_start,
    class_count,
    gain_attend,
    shift_attend,
    qkv_weight,
    qv_bias,
    out_weight,
    out_bias,
    gain_mlp,
    shift_mlp,
    up_weight,
    up_bias,
    down_weight,
    down_bias,
    cls_weight,
    cls_bias,
    logit_grad,
):
    row_count = patches.shape[0]
    slot_count = img_length.shape[0]
    block_rows = min(QBLK, row_count)
    positions = jnp.arange(row_count, dtype=jnp.int32)
    inside = (positions[None, :] >= img_start[:, None]) & (
        positions[None, :] < (img_start + img_length)[:, None]
    )
    member = inside.astype(jnp.float32)
    live_rows = jnp.sum(inside.astype(jnp.int32), axis=0)
    segment = (
        jnp.sum(inside.astype(jnp.int32) * jnp.arange(slot_count, dtype=jnp.int32)[:, None], axis=0)
        + (1 - live_rows) * slot_count
    )
    same_image = segment[:, None] == segment[None, :]
    stacked = (
        gain_attend,
        shift_attend,
        qkv_weight,
        qv_bias,
        out_weight,
        out_bias,
        gain_mlp,
        shift_mlp,
        up_weight,
        up_bias,
        down_weight,
        down_bias,
    )
    stream = patches.astype(jnp.float32)
    caches = []
    for layer_index in range(LAYERS):
        weights = tuple((weight[layer_index] for weight in stacked))
        stream, cache = layer_forward(stream, weights, same_image, block_rows)
        caches.append(cache)
    counts = jnp.maximum(img_length, 1).astype(jnp.float32)
    pooled = (
        jnp.dot(member, stream, precision=HIGHEST, preferred_element_type=jnp.float32)
        / counts[:, None]
    )
    gathered = lax.all_gather(pooled.astype(jnp.bfloat16), "dp", axis=0, tiled=True)
    live_columns = jnp.arange(cls_weight.shape[1], dtype=jnp.int32) < class_count[0]
    scores = jnp.dot(gathered, cls_weight, preferred_element_type=jnp.float32) + cls_bias.astype(
        jnp.float32
    )
    logits = jnp.where(live_columns[None, :], scores, 0.0)
    masked_grad = jnp.where(live_columns[None, :], logit_grad, jnp.zeros_like(logit_grad))
    grad_cls_weight = jnp.einsum(
        "id,ic->dc", gathered, masked_grad, preferred_element_type=jnp.float32
    )
    grad_cls_bias = jnp.sum(masked_grad.astype(jnp.float32), axis=0)
    pooled_grad = lax.psum_scatter(
        jnp.einsum("ic,dc->id", masked_grad, cls_weight, preferred_element_type=jnp.float32),
        "dp",
        scatter_dimension=0,
        tiled=True,
    )
    grad_stream = jnp.einsum(
        "it,id->td",
        member,
        pooled_grad / counts[:, None],
        precision=HIGHEST,
        preferred_element_type=jnp.float32,
    )
    ordered = []
    for layer_index in reversed(range(LAYERS)):
        weights = tuple((weight[layer_index] for weight in stacked))
        grad_stream, mlp_terms = mlp_backward(grad_stream, caches[layer_index], weights)
        grad_stream, attend_terms = attention_backward(
            grad_stream, caches[layer_index], weights, same_image, block_rows
        )
        layer_terms = tuple(attend_terms) + tuple(mlp_terms)
        ordered.insert(0, tuple(layer_terms))
    stacked_terms = tuple(
        (jnp.stack([layer_terms[position] for layer_terms in ordered]) for position in range(12))
    )
    final_terms = (
        lax.psum_scatter(stacked_terms[0], "dp", scatter_dimension=1, tiled=True),
        lax.psum_scatter(stacked_terms[1], "dp", scatter_dimension=1, tiled=True),
        lax.psum_scatter(stacked_terms[2], "dp", scatter_dimension=1, tiled=True),
        lax.psum_scatter(stacked_terms[3], "dp", scatter_dimension=1, tiled=True),
        lax.psum_scatter(stacked_terms[4], "dp", scatter_dimension=1, tiled=True),
        lax.psum_scatter(stacked_terms[5], "dp", scatter_dimension=1, tiled=True),
        lax.psum_scatter(stacked_terms[6], "dp", scatter_dimension=1, tiled=True),
        lax.psum_scatter(stacked_terms[7], "dp", scatter_dimension=1, tiled=True),
        lax.psum_scatter(stacked_terms[8], "dp", scatter_dimension=1, tiled=True),
        lax.psum_scatter(stacked_terms[9], "dp", scatter_dimension=1, tiled=True),
        lax.psum_scatter(stacked_terms[10], "dp", scatter_dimension=1, tiled=True),
        lax.psum_scatter(stacked_terms[11], "dp", scatter_dimension=1, tiled=True),
    )
    return (logits, grad_stream) + tuple(final_terms) + (grad_cls_weight, grad_cls_bias)


def solution(mesh):
    placed = (
        P("dp", None),
        P("dp"),
        P("dp"),
        P("dp"),
        P(),
        P(),
        P(),
        P(),
        P(),
        P(),
        P(),
        P(),
        P(),
        P(),
        P(),
        P(),
        P(None, "dp"),
        P("dp"),
        P(None, "dp"),
    )
    return jax.shard_map(
        local,
        mesh=mesh,
        in_specs=placed,
        out_specs=(
            P(None, "dp"),
            P("dp", None),
            P(None, "dp"),
            P(None, "dp"),
            P(None, "dp", None),
            P(None, "dp"),
            P(None, "dp", None),
            P(None, "dp"),
            P(None, "dp"),
            P(None, "dp"),
            P(None, "dp", None),
            P(None, "dp"),
            P(None, "dp", None),
            P(None, "dp"),
            P(None, "dp"),
            P("dp"),
        ),
        check_vma=False,
    )
```

profile of v0, /device:TPU:0, one launch (start us, length us, event | category | flops | bytes accessed | tf_op | source)
XLA Modules:
  0.0 1705.5 jit_solution(15348567799914056488)
XLA Ops:
  36.5 72.9 %while.54 = (s32[]{:T(128)}, bf16[2,512,12,64]{1,3,2,0:T(8,128)(2,1)}, f32[2,12,512]{2,1,0:T(8,128)S(1)}, pred[2,512,1024]{2,1,0:T(8,128)(4,1)S(1)}, bf16[2,512,...) while((s32[]{:T(128)}, ...), condition=%wide.region_7.8_spmd, body=%wide.region_4.7_spmd.sunk | while | flops 1686497280 | bytes 190014608 | solution.py:59
  120.2 36.6 %multiply_convert_fusion.3 = (bf16[1024,3072]{1,0:T(8,128)(2,1)}, f32[1024,3072]{1,0:T(8,128)}, f32[1024,3072]{1,0:T(8,128)}) fusion(f32[3072]{0:T(1024)S(1)} %bitcast.365, bf16[2,768,3072]{2,1,0:T(8,128)(2,1)S(1)} %bitcast.371, f32[1024,768]{0,1:T(8,128)S(1)} %get-tuple-element.615, f32[768]{0:T(1024)S(1)} %get-tuple-element.493, ...), kind=kOutput, calls=%fused_computation.112 | convolution fusion | flops 5043388416 | bytes 39350272 | tf_op jit(solution)/shard_map/dot_general | solution.py:147
  185.3 72.1 %while.55 = (s32[]{:T(128)}, bf16[2,512,12,64]{1,3,2,0:T(8,128)(2,1)}, f32[2,12,512]{2,1,0:T(8,128)S(1)}, pred[2,512,1024]{2,1,0:T(8,128)(4,1)S(1)}, bf16[2,512,...) while((s32[]{:T(128)}, ...), condition=%wide.region_15.16_spmd, body=%wide.region_12.15_spmd.sunk | while | flops 1686497280 | bytes 190014608 | solution.py:59
  267.4 37.0 %multiply_convert_fusion.2 = (bf16[1024,3072]{1,0:T(8,128)(2,1)}, f32[1024,3072]{1,0:T(8,128)}, f32[1024,3072]{1,0:T(8,128)}) fusion(f32[3072]{0:T(1024)S(1)} %bitcast.368, bf16[2,768,3072]{2,1,0:T(8,128)(2,1)S(1)} %bitcast.373, f32[1024,768]{0,1:T(8,128)S(1)} %get-tuple-element.620, f32[768]{0:T(1024)S(1)} %copy-done.144, f32[768]{0:T(1024)S(1)} %copy-done.94, ...), kind=kOutput, calls=%fused_computation.99 | convolution fusion | flops 5043388416 | bytes 39350272 | tf_op jit(solution)/shard_map/dot_general | solution.py:147
  312.5 19.3 %convert_reduce_fusion = (f32[3072]{0:T(1024)}, bf16[1024,3072]{1,0:T(8,128)(2,1)}) fusion(f32[1024,3072]{1,0:T(8,128)} %get-tuple-element.587, bf16[2,3072,768]{2,1,0:T(8,128)(2,1)} %param.41, f32[1024,768]{1,0:T(8,128)} %get-tuple-element.631, f32[1024,3072]{1,0:T(8,128)} %get-tuple-element.621, f32[3072]{0:T(1024)S(1)} %bitcast.369), kind=kOutput, calls=%fused_computation.95 | convolution fusion | flops 4886098944 | bytes 39346176 | tf_op jit(solution)/shard_map/td,fd->tf/dot_general | solution.py:181
  364.8 167.3 %while.56 = (s32[]{:T(128)}, f32[1024,12,64]{0,2,1:T(8,128)}, f32[1024,12,64]{0,2,1:T(8,128)}, bf16[2,512,12,64]{1,3,2,0:T(8,128)(2,1)}, bf16[2,512,12,64]{1,3,2...) while((s32[]{:T(128)}, f32[1024,12,64]{0,2,1:T(8,128)}, ...), condition=%wide.region_23.24_spmd.clone, body=%wide.region_21.23_spmd.clone.sunk | while | flops 4125222912 | bytes 213559952 | solution.py:101
  376.4 18.0 %multiply_reduce_fusion.13 = (f32[12,512]{1,0:T(8,128)S(1)}, f32[12,512,1024]{2,1,0:T(8,128)}) fusion(f32[12,512,1024]{2,1,0:T(8,128)} %fusion.271, f32[12,512]{1,0:T(8,128)S(1)} %dynamic-slice_bitcast_fusion.14, pred[512,1024]{1,0:T(8,128)(4,1)S(1)} %dynamic-slice_bitcast_fusion.15, bf16[1024,12,64]{0,2,1:T(8,128)(2,1)} %get-tuple-element.943, ...), kind=kOutput, calls=%fused_computation.35.clone.1 | convolution fusion | flops 836757504 | bytes 53264896 | tf_op jit(solution)/shard_map/while/body/eval_jaxpr/qhd,khd->hqk/dot_general | solution.py:82
  394.4 21.3 %multiply_convert_fusion.6 = bf16[12,512,1024]{2,1,0:T(8,128)(2,1)} fusion(f32[12,512,1024]{2,1,0:T(8,128)} %get-tuple-element.848, f32[12,512,1024]{2,1,0:T(8,128)} %fusion.271, f32[12,512]{1,0:T(8,128)S(1)} %get-tuple-element.849, f32[12,512]{1,0:T(8,128)S(1)} %dynamic-slice_bitcast_fusion.14, pred[512,1024]{1,0:T(8,128)(4,1)S(1)} %dynamic-slice_bitcast_fusion.15), kind=kLoop, calls=%fused_computation.34.clone.1 | loop fusion | flops 37748736 | bytes 63488000 | tf_op jit(solution)/shard_map/while/body/eval_jaxpr/convert_element_type | solution.py:86
  458.8 18.0 %multiply_reduce_fusion.13 = (f32[12,512]{1,0:T(8,128)S(1)}, f32[12,512,1024]{2,1,0:T(8,128)}) fusion(f32[12,512,1024]{2,1,0:T(8,128)} %fusion.271, f32[12,512]{1,0:T(8,128)S(1)} %dynamic-slice_bitcast_fusion.14, pred[512,1024]{1,0:T(8,128)(4,1)S(1)} %dynamic-slice_bitcast_fusion.15, bf16[1024,12,64]{0,2,1:T(8,128)(2,1)} %get-tuple-element.943, ...), kind=kOutput, calls=%fused_computation.35.clone.1 | convolution fusion | flops 836757504 | bytes 53264896 | tf_op jit(solution)/shard_map/while/body/eval_jaxpr/qhd,khd->hqk/dot_general | solution.py:82
  476.8 21.3 %multiply_convert_fusion.6 = bf16[12,512,1024]{2,1,0:T(8,128)(2,1)} fusion(f32[12,512,1024]{2,1,0:T(8,128)} %get-tuple-element.848, f32[12,512,1024]{2,1,0:T(8,128)} %fusion.271, f32[12,512]{1,0:T(8,128)S(1)} %get-tuple-element.849, f32[12,512]{1,0:T(8,128)S(1)} %dynamic-slice_bitcast_fusion.14, pred[512,1024]{1,0:T(8,128)(4,1)S(1)} %dynamic-slice_bitcast_fusion.15), kind=kLoop, calls=%fused_computation.34.clone.1 | loop fusion | flops 37748736 | bytes 63488000 | tf_op jit(solution)/shard_map/while/body/eval_jaxpr/convert_element_type | solution.py:86
  517.2 14.5 bitcast_add_fusion.9
  561.1 18.7 %convert_reduce_fusion.1 = (f32[3072]{0:T(1024)}, bf16[1024,3072]{1,0:T(8,128)(2,1)}) fusion(f32[1024,3072]{1,0:T(8,128)} %get-tuple-element.589, bf16[2,3072,768]{2,1,0:T(8,128)(2,1)} %param.41, f32[1024,768]{0,1:T(8,128)S(1)} %get-tuple-element.577, f32[1024,3072]{1,0:T(8,128)} %get-tuple-element.616, f32[3072]{0:T(1024)S(1)} %bitcast.366), kind=kOutput, calls=%fused_computation.96 | convolution fusion | flops 4886098944 | bytes 39346176 | tf_op jit(solution)/shard_map/td,fd->tf/dot_general | solution.py:181
  617.4 167.1 %while.57 = (s32[]{:T(128)}, f32[1024,12,64]{0,2,1:T(8,128)}, f32[1024,12,64]{0,2,1:T(8,128)}, bf16[2,512,12,64]{1,3,2,0:T(8,128)(2,1)}, bf16[2,512,12,64]{1,3,2...) while((s32[]{:T(128)}, f32[1024,12,64]{0,2,1:T(8,128)}, ...), condition=%wide.region_30.31_spmd.clone, body=%wide.region_28.30_spmd.clone.sunk | while | flops 4125222912 | bytes 213559952 | solution.py:101
  629.2 18.0 %multiply_reduce_fusion.14 = (f32[12,512]{1,0:T(8,128)S(1)}, f32[12,512,1024]{2,1,0:T(8,128)}) fusion(f32[12,512,1024]{2,1,0:T(8,128)} %fusion.281, f32[12,512]{1,0:T(8,128)S(1)} %dynamic-slice_bitcast_fusion.16, pred[512,1024]{1,0:T(8,128)(4,1)S(1)} %dynamic-slice_bitcast_fusion.17, bf16[1024,12,64]{0,2,1:T(8,128)(2,1)} %get-tuple-element.979, ...), kind=kOutput, calls=%fused_computation.62.clone.1 | convolution fusion | flops 836757504 | bytes 53264896 | tf_op jit(solution)/shard_map/while/body/eval_jaxpr/qhd,khd->hqk/dot_general | solution.py:82
  647.2 21.2 %multiply_convert_fusion.7 = bf16[12,512,1024]{2,1,0:T(8,128)(2,1)} fusion(f32[12,512,1024]{2,1,0:T(8,128)} %get-tuple-element.860, f32[12,512,1024]{2,1,0:T(8,128)} %fusion.281, f32[12,512]{1,0:T(8,128)S(1)} %get-tuple-element.861, f32[12,512]{1,0:T(8,128)S(1)} %dynamic-slice_bitcast_fusion.16, pred[512,1024]{1,0:T(8,128)(4,1)S(1)} %dynamic-slice_bitcast_fusion.17), kind=kLoop, calls=%fused_computation.61.clone.1 | loop fusion | flops 37748736 | bytes 63488000 | tf_op jit(solution)/shard_map/while/body/eval_jaxpr/convert_element_type | solution.py:86
  711.6 18.0 %multiply_reduce_fusion.14 = (f32[12,512]{1,0:T(8,128)S(1)}, f32[12,512,1024]{2,1,0:T(8,128)}) fusion(f32[12,512,1024]{2,1,0:T(8,128)} %fusion.281, f32[12,512]{1,0:T(8,128)S(1)} %dynamic-slice_bitcast_fusion.16, pred[512,1024]{1,0:T(8,128)(4,1)S(1)} %dynamic-slice_bitcast_fusion.17, bf16[1024,12,64]{0,2,1:T(8,128)(2,1)} %get-tuple-element.979, ...), kind=kOutput, calls=%fused_computation.62.clone.1 | convolution fusion | flops 836757504 | bytes 53264896 | tf_op jit(solution)/shard_map/while/body/eval_jaxpr/qhd,khd->hqk/dot_general | solution.py:82
  729.6 21.2 %multiply_convert_fusion.7 = bf16[12,512,1024]{2,1,0:T(8,128)(2,1)} fusion(f32[12,512,1024]{2,1,0:T(8,128)} %get-tuple-element.860, f32[12,512,1024]{2,1,0:T(8,128)} %fusion.281, f32[12,512]{1,0:T(8,128)S(1)} %get-tuple-element.861, f32[12,512]{1,0:T(8,128)S(1)} %dynamic-slice_bitcast_fusion.16, pred[512,1024]{1,0:T(8,128)(4,1)S(1)} %dynamic-slice_bitcast_fusion.17), kind=kLoop, calls=%fused_computation.61.clone.1 | loop fusion | flops 37748736 | bytes 63488000 | tf_op jit(solution)/shard_map/while/body/eval_jaxpr/convert_element_type | solution.py:86
  769.9 14.5 bitcast_add_fusion.11
  887.9 45.6 %all_gather.3 = bf16[512,768]{1,0:T(8,128)(2,1)S(1)} all-gather(bf16[16,768]{1,0:T(8,128)(2,1)S(1)} %fusion.140), channel_id=1, replica_groups=mesh['dp'=32] {'dp'}, dimensions={0}, use_global_device_ids=true | all-gather | bytes 811008 | tf_op jit(solution)/shard_map/all_gather | solution.py:302
  958.8 37.7 %all-reduce.6 = (f32[2,768]{1,0:T(2,128)S(1)}, f32[2,768]{1,0:T(2,128)S(1)}, f32[2,768]{1,0:T(2,128)S(1)}, f32[2,768]{1,0:T(2,128)S(1)}, f32[2,768]{1,0:T(2,128)S(1)}, /*index=5*/f32[2,768]{1,0:T(2,128)S(1)}) all-reduce(f32[2,768]{1,0:T(2,128)S(1)} %pad_maximum_fusion.12, ...), channel_id=3, replica_groups=mesh['dp'=32] {'dp'}, use_global_device_ids=true, to_apply=%region_35.36.clone | all-reduce | flops 9216 | bytes 73728
  1003.2 104.7 %reduce-scatter.22.cloned.1.call-done = f32[2,24,768]{2,1,0:T(8,128)} async-done(((f32[2,768,768]{2,1,0:T(8,128)}), f32[2,24,768]{2,1,0:T(8,128)}) %reduce-scatter.22.cloned.1.call-update) | async-done | bytes 147472 | tf_op jit(solution)/shard_map/reduce_scatter | solution.py:343
  1107.8 168.0 %reduce-scatter.20.cloned.1.call-done = f32[2,24,2304]{2,1,0:T(8,128)} async-done(((f32[2,768,2304]{2,1,0:T(8,128)}), f32[2,24,2304]{2,1,0:T(8,128)}) %reduce-scatter.20.cloned.1.call-update) | async-done | bytes 442384 | tf_op jit(solution)/shard_map/reduce_scatter | solution.py:341
  1275.9 211.0 %reduce-scatter.26.cloned.1.call-done = f32[2,96,768]{2,1,0:T(8,128)} async-done(((f32[2,3072,768]{2,1,0:T(8,128)}), f32[2,96,768]{2,1,0:T(8,128)}) %reduce-scatter.26.cloned.1.call-update) | async-done | bytes 589840 | tf_op jit(solution)/shard_map/reduce_scatter | solution.py:349
  1486.9 211.3 %reduce-scatter.24.cloned.1.call-done = f32[2,24,3072]{2,1,0:T(8,128)} async-done(((f32[2,768,3072]{2,1,0:T(8,128)}), f32[2,24,3072]{2,1,0:T(8,128)}) %reduce-scatter.24.cloned.1.call-update) | async-done | bytes 589840 | tf_op jit(solution)/shard_map/reduce_scatter | solution.py:347
  (566 shorter events, 610.4 us)
Async XLA Ops:
  7.2 297.3 %reduce-scatter.18.cloned.1.call-start = ((), (), s32[]{:S(2)}) async-start(), calls=%async_computation.7 | async-start | bytes 1622016 | tf_op jit(solution)/shard_map/reduce_scatter | solution.py:313
  11.0 989.3 %reduce-scatter.28.cloned.1.call-start = ((), (), s32[]{:S(2)}) async-start(), calls=%async_computation.12 | async-start | bytes 811008
  115.9 40.9 %copy-start.27 = (f32[1024,768]{0,1:T(8,128)}, f32[1024,768]{0,1:T(8,128)S(1)}, u32[]{:S(2)}) copy-start(f32[1024,768]{0,1:T(8,128)S(1)} %get-tuple-element.615) | copy-start | bytes 9437188
  116.0 40.8 %copy-start.75 = (f32[1024]{0:T(1024)}, f32[1024]{0:T(1024)S(1)}, u32[]{:S(2)}) copy-start(f32[1024]{0:T(1024)S(1)} %broadcast_multiply_fusion.2) | copy-start | bytes 12292
  116.4 40.4 %copy-start.90 = (f32[1024]{0:T(1024)}, f32[1024]{0:T(1024)S(1)}, u32[]{:S(2)}) copy-start(f32[1024]{0:T(1024)S(1)} %multiply_reduce_fusion.10) | copy-start | bytes 12292
  118.3 38.5 %copy-start.99 = (f32[1024]{0:T(1024)}, f32[1024]{0:T(1024)S(1)}, u32[]{:S(2)}) copy-start(f32[1024]{0:T(1024)S(1)} %fusion.159) | copy-start | bytes 12292
  118.9 37.9 %copy-start.126 = (f32[1,3072]{1,0:T(1,128)}, f32[1,3072]{1,0:T(1,128)S(1)}, u32[]{:S(2)}) copy-start(f32[1,3072]{1,0:T(1,128)S(1)} %get-tuple-element.609) | copy-start | bytes 36868
  263.5 85.7 %copy-start.20 = (f32[1024,768]{0,1:T(8,128)}, f32[1024,768]{0,1:T(8,128)S(1)}, u32[]{:S(2)}) copy-start(f32[1024,768]{0,1:T(8,128)S(1)} %get-tuple-element.620) | copy-start | bytes 9437188
  263.6 85.7 %copy-start.78 = (f32[1024]{0:T(1024)}, f32[1024]{0:T(1024)S(1)}, u32[]{:S(2)}) copy-start(f32[1024]{0:T(1024)S(1)} %broadcast_multiply_fusion) | copy-start | bytes 12292
  264.0 85.3 %copy-start.102 = (f32[1024]{0:T(1024)}, f32[1024]{0:T(1024)S(1)}, u32[]{:S(2)}) copy-start(f32[1024]{0:T(1024)S(1)} %fusion.161) | copy-start | bytes 12292
  793.9 207.8 %reduce-scatter.30.cloned.1.call-start = ((), (), s32[]{:S(2)}) async-start(), calls=%async_computation.13 | async-start | bytes 1622016
  795.7 312.1 %reduce-scatter.22.cloned.1.call-start = ((), (), s32[]{:S(2)}) async-start(), calls=%async_computation.9 | async-start | bytes 4866048 | tf_op jit(solution)/shard_map/reduce_scatter | solution.py:343
  800.0 475.9 %reduce-scatter.20.cloned.1.call-start = ((), (), s32[]{:S(2)}) async-start(), calls=%async_computation.8 | async-start | bytes 14598144 | tf_op jit(solution)/shard_map/reduce_scatter | solution.py:341
  828.9 658.0 %reduce-scatter.26.cloned.1.call-start = ((), (), s32[]{:S(2)}) async-start(), calls=%async_computation.11 | async-start | bytes 19464192 | tf_op jit(solution)/shard_map/reduce_scatter | solution.py:349
  851.8 846.4 %reduce-scatter.24.cloned.1.call-start = ((), (), s32[]{:S(2)}) async-start(), calls=%async_computation.10 | async-start | bytes 19464192 | tf_op jit(solution)/shard_map/reduce_scatter | solution.py:347
  886.0 49.5 %copy-start.151 = (f32[768]{0:T(1024)S(1)}, f32[768]{0:T(1024)}, u32[]{:S(2)}) copy-start(f32[768]{0:T(1024)} %get-tuple-element.628) | copy-start | bytes 9220
  886.0 49.5 %copy-start.149 = (f32[768]{0:T(1024)S(1)}, f32[768]{0:T(1024)}, u32[]{:S(2)}) copy-start(f32[768]{0:T(1024)} %get-tuple-element.626) | copy-start | bytes 9220
  886.0 49.5 %copy-start.117 = (f32[768]{0:T(1024)S(1)}, f32[768]{0:T(1024)}, u32[]{:S(2)}) copy-start(f32[768]{0:T(1024)} %get-tuple-element.478) | copy-start | bytes 9220
  886.1 49.5 %copy-start.116 = (f32[768]{0:T(1024)S(1)}, f32[768]{0:T(1024)}, u32[]{:S(2)}) copy-start(f32[768]{0:T(1024)} %get-tuple-element.480) | copy-start | bytes 9220
  886.1 49.5 %copy-start.115 = (f32[768]{0:T(1024)S(1)}, f32[768]{0:T(1024)}, u32[]{:S(2)}) copy-start(f32[768]{0:T(1024)} %get-tuple-element.578) | copy-start | bytes 9220
  886.1 49.5 %copy-start.112 = (f32[768]{0:T(1024)S(1)}, f32[768]{0:T(1024)}, u32[]{:S(2)}) copy-start(f32[768]{0:T(1024)} %get-tuple-element.580) | copy-start | bytes 9220
  886.1 49.5 %copy-start.43 = (bf16[96,8,2,512]{3,1,2,0:T(8,128)(2,1)S(1)}, bf16[96,8,2,512]{3,1,2,0:T(8,128)(2,1)}, u32[]{:S(2)}) copy-start(bf16[96,8,2,512]{3,1,2,0:T(8,128)(2,1)} %copy-done.42) | copy-start | bytes 4718596
  886.1 49.5 %copy-start.51 = (bf16[1024,12,64]{0,2,1:T(8,128)(2,1)S(1)}, bf16[1024,12,64]{0,2,1:T(8,128)(2,1)}, u32[]{:S(2)}) copy-start(bf16[1024,12,64]{0,2,1:T(8,128)(2,1)} %copy-done.50) | copy-start | bytes 4718596
  886.1 49.5 %copy-start.53 = (bf16[1024,12,64]{0,2,1:T(8,128)(2,1)S(1)}, bf16[1024,12,64]{0,2,1:T(8,128)(2,1)}, u32[]{:S(2)}) copy-start(bf16[1024,12,64]{0,2,1:T(8,128)(2,1)} %copy-done.52) | copy-start | bytes 4718596
  (153 other events, 961.2 us)
Sparse Core Ops, SparseCore 0:
  13.3 100.6 reduce-scatter.17
  794.0 98.9 reduce-scatter.27
  898.2 97.0 reduce-scatter.29
  1001.2 106.5 reduce-scatter.21
  1114.3 161.5 reduce-scatter.19
  1282.7 204.1 reduce-scatter.25
  1493.9 204.2 reduce-scatter.23
where the time goes:
time: 1720 us; the launch traced here: 1710 us
  waiting for transfers between devices  695 us (40%)
  matrix products  580 us (34%)
  other arithmetic  201 us (12%)
  local copies, waits for them, and re-layouts  126 us (7%)
  blocking collectives  83.3 us (5%)
  between operations  17.5 us (1%)
    reduce_scatter x1, waiting for transfers between devices, local(): lax.psum_scatter(stacked_terms[8], 'dp', scatter_dimension=1, tiled=True)  211 us
    reduce_scatter x1, waiting for transfers between devices, local(): lax.psum_scatter(stacked_terms[10], 'dp', scatter_dimension=1, tiled=True)  211 us
    reduce_scatter x1, waiting for transfers between devices, local(): lax.psum_scatter(stacked_terms[2], 'dp', scatter_dimension=1, tiled=True)  168 us
    reduce_scatter x1, waiting for transfers between devices, local(): lax.psum_scatter(stacked_terms[4], 'dp', scatter_dimension=1, tiled=True)  105 us
    dot_general x8, matrix products, block_scores(): jnp.einsum('qhd,khd->hqk', query_piece, keys_all, preferred_element_type=...  93.7 us
    convert_element_type x4, other arithmetic, one_block(): (probabilities * (grad_probs - inner_sums)).astype(jnp.bfloat16)  84.9 us
    dot_general x2, matrix products, layer_forward(): jnp.dot(normed_two, up_w, preferred_element_type=jnp.float32)  73.6 us
    dot_general x4, matrix products, one_block(): jnp.einsum('qhd,khd->hqk', grad_piece, values_all, preferred_element_type...  72 us
  transfers between devices with their start and end apart: 7, of which 4 were waited for; matrix products, arithmetic and copies ran while one was open for 23% of the time, Pallas kernels for 0%

commit v1 on v0

v1 whole, which is shorter than its diff:
```python
from functools import partial

import jax
import jax.numpy as jnp
from jax import lax
from jax.experimental import pallas as pl
from jax.experimental.pallas import tpu as pltpu
from jax.sharding import PartitionSpec as P

HD = 64
LAYERS = 2
BIG = 1e30
EPSILON = 1e-06
HIGHEST = lax.Precision.HIGHEST
NT = (((1,), (1,)), ((), ()))
f32 = jnp.float32
bf16 = jnp.bfloat16
VMEM_LIMIT = 56 << 20


def layer_norm(stream, gain_vector, shift_vector):
    center = stream - jnp.mean(stream, axis=-1, keepdims=True)
    spread = jnp.mean(center * center, axis=-1, keepdims=True)
    return center * lax.rsqrt(spread + EPSILON) * gain_vector + shift_vector


def dot32(left, right):
    return jnp.dot(left, right, preferred_element_type=f32)


def dot_nt(left, right):
    return lax.dot_general(left, right, NT, preferred_element_type=f32)


def seg_features(segment, slot_count):
    lane = jnp.arange(128, dtype=jnp.int32) % HD
    hit = segment[:, None] == lane[None, :]
    live = (lane <= slot_count)[None, :]
    query_side = (hit & live).astype(bf16)
    key_side = jnp.where(live & ~hit, -BIG, 0.0).astype(bf16)
    return query_side, key_side


def attend_forward_kernel(q_ref, k_ref, v_ref, fq_ref, fk_ref, o_ref, lse_ref, *, chunk):
    rows = q_ref.shape[0]
    left = lax.broadcasted_iota(jnp.int32, (rows, 128), 1) < HD
    q = q_ref[...] * jnp.asarray(HD**-0.5, bf16)
    k = k_ref[...]
    fq = fq_ref[...]
    fk = fk_ref[...]
    v_t = v_ref[...].T
    q_side = [jnp.where(left, q, fq), jnp.where(left, fq, q)]
    k_side = [jnp.where(left, k, fk), jnp.where(left, fk, k)]
    for c in range(rows // chunk):
        span = slice(c * chunk, (c + 1) * chunk)
        outs = []
        for h in range(2):
            scores = dot_nt(k_side[h], q_side[h][span])
            largest = jnp.max(scores, axis=0, keepdims=True)
            p = jnp.exp(scores - largest)
            total = jnp.sum(p, axis=0, keepdims=True)
            mixed = dot32(v_t[h * HD : (h + 1) * HD], p.astype(bf16))
            outs.append(mixed / total)
            lse_ref[0, h : h + 1, span] = largest + jnp.log(total)
        o_ref[span, :] = jnp.concatenate(outs, axis=0).T.astype(bf16)


def attend_forward(joined, fq, fk):
    rows = joined.shape[0]
    width = joined.shape[1] // 3
    n = width // 128
    col = lambda off: pl.BlockSpec((rows, 128), lambda i, off=off: (0, off + i))
    full = pl.BlockSpec((rows, 128), lambda i: (0, 0))
    return pl.pallas_call(
        partial(attend_forward_kernel, chunk=rows),
        grid=(n,),
        in_specs=[col(0), col(n), col(2 * n), full, full],
        out_specs=[
            pl.BlockSpec((rows, 128), lambda i: (0, i)),
            pl.BlockSpec((1, 2, rows), lambda i: (i, 0, 0)),
        ],
        out_shape=[
            jax.ShapeDtypeStruct((rows, width), bf16),
            jax.ShapeDtypeStruct((n, 2, rows), f32),
        ],
        compiler_params=pltpu.CompilerParams(vmem_limit_bytes=VMEM_LIMIT),
        cost_estimate=pl.CostEstimate(
            flops=16 * rows * rows * width, bytes_accessed=10 * rows * width, transcendentals=0
        ),
        name="attend_forward",
    )(joined, joined, joined, fq, fk)


def attend_backward_kernel(
    q_ref, k_ref, v_ref, g_ref, o_ref, lse_ref, fq_ref, fk_ref, dj_ref, cs_ref, *, chunk
):
    rows = q_ref.shape[0]
    width = dj_ref.shape[1] // 3
    step = pl.program_id(0)
    left = lax.broadcasted_iota(jnp.int32, (rows, 128), 1) < HD
    left_chunk = left[:chunk]
    scale = HD**-0.5
    q = q_ref[...] * jnp.asarray(scale, bf16)
    k = k_ref[...]
    v = v_ref[...]
    g = g_ref[...]
    fq = fq_ref[...]
    fk = fk_ref[...]
    zero = jnp.zeros_like(q)
    k_t = k.T
    product_t = (g.astype(f32) * o_ref[...].astype(f32)).T
    q_side = [jnp.where(left, q, fq), jnp.where(left, fq, q)]
    k_side = [jnp.where(left, k, fk), jnp.where(left, fk, k)]
    v_side = [jnp.where(left, v, zero), jnp.where(left, zero, v)]
    delta = [jnp.sum(product_t[h * HD : (h + 1) * HD], axis=0, keepdims=True) for h in range(2)]
    lse = [lse_ref[0, h : h + 1, :] for h in range(2)]
    dq = [None, None]
    sum_v = jnp.zeros((1, 128), f32)
    for c in range(rows // chunk):
        span = slice(c * chunk, (c + 1) * chunk)
        dk = []
        dv = []
        for h in range(2):
            scores = dot_nt(k_side[h][span], q_side[h])
            p = jnp.exp(scores - lse[h])
            dp = dot_nt(v_side[h][span], g)
            dv.append(dot32(p.astype(bf16), g))
            ds = (p * (dp - delta[h])).astype(bf16)
            dk.append(dot32(ds, q))
            part = dot32(k_t[h * HD : (h + 1) * HD, span], ds)
            dq[h] = part if dq[h] is None else dq[h] + part
        dk_low = jnp.where(left_chunk, dk[0], dk[1]).astype(bf16)
        dv_low = jnp.where(left_chunk, dv[0], dv[1]).astype(bf16)
        dj_ref[span, pl.ds(pl.multiple_of(width + step * 128, 128), 128)] = dk_low
        dj_ref[span, pl.ds(pl.multiple_of(2 * width + step * 128, 128), 128)] = dv_low
        sum_v += jnp.sum(dv_low.astype(f32), axis=0, keepdims=True)
    dq_low = (jnp.concatenate(dq, axis=0) * scale).T.astype(bf16)
    dj_ref[:, pl.ds(pl.multiple_of(step * 128, 128), 128)] = dq_low
    cs_ref[0:1, :] = jnp.sum(dq_low.astype(f32), axis=0, keepdims=True)
    cs_ref[1:2, :] = sum_v


def attend_backward(joined, grad_attended, attended, lse, fq, fk):
    rows = joined.shape[0]
    width = joined.shape[1] // 3
    n = width // 128
    col = lambda off: pl.BlockSpec((rows, 128), lambda i, off=off: (0, off + i))
    full = pl.BlockSpec((rows, 128), lambda i: (0, 0))
    return pl.pallas_call(
        partial(attend_backward_kernel, chunk=rows // 2),
        grid=(n,),
        in_specs=[
            col(0),
            col(n),
            col(2 * n),
            col(0),
            col(0),
            pl.BlockSpec((1, 2, rows), lambda i: (i, 0, 0)),
            full,
            full,
        ],
        out_specs=[
            pl.BlockSpec((rows, 3 * width), lambda i: (0, 0)),
            pl.BlockSpec((2, 128), lambda i: (0, i)),
        ],
        out_shape=[
            jax.ShapeDtypeStruct((rows, 3 * width), bf16),
            jax.ShapeDtypeStruct((2, width), f32),
        ],
        compiler_params=pltpu.CompilerParams(vmem_limit_bytes=VMEM_LIMIT),
        cost_estimate=pl.CostEstimate(
            flops=40 * rows * rows * width, bytes_accessed=16 * rows * width, transcendentals=0
        ),
        name="attend_backward",
    )(joined, joined, joined, grad_attended, attended, lse, fq, fk)


def scatter_sum(blocks, me, order, wire):
    n = blocks.shape[0]
    rest = blocks.shape[1:]
    low_bits = n.bit_length() - 3
    dims = (4,) + (2,) * low_bits
    terms = [blocks.reshape(dims + rest)]
    axes = ["top"] + list(range(low_bits - 1, -1, -1))

    def pick(values, axis, index):
        return lax.dynamic_index_in_dim(values, index, axis, keepdims=False)

    def total(values):
        out = values[0].astype(f32)
        for value in values[1:]:
            out = out + value.astype(f32)
        return out

    for bit in order:
        axis = axes.index(bit)
        mine = (me >> bit) & 1
        sent = total([pick(term, axis, 1 - mine) for term in terms]).astype(wire)
        came = lax.ppermute(sent, "dp", [(i, i ^ (1 << bit)) for i in range(n)])
        terms = [pick(term, axis, mine) for term in terms] + [came]
        axes.remove(bit)
    mine = me >> low_bits
    arrived = []
    for k in range(1, 4):
        sent = total([pick(term, 0, mine ^ k) for term in terms]).astype(wire)
        arrived.append(lax.ppermute(sent, "dp", [(i, i ^ (k << low_bits)) for i in range(n)]))
    return total([pick(term, 0, mine) for term in terms] + arrived)


def reduce_rows(grad, me, n, flip):
    rows, columns = grad.shape
    if n < 8 or n & (n - 1) or (rows // n) % 8:
        return lax.psum_scatter(grad.astype(f32), "dp", scatter_dimension=0, tiled=True)
    low_bits = n.bit_length() - 3
    middle = list(range(1, low_bits))
    order = [0] + (middle[::-1] if flip else middle)
    return scatter_sum(grad.reshape(n, rows // n, columns), me, order, bf16)


def reduce_small(vectors, me, n):
    pieces = [vector.reshape(LAYERS, n, -1).transpose(1, 0, 2).reshape(n, -1) for vector in vectors]
    packed = jnp.concatenate(pieces, axis=1)
    size = packed.shape[1]
    padded = jnp.pad(packed, ((0, 0), (0, -size % 1024))).reshape(n, -1, 128)
    if n < 8 or n & (n - 1):
        mine = lax.psum_scatter(padded, "dp", scatter_dimension=0, tiled=False)
    else:
        mine = scatter_sum(padded, me, list(range(n.bit_length() - 3)), f32)
    flat = mine.reshape(-1)
    outs = []
    start = 0
    for piece in pieces:
        outs.append(flat[start : start + piece.shape[1]].reshape(LAYERS, -1))
        start += piece.shape[1]
    return outs


def layer_forward(stream, weights, fq, fk):
    gain_one, shift_one, qkv_w, qv_b, out_w, out_b, gain_two, shift_two, up_w, up_b, down_w, down_b = weights
    width = stream.shape[1]
    normed = layer_norm(stream, gain_one.astype(f32), shift_one.astype(f32)).astype(bf16)
    bias_full = jnp.concatenate([qv_b[:width], jnp.zeros((width,), bf16), qv_b[width:]]).astype(f32)
    joined = (dot32(normed, qkv_w) + bias_full).astype(bf16)
    attended, lse = attend_forward(joined, fq, fk)
    middle = stream + dot32(attended, out_w) + out_b.astype(f32)
    normed_two = layer_norm(middle, gain_two.astype(f32), shift_two.astype(f32)).astype(bf16)
    hidden = dot32(normed_two, up_w) + up_b.astype(f32)
    activated = jax.nn.gelu(hidden, approximate=False).astype(bf16)
    output = middle + dot32(activated, down_w) + down_b.astype(f32)
    return output, (stream, normed, joined, attended, lse, middle, normed_two, hidden, activated)


def norm_backward(grad_normed, values, gain, shift):
    unused, back = jax.vjp(layer_norm, values, gain.astype(f32), shift.astype(f32))
    return back(grad_normed)


def layer_backward(grad_stream, cache, weights, fq, fk, me, n):
    stream, normed, joined, attended, lse, middle, normed_two, hidden, activated = cache
    gain_one, shift_one, qkv_w, qv_b, out_w, out_b, gain_two, shift_two, up_w, up_b, down_w, down_b = weights
    grad_low = grad_stream.astype(bf16)
    grad_down_w = jnp.einsum("tf,td->fd", activated, grad_low, preferred_element_type=f32).astype(bf16)
    down_sum = reduce_rows(grad_down_w, me, n, False)
    grad_down_b = jnp.sum(grad_low.astype(f32), axis=0)
    grad_activated = dot_nt(grad_low, down_w)
    unused, gelu_back = jax.vjp(partial(jax.nn.gelu, approximate=False), hidden)
    grad_hidden = gelu_back(grad_activated)[0].astype(bf16)
    grad_up_w = jnp.einsum("td,tf->df", normed_two, grad_hidden, preferred_element_type=f32).astype(bf16)
    up_sum = reduce_rows(grad_up_w, me, n, True)
    grad_up_b = jnp.sum(grad_hidden.astype(f32), axis=0)
    grad_normed = dot_nt(grad_hidden, up_w)
    grad_input, grad_gain_two, grad_shift_two = norm_backward(grad_normed, middle, gain_two, shift_two)
    grad_middle = grad_stream + grad_input
    branch = grad_middle.astype(bf16)
    grad_out_w = jnp.einsum("tc,td->cd", attended, branch, preferred_element_type=f32).astype(bf16)
    out_sum = reduce_rows(grad_out_w, me, n, True)
    grad_out_b = jnp.sum(branch.astype(f32), axis=0)
    grad_attended = dot_nt(branch, out_w).astype(bf16)
    grad_joined, column_sums = attend_backward(joined, grad_attended, attended, lse, fq, fk)
    grad_qkv_w = jnp.einsum("td,te->de", normed, grad_joined, preferred_element_type=f32).astype(bf16)
    qkv_sum = reduce_rows(grad_qkv_w, me, n, False)
    grad_qv_b = column_sums.reshape(-1)
    grad_normed = dot_nt(grad_joined, qkv_w)
    grad_input, grad_gain_one, grad_shift_one = norm_backward(grad_normed, stream, gain_one, shift_one)
    small = (
        grad_gain_one,
        grad_shift_one,
        grad_qv_b,
        grad_out_b,
        grad_gain_two,
        grad_shift_two,
        grad_up_b,
        grad_down_b,
    )
    return grad_middle + grad_input, (qkv_sum, out_sum, up_sum, down_sum), small


def local(n, *arguments):
    (
        patches,
        img_length,
        img_start,
        class_count,
        *stacked,
        cls_weight,
        cls_bias,
        logit_grad,
    ) = arguments
    me = lax.axis_index("dp")
    row_count = patches.shape[0]
    slot_count = img_length.shape[0]
    positions = jnp.arange(row_count, dtype=jnp.int32)
    inside = (positions[None, :] >= img_start[:, None]) & (
        positions[None, :] < (img_start + img_length)[:, None]
    )
    member = inside.astype(f32)
    live_rows = jnp.sum(inside.astype(jnp.int32), axis=0)
    segment = (
        jnp.sum(inside.astype(jnp.int32) * jnp.arange(slot_count, dtype=jnp.int32)[:, None], axis=0)
        + (1 - live_rows) * slot_count
    )
    fq, fk = seg_features(segment, slot_count)
    counts = jnp.maximum(img_length, 1).astype(f32)
    live_columns = jnp.arange(cls_weight.shape[1], dtype=jnp.int32) < class_count[0]
    masked_grad = jnp.where(live_columns[None, :], logit_grad, jnp.zeros_like(logit_grad))
    pooled_grad = lax.psum_scatter(
        dot_nt(masked_grad, cls_weight), "dp", scatter_dimension=0, tiled=True
    )
    stream = patches.astype(f32)
    layers = [tuple(weight[layer] for weight in stacked) for layer in range(LAYERS)]
    caches = []
    for weights in layers:
        stream, cache = layer_forward(stream, weights, fq, fk)
        caches.append(cache)
    pooled = (
        jnp.dot(member, stream, precision=HIGHEST, preferred_element_type=f32) / counts[:, None]
    )
    gathered = lax.all_gather(pooled.astype(bf16), "dp", axis=0, tiled=True)
    scores = dot32(gathered, cls_weight) + cls_bias.astype(f32)
    logits = jnp.where(live_columns[None, :], scores, 0.0)
    grad_cls_weight = jnp.einsum("id,ic->dc", gathered, masked_grad, preferred_element_type=f32)
    grad_cls_bias = jnp.sum(masked_grad.astype(f32), axis=0)
    grad_stream = jnp.einsum(
        "it,id->td",
        member,
        pooled_grad / counts[:, None],
        precision=HIGHEST,
        preferred_element_type=f32,
    )
    large = [None] * LAYERS
    small = [None] * LAYERS
    for layer in reversed(range(LAYERS)):
        grad_stream, large[layer], small[layer] = layer_backward(
            grad_stream, caches[layer], layers[layer], fq, fk, me, n
        )
    qkv_sum, out_sum, up_sum, down_sum = (jnp.stack(pair) for pair in zip(*large))
    gain_one, shift_one, qv_b, out_b, gain_two, shift_two, up_b, down_b = reduce_small(
        [jnp.stack(pair) for pair in zip(*small)], me, n
    )
    return (
        logits,
        grad_stream,
        gain_one,
        shift_one,
        qkv_sum,
        qv_b,
        out_sum,
        out_b,
        gain_two,
        shift_two,
        up_sum,
        up_b,
        down_sum,
        down_b,
        grad_cls_weight,
        grad_cls_bias,
    )


def solution(mesh):
    whole = P()
    placed = (
        (P("dp", None), P("dp"), P("dp"), P("dp"))
        + (whole,) * 12
        + (P(None, "dp"), P("dp"), P(None, "dp"))
    )
    vector = P(None, "dp")
    matrix = P(None, "dp", None)
    return jax.shard_map(
        partial(local, mesh.size),
        mesh=mesh,
        in_specs=placed,
        out_specs=(
            P(None, "dp"),
            P("dp", None),
            vector,
            vector,
            matrix,
            vector,
            matrix,
            vector,
            vector,
            vector,
            matrix,
            vector,
            matrix,
            vector,
            P(None, "dp"),
            P("dp"),
        ),
        check_vma=False,
    )
```

time: 1720 us -> 744 us (0.43)
  waiting for transfers between devices: 695 us -> 107 us
  matrix products: 580 us -> 257 us
  other arithmetic: 201 us -> 77.1 us
  Pallas kernels: 0 us -> 116 us
  local copies, waits for them, and re-layouts: 126 us -> 56.7 us
  starting transfers between devices: 0.29 us -> 59 us
  blocking collectives: 83.3 us -> 45.4 us
    reduce_scatter x5 -> x1, waiting for transfers between devices: 695 us -> 0.01 us  [local(): lax.psum_scatter(dot_nt(masked_grad, cls_weight), 'dp', scatter_dimension...]
    dot_general x56 -> x28, matrix products: 576 us -> 252 us  [the longest x9 113 us: dot32(): return jnp.dot(left, right, preferred_element_type=f32)]
    pallas_call x0 -> x4, Pallas kernels: none -> 116 us  [the longest x2 74.2 us: attend_backward(): pl.pallas_call(partial(attend_backward_kernel, chunk=rows // 2), grid=(n,...]
    ppermute x0 -> x54, waiting for transfers between devices: none -> 107 us  [the longest x27 77.6 us: scatter_sum(): came = lax.ppermute(sent, 'dp', [(i, i ^ 1 << bit) for i in range(n)])]
    ppermute x0 -> x54, starting transfers between devices: none -> 59 us  [the longest x27 42.1 us: scatter_sum(): lax.ppermute(sent, 'dp', [(i, i ^ k << low_bits) for i in range(n)])]
    convert_element_type x7 -> x29, other arithmetic: 86 us -> 32.8 us  [the longest x16 20.9 us: scatter_sum(): sent = total([pick(term, axis, 1 - mine) for term in terms]).astype(wire)]
    reduce_sum x10 -> x4, other arithmetic: 56.4 us -> 3.82 us  [the longest x1 1.63 us: layer_backward(): grad_down_b = jnp.sum(grad_low.astype(f32), axis=0)]
    unnamed x1 -> x0, blocking collectives: 37.7 us -> none
  transfers between devices with their start and end apart: 7 -> 55, of which waited for: 4 -> 20; matrix products, arithmetic and copies ran while one was open for 23% -> 28% of each run, Pallas kernels for 0% -> 6%
where the time goes in v1:
time: 744 us; the launch traced here: 735 us
  matrix products  257 us (35%)
  Pallas kernels  116 us (16%)
  waiting for transfers between devices  107 us (14%)
  other arithmetic  77.1 us (10%)
  starting transfers between devices  59 us (8%)
  local copies, waits for them, and re-layouts  56.7 us (8%)
  blocking collectives  45.4 us (6%)
  between operations  17.2 us (2%)
    dot_general x9, matrix products, dot32(): return jnp.dot(left, right, preferred_element_type=f32)  113 us
    dot_general x9, matrix products, dot_nt(): return lax.dot_general(left, right, NT, preferred_element_type=f32)  82.1 us
    ppermute x27, waiting for transfers between devices, scatter_sum(): came = lax.ppermute(sent, 'dp', [(i, i ^ 1 << bit) for i in range(n)])  77.6 us
    pallas_call x2, Pallas kernels, attend_backward(): pl.pallas_call(partial(attend_backward_kernel, chunk=rows // 2), grid=(n,...  74.2 us
    all_gather x1, blocking collectives, local(): gathered = lax.all_gather(pooled.astype(bf16), 'dp', axis=0, tiled=True)  45.4 us
    ppermute x27, starting transfers between devices, scatter_sum(): lax.ppermute(sent, 'dp', [(i, i ^ k << low_bits) for i in range(n)])  42.1 us
    pallas_call x2, Pallas kernels, attend_forward(): pl.pallas_call(partial(attend_forward_kernel, chunk=rows), grid=(n,), in_...  41.5 us
    ppermute x27, waiting for transfers between devices, scatter_sum(): lax.ppermute(sent, 'dp', [(i, i ^ k << low_bits) for i in range(n)])  29.8 us
  transfers between devices with their start and end apart: 55, of which 20 were waited for; matrix products, arithmetic and copies ran while one was open for 28% of the time, Pallas kernels for 6%

profile of v1, /device:TPU:0, one launch (start us, length us, event | category | flops | bytes accessed | tf_op | source)
XLA Modules:
  0.0 735.1 jit_solution(6251611237092877750)
XLA Ops:
  16.5 7.8 %add_convert_fusion.3.q_ref.k_ref.v_ref = bf16[1024,2304]{1,0:T(8,128)(2,1)} fusion(f32[2304]{0:T(1024)S(1)} %get-tuple-element.156, bf16[2,768,2304]{2,1,0:T(8,128)(2,1)} %param.25, bf16[1024,768]{0,1:T(8,128)(2,1)S(1)} %copy.121, f32[768]{0:T(1024)S(1)} %get-tuple-element.103, f32[768]{0:T(1024)S(1)} %get-tuple-element.101, f32[1024]{0:T(1024)S(1)} %fusion.236, ...), kind=kOutput, calls=%fused_computation.37 | convolution fusion | flops 3633315840 | bytes 9853952 | tf_op jit(solution)/shard_map/dot_general | solution.py:28
  24.4 20.8 %attend_forward.2 = (bf16[1024,768]{1,0:T(8,128)(2,1)}, f32[6,2,1024]{2,1,0:T(2,128)}) custom-call(bf16[1024,2304]{1,0:T(8,128)(2,1)} %add_convert_fusion.3.q_ref.k_ref.v_ref, bf16[1024,2304]{1,0:T(8,128)(2,1)} %add_convert_fusion.3.q_ref.k_ref.v_ref, bf16[1024,2304]{1,0:T(8,128)(2,1)} %add_convert_fusion.3.q_ref.k_ref.v_ref, ...), custom_call_target="tpu_custom_call" | custom-call | flops 12884901888 | bytes 7864320 | tf_op jit(solution)/shard_map/attend_forward/pallas_call | solution.py:74
  50.3 38.2 %multiply_convert_fusion.1 = (bf16[1024,3072]{1,0:T(8,128)(2,1)}, f32[1024,3072]{1,0:T(8,128)}, f32[1024,3072]{1,0:T(8,128)}) fusion(f32[3072]{0:T(1024)S(1)} %bitcast.951, bf16[2,768,3072]{2,1,0:T(8,128)(2,1)} %param.31, f32[1024,768]{0,1:T(8,128)S(1)} %get-tuple-element.160, f32[768]{0:T(1024)S(1)} %get-tuple-element.97, f32[768]{0:T(1024)S(1)} %get-tuple-element.181, ...), kind=kOutput, calls=%fused_computation.21 | convolution fusion | flops 5043388416 | bytes 39348224 | tf_op jit(solution)/shard_map/dot_general | solution.py:28
  88.6 7.7 %fusion.257 = (f32[1024]{0:T(1024)S(1)}, f32[1024,768]{0,1:T(8,128)S(1)}) fusion(f32[768]{0:T(1024)S(1)} %get-tuple-element.93, f32[1024,768]{0,1:T(8,128)S(1)} %get-tuple-element.160, bf16[1024,3072]{1,0:T(8,128)(2,1)} %get-tuple-element.118, bf16[2,3072,768]{2,1,0:T(8,128)(2,1)S(1)} %bitcast.956), kind=kOutput, calls=%fused_computation.554 | convolution fusion | flops 4834196480 | bytes 17309696 | tf_op jit(solution)/shard_map/dot_general | solution.py:28
  98.2 7.7 %add_convert_fusion.2.q_ref.k_ref.v_ref = bf16[1024,2304]{1,0:T(8,128)(2,1)} fusion(f32[2304]{0:T(1024)S(1)} %get-tuple-element.155, bf16[2,768,2304]{2,1,0:T(8,128)(2,1)} %param.25, f32[1024,768]{0,1:T(8,128)S(1)} %get-tuple-element.163, f32[768]{0:T(1024)S(1)} %get-tuple-element.102, f32[768]{0:T(1024)S(1)} %get-tuple-element.100, f32[1024]{0:T(1024)S(1)} %fusion.238, ...), kind=kOutput, calls=%fused_computation.36 | convolution fusion | flops 3632529408 | bytes 11426816 | tf_op jit(solution)/shard_map/dot_general | solution.py:28
  105.9 20.7 %attend_forward.3 = (bf16[1024,768]{1,0:T(8,128)(2,1)}, f32[6,2,1024]{2,1,0:T(2,128)}) custom-call(bf16[1024,2304]{1,0:T(8,128)(2,1)} %add_convert_fusion.2.q_ref.k_ref.v_ref, bf16[1024,2304]{1,0:T(8,128)(2,1)} %add_convert_fusion.2.q_ref.k_ref.v_ref, bf16[1024,2304]{1,0:T(8,128)(2,1)} %add_convert_fusion.2.q_ref.k_ref.v_ref, ...), custom_call_target="tpu_custom_call" | custom-call | flops 12884901888 | bytes 7864320 | tf_op jit(solution)/shard_map/attend_forward/pallas_call | solution.py:74
  130.4 37.4 %multiply_convert_fusion = (bf16[1024,3072]{1,0:T(8,128)(2,1)S(1)}, f32[1024,3072]{1,0:T(8,128)}, f32[1024,3072]{1,0:T(8,128)}) fusion(f32[3072]{0:T(1024)S(1)} %bitcast.953, bf16[2,768,3072]{2,1,0:T(8,128)(2,1)} %param.31, f32[1024,768]{0,1:T(8,128)S(1)} %get-tuple-element.165, f32[768]{0:T(1024)S(1)} %get-tuple-element.96, ...), kind=kOutput, calls=%fused_computation.8 | convolution fusion | flops 5043388416 | bytes 39348224 | tf_op jit(solution)/shard_map/dot_general | solution.py:28
  179.2 45.4 %all_gather.3 = bf16[512,768]{1,0:T(8,128)(2,1)S(1)} all-gather(bf16[16,768]{1,0:T(8,128)(2,1)S(1)} %fusion.82), channel_id=1, replica_groups=mesh['dp'=32] {'dp'}, dimensions={0}, use_global_device_ids=true | all-gather | bytes 811008 | tf_op jit(solution)/shard_map/all_gather | solution.py:338
  235.1 9.6 %convolution_convert_fusion = bf16[3072,768]{1,0:T(8,128)(2,1)} fusion(bf16[1024,3072]{1,0:T(8,128)(2,1)} %copy-done.114, f32[1024,768]{1,0:T(8,128)} %get-tuple-element.180), kind=kOutput, calls=%fused_computation.38 | convolution fusion | flops 4834983936 | bytes 14155776 | tf_op jit(solution)/shard_map/tf,td->fd/dot_general | solution.py:262
  244.7 19.3 %convert_reduce_fusion = (f32[3072]{0:T(1024)}, bf16[1024,3072]{1,0:T(8,128)(2,1)}) fusion(f32[1024,3072]{1,0:T(8,128)} %get-tuple-element.117, bf16[2,3072,768]{2,1,0:T(8,128)(2,1)} %param.33, f32[1024,768]{1,0:T(8,128)} %get-tuple-element.180, f32[1024,3072]{1,0:T(8,128)} %get-tuple-element.166, f32[3072]{0:T(1024)S(1)} %bitcast.954), kind=kOutput, calls=%fused_computation.4 | convolution fusion | flops 4886098944 | bytes 39346176 | tf_op jit(solution)/shard_map/dot_general | solution.py:32
  264.0 10.5 %fusion.261 = (f32[768]{0:T(1024)}, f32[1024,768]{1,0:T(8,128)}) fusion(bf16[1024,3072]{1,0:T(8,128)(2,1)} %get-tuple-element.176, bf16[2,768,3072]{2,1,0:T(8,128)(2,1)} %param.31), kind=kOutput, calls=%fused_computation.558 | convolution fusion | flops 4832623616 | bytes 14158848 | tf_op jit(solution)/shard_map/dot_general | solution.py:32
  295.0 37.1 %attend_backward.2 = (bf16[1024,2304]{1,0:T(8,128)(2,1)}, f32[2,768]{1,0:T(2,128)}) custom-call(bf16[1024,2304]{1,0:T(8,128)(2,1)} %add_convert_fusion.2.q_ref.k_ref.v_ref, bf16[1024,2304]{1,0:T(8,128)(2,1)} %add_convert_fusion.2.q_ref.k_ref.v_ref, bf16[1024,2304]{1,0:T(8,128)(2,1)} %add_convert_fusion.2.q_ref.k_ref.v_ref, ...), custom_call_target="tpu_custom_call" | custom-call | flops 32212254720 | bytes 12582912 | tf_op jit(solution)/shard_map/attend_backward/pallas_call | solution.py:149
  332.2 8.4 %fusion.259 = (f32[768]{0:T(1024)}, f32[1024,768]{1,0:T(8,128)}) fusion(bf16[1024,2304]{1,0:T(8,128)(2,1)} %get-tuple-element.27, bf16[2,768,2304]{2,1,0:T(8,128)(2,1)S(1)} %bitcast.960), kind=kOutput, calls=%fused_computation.556 | convolution fusion | flops 3624664320 | bytes 11406336 | tf_op jit(solution)/shard_map/dot_general | solution.py:32
  359.3 18.9 %convert_reduce_fusion.1 = (f32[3072]{0:T(1024)S(1)}, bf16[1024,3072]{1,0:T(8,128)(2,1)}) fusion(f32[1024,3072]{1,0:T(8,128)} %get-tuple-element.119, bf16[2,3072,768]{2,1,0:T(8,128)(2,1)} %param.33, f32[1024,768]{0,1:T(8,128)} %copy-done.16, f32[1024,3072]{1,0:T(8,128)} %get-tuple-element.161, f32[3072]{0:T(1024)S(1)} %bitcast.952), kind=kOutput, calls=%fused_computation.5 | convolution fusion | flops 4886098944 | bytes 39346176 | tf_op jit(solution)/shard_map/dot_general | solution.py:32
  378.2 10.4 %convolution_convert_fusion.3 = bf16[768,3072]{1,0:T(8,128)(2,1)} fusion(bf16[1024,3072]{1,0:T(8,128)(2,1)} %get-tuple-element.178, f32[1024,768]{0,1:T(8,128)} %copy-done.10, f32[768]{0:T(1024)S(1)} %copy-done.101, f32[768]{0:T(1024)S(1)} %copy-done.65, f32[1024]{0:T(1024)S(1)} %copy-done.67, f32[1024]{0:T(1024)S(1)} %copy-done.40), kind=kOutput, calls=%fused_computation.41 | convolution fusion | flops 4838129664 | bytes 14170112 | tf_op jit(solution)/shard_map/td,tf->df/dot_general | solution.py:268
  388.6 9.2 %fusion.262 = (f32[768]{0:T(1024)S(1)}, f32[1024,768]{1,0:T(8,128)}) fusion(bf16[1024,3072]{1,0:T(8,128)(2,1)S(1)} %copy-done.112, bf16[2,768,3072]{2,1,0:T(8,128)(2,1)} %param.31), kind=kOutput, calls=%fused_computation.559 | convolution fusion | flops 4832623616 | bytes 14158848 | tf_op jit(solution)/shard_map/dot_general | solution.py:32
  422.7 37.0 %attend_backward.3 = (bf16[1024,2304]{1,0:T(8,128)(2,1)}, f32[2,768]{1,0:T(2,128)}) custom-call(bf16[1024,2304]{1,0:T(8,128)(2,1)} %add_convert_fusion.3.q_ref.k_ref.v_ref, bf16[1024,2304]{1,0:T(8,128)(2,1)} %add_convert_fusion.3.q_ref.k_ref.v_ref, bf16[1024,2304]{1,0:T(8,128)(2,1)} %add_convert_fusion.3.q_ref.k_ref.v_ref, ...), custom_call_target="tpu_custom_call" | custom-call | flops 32212254720 | bytes 12582912 | tf_op jit(solution)/shard_map/attend_backward/pallas_call | solution.py:149
  459.8 8.4 %convolution_convert_fusion.5 = bf16[768,2304]{1,0:T(8,128)(2,1)} fusion(bf16[1024,2304]{1,0:T(8,128)(2,1)} %get-tuple-element.29, bf16[1024,768]{0,1:T(8,128)(2,1)S(1)} %copy-done.3, f32[768]{0:T(1024)S(1)} %copy-done.97, f32[768]{0:T(1024)S(1)} %copy-done.42, f32[1024]{0:T(1024)S(1)} %copy-done.69, f32[1024]{0:T(1024)S(1)} %copy-done.36), kind=kOutput, calls=%fused_computation.43 | convolution fusion | flops 3630366720 | bytes 9844736 | tf_op jit(solution)/shard_map/td,te->de/dot_general | solution.py:280
  468.3 8.1 %fusion.260 = (f32[768]{0:T(1024)}, f32[1024,768]{1,0:T(8,128)}) fusion(bf16[1024,2304]{1,0:T(8,128)(2,1)S(1)} %copy-done.113, bf16[2,768,2304]{2,1,0:T(8,128)(2,1)} %param.25), kind=kOutput, calls=%fused_computation.557 | convolution fusion | flops 3624664320 | bytes 11406336 | tf_op jit(solution)/shard_map/dot_general | solution.py:32
  572.1 12.4 %collective-permute-done.7 = bf16[4,2,24,2304]{3,2,1,0:T(8,128)(2,1)S(1)} collective-permute-done((bf16[4,2,24,2304]{3,2,1,0:T(8,128)(2,1)S(1)}, bf16[4,2,24,2304]{3,2,1,0:T(8,128)(2,1)S(1)}, u32[]{:S(2)}, u32[]{:S(2)}) %collective-permute-start.7) | collective-permute-done | bytes 884768 | tf_op jit(solution)/shard_map/ppermute | solution.py:199
  586.2 17.3 %collective-permute-done.13 = bf16[4,2,24,2304]{3,2,1,0:T(8,128)(2,1)S(1)} collective-permute-done((bf16[4,2,24,2304]{3,2,1,0:T(8,128)(2,1)S(1)}, bf16[4,2,24,2304]{3,2,1,0:T(8,128)(2,1)S(1)}, u32[]{:S(2)}, u32[]{:S(2)}) %collective-permute-start.13) | collective-permute-done | bytes 884768 | tf_op jit(solution)/shard_map/ppermute | solution.py:199
  636.3 21.6 %collective-permute-done.37 = bf16[4,2,24,3072]{3,2,1,0:T(8,128)(2,1)S(1)} collective-permute-done((bf16[4,2,24,3072]{3,2,1,0:T(8,128)(2,1)S(1)}, bf16[4,2,24,3072]{3,2,1,0:T(8,128)(2,1)S(1)}, u32[]{:S(2)}, u32[]{:S(2)}) %collective-permute-start.37) | collective-permute-done | bytes 1179680 | tf_op jit(solution)/shard_map/ppermute | solution.py:199
  660.1 10.4 %collective-permute-done.44 = bf16[4,96,768]{2,1,0:T(8,128)(2,1)S(1)} collective-permute-done((bf16[4,96,768]{2,1,0:T(8,128)(2,1)S(1)}, bf16[4,96,768]{2,1,0:T(8,128)(2,1)S(1)}, u32[]{:S(2)}, u32[]{:S(2)}) %collective-permute-start.44) | collective-permute-done | bytes 589856 | tf_op jit(solution)/shard_map/ppermute | solution.py:199
  684.5 9.9 %collective-permute-done.34 = bf16[24,3072]{1,0:T(8,128)(2,1)S(1)} collective-permute-done((bf16[24,3072]{1,0:T(8,128)(2,1)S(1)}, bf16[24,3072]{1,0:T(8,128)(2,1)S(1)}, u32[]{:S(2)}, u32[]{:S(2)}) %collective-permute-start.34) | collective-permute-done | bytes 147488 | tf_op jit(solution)/shard_map/ppermute | solution.py:206
  (560 shorter events, 283.5 us)
Async XLA Ops:
  7.2 219.4 %reduce-scatter.2.cloned.1.call-start = ((), (), s32[]{:S(2)}) async-start(), calls=%async_computation.1 | async-start | bytes 1622016 | tf_op jit(solution)/shard_map/reduce_scatter | solution.py:326
  477.3 28.3 %collective-permute-start.18 = (bf16[4,2,2,24,768]{4,3,2,1,0:T(8,128)(2,1)}, bf16[4,2,2,24,768]{4,3,2,1,0:T(8,128)(2,1)}, u32[]{:S(2)}, u32[]{:S(2)}) collective-permute-start(bf16[4,2,2,24,768]{4,3,2,1,0:T(8,128)(2,1)} %dynamic-slice_bitcast_fusion.7), channel_id=1, source_target_pairs={{0,1},{1,0},{2,3},{3,2},{4,5},{5,4},{6,7},{7,6},{8,9},{9,8},{10,11... | collective-permute-start | bytes 1769480 | tf_op jit(solution)/shard_map/ppermute | solution.py:199
  477.7 29.3 %collective-permute-start.24 = (bf16[4,2,2,24,768]{4,3,2,1,0:T(8,128)(2,1)S(1)}, bf16[4,2,2,24,768]{4,3,2,1,0:T(8,128)(2,1)}, u32[]{:S(2)}, u32[]{:S(2)}) collective-permute-start(bf16[4,2,2,24,768]{4,3,2,1,0:T(8,128)(2,1)S(1)} %dynamic-slice_bitcast_fusion.6), channel_id=1, source_target_pairs={{0,1},{1,0},{2,3},{3,2},{4,5},{5,4},{6,7},{7,6},{8,9},{9,8},{10,11... | collective-permute-start | bytes 1769480 | tf_op jit(solution)/shard_map/ppermute | solution.py:199
  532.8 31.0 %collective-permute-start.42 = (bf16[4,2,2,96,768]{4,3,2,1,0:T(8,128)(2,1)}, bf16[4,2,2,96,768]{4,3,2,1,0:T(8,128)(2,1)}, u32[]{:S(2)}, u32[]{:S(2)}) collective-permute-start(bf16[4,2,2,96,768]{4,3,2,1,0:T(8,128)(2,1)} %dynamic-slice_bitcast_fusion.1), channel_id=1, source_target_pairs={{0,1},{1,0},{2,3},{3,2},{4,5},{5,4},{6,7},{7,6},{8,9},{9,8},{10,11... | collective-permute-start | bytes 7077896 | tf_op jit(solution)/shard_map/ppermute | solution.py:199
  532.9 25.8 %collective-permute-start.6 = (bf16[4,2,2,24,2304]{4,3,2,1,0:T(8,128)(2,1)}, bf16[4,2,2,24,2304]{4,3,2,1,0:T(8,128)(2,1)}, u32[]{:S(2)}, u32[]{:S(2)}) collective-permute-start(bf16[4,2,2,24,2304]{4,3,2,1,0:T(8,128)(2,1)} %dynamic-slice_bitcast_fusion.5), channel_id=1, source_target_pairs={{0,1},{1,0},{2,3},{3,2},{4,5},{5,4},{6,7},{7,6},{8,9},{9,8},{10,11... | collective-permute-start | bytes 5308424 | tf_op jit(solution)/shard_map/ppermute | solution.py:199
  539.3 28.1 %collective-permute-start.30 = (bf16[4,2,2,24,3072]{4,3,2,1,0:T(8,128)(2,1)}, bf16[4,2,2,24,3072]{4,3,2,1,0:T(8,128)(2,1)}, u32[]{:S(2)}, u32[]{:S(2)}) collective-permute-start(bf16[4,2,2,24,3072]{4,3,2,1,0:T(8,128)(2,1)} %dynamic-slice_bitcast_fusion.3), channel_id=1, source_target_pairs={{0,1},{1,0},{2,3},{3,2},{4,5},{5,4},{6,7},{7,6},{8,9},{9,8},{10,11... | collective-permute-start | bytes 7077896 | tf_op jit(solution)/shard_map/ppermute | solution.py:199
  541.3 20.6 %collective-permute-start.12 = (bf16[4,2,2,24,2304]{4,3,2,1,0:T(8,128)(2,1)}, bf16[4,2,2,24,2304]{4,3,2,1,0:T(8,128)(2,1)}, u32[]{:S(2)}, u32[]{:S(2)}) collective-permute-start(bf16[4,2,2,24,2304]{4,3,2,1,0:T(8,128)(2,1)} %dynamic-slice_bitcast_fusion.4), channel_id=1, source_target_pairs={{0,1},{1,0},{2,3},{3,2},{4,5},{5,4},{6,7},{7,6},{8,9},{9,8},{10,11... | collective-permute-start | bytes 5308424 | tf_op jit(solution)/shard_map/ppermute | solution.py:199
  548.6 21.4 %collective-permute-start.36 = (bf16[4,2,2,24,3072]{4,3,2,1,0:T(8,128)(2,1)}, bf16[4,2,2,24,3072]{4,3,2,1,0:T(8,128)(2,1)}, u32[]{:S(2)}, u32[]{:S(2)}) collective-permute-start(bf16[4,2,2,24,3072]{4,3,2,1,0:T(8,128)(2,1)} %dynamic-slice_bitcast_fusion.2), channel_id=1, source_target_pairs={{0,1},{1,0},{2,3},{3,2},{4,5},{5,4},{6,7},{7,6},{8,9},{9,8},{10,11... | collective-permute-start | bytes 7077896 | tf_op jit(solution)/shard_map/ppermute | solution.py:199
  558.6 46.4 %collective-permute-start.48 = (bf16[4,2,2,96,768]{4,3,2,1,0:T(8,128)(2,1)S(1)}, bf16[4,2,2,96,768]{4,3,2,1,0:T(8,128)(2,1)S(1)}, u32[]{:S(2)}, u32[]{:S(2)}) collective-permute-start(bf16[4,2,2,96,768]{4,3,2,1,0:T(8,128)(2,1)S(1)} %dynamic-slice_bitcast_fusion), channel_id=1, source_target_pairs={{0,1},{1,0},{2,3},{3,2},{4,5},{5,4},{6,7},{7,6},{8,9},{9,8},{10,11... | collective-permute-start | bytes 7077896 | tf_op jit(solution)/shard_map/ppermute | solution.py:199
  561.9 22.6 %collective-permute-start.7 = (bf16[4,2,24,2304]{3,2,1,0:T(8,128)(2,1)S(1)}, bf16[4,2,24,2304]{3,2,1,0:T(8,128)(2,1)S(1)}, u32[]{:S(2)}, u32[]{:S(2)}) collective-permute-start(bf16[4,2,24,2304]{3,2,1,0:T(8,128)(2,1)S(1)} %fusion.64), channel_id=1, source_target_pairs={{0,2},{1,3},{2,0},{3,1},{4,6},{5,7},{6,4},{7,5},{8,10},{9,11},{10,... | collective-permute-start | bytes 2654216 | tf_op jit(solution)/shard_map/ppermute | solution.py:199
  563.9 39.6 %collective-permute-start.13 = (bf16[4,2,24,2304]{3,2,1,0:T(8,128)(2,1)S(1)}, bf16[4,2,24,2304]{3,2,1,0:T(8,128)(2,1)S(1)}, u32[]{:S(2)}, u32[]{:S(2)}) collective-permute-start(bf16[4,2,24,2304]{3,2,1,0:T(8,128)(2,1)S(1)} %fusion.63), channel_id=1, source_target_pairs={{0,2},{1,3},{2,0},{3,1},{4,6},{5,7},{6,4},{7,5},{8,10},{9,11},{10,... | collective-permute-start | bytes 2654216 | tf_op jit(solution)/shard_map/ppermute | solution.py:199
  567.4 63.7 %collective-permute-start.43 = (bf16[4,2,96,768]{3,2,1,0:T(8,128)(2,1)S(1)}, bf16[4,2,96,768]{3,2,1,0:T(8,128)(2,1)S(1)}, u32[]{:S(2)}, u32[]{:S(2)}) collective-permute-start(bf16[4,2,96,768]{3,2,1,0:T(8,128)(2,1)S(1)} %fusion.60), channel_id=1, source_target_pairs={{0,2},{1,3},{2,0},{3,1},{4,6},{5,7},{6,4},{7,5},{8,10},{9,11},{10,... | collective-permute-start | bytes 3538952 | tf_op jit(solution)/shard_map/ppermute | solution.py:199
  570.0 64.4 %collective-permute-start.31 = (bf16[4,2,24,3072]{3,2,1,0:T(8,128)(2,1)S(1)}, bf16[4,2,24,3072]{3,2,1,0:T(8,128)(2,1)S(1)}, u32[]{:S(2)}, u32[]{:S(2)}) collective-permute-start(bf16[4,2,24,3072]{3,2,1,0:T(8,128)(2,1)S(1)} %fusion.62), channel_id=1, source_target_pairs={{0,4},{1,5},{2,6},{3,7},{4,0},{5,1},{6,2},{7,3},{8,12},{9,13},{10,... | collective-permute-start | bytes 3538952 | tf_op jit(solution)/shard_map/ppermute | solution.py:199
  585.8 21.8 %collective-permute-start.8 = (bf16[4,24,2304]{2,1,0:T(8,128)(2,1)S(1)}, bf16[4,24,2304]{2,1,0:T(8,128)(2,1)S(1)}, u32[]{:S(2)}, u32[]{:S(2)}) collective-permute-start(bf16[4,24,2304]{2,1,0:T(8,128)(2,1)S(1)} %fusion.90), channel_id=1, source_target_pairs={{0,4},{1,5},{2,6},{3,7},{4,0},{5,1},{6,2},{7,3},{8,12},{9,13},{10,... | collective-permute-start | bytes 1327112 | tf_op jit(solution)/shard_map/ppermute | solution.py:199
  625.7 33.9 %collective-permute-start.49 = (bf16[4,2,96,768]{3,2,1,0:T(8,128)(2,1)S(1)}, bf16[4,2,96,768]{3,2,1,0:T(8,128)(2,1)S(1)}, u32[]{:S(2)}, u32[]{:S(2)}) collective-permute-start(bf16[4,2,96,768]{3,2,1,0:T(8,128)(2,1)S(1)} %fusion.59), channel_id=1, source_target_pairs={{0,2},{1,3},{2,0},{3,1},{4,6},{5,7},{6,4},{7,5},{8,10},{9,11},{10,... | collective-permute-start | bytes 3538952 | tf_op jit(solution)/shard_map/ppermute | solution.py:199
  629.1 28.8 %collective-permute-start.37 = (bf16[4,2,24,3072]{3,2,1,0:T(8,128)(2,1)S(1)}, bf16[4,2,24,3072]{3,2,1,0:T(8,128)(2,1)S(1)}, u32[]{:S(2)}, u32[]{:S(2)}) collective-permute-start(bf16[4,2,24,3072]{3,2,1,0:T(8,128)(2,1)S(1)} %fusion.61), channel_id=1, source_target_pairs={{0,4},{1,5},{2,6},{3,7},{4,0},{5,1},{6,2},{7,3},{8,12},{9,13},{10,... | collective-permute-start | bytes 3538952 | tf_op jit(solution)/shard_map/ppermute | solution.py:199
  632.6 37.9 %collective-permute-start.44 = (bf16[4,96,768]{2,1,0:T(8,128)(2,1)S(1)}, bf16[4,96,768]{2,1,0:T(8,128)(2,1)S(1)}, u32[]{:S(2)}, u32[]{:S(2)}) collective-permute-start(bf16[4,96,768]{2,1,0:T(8,128)(2,1)S(1)} %fusion.71), channel_id=1, source_target_pairs={{0,4},{1,5},{2,6},{3,7},{4,0},{5,1},{6,2},{7,3},{8,12},{9,13},{10,... | collective-permute-start | bytes 1769480 | tf_op jit(solution)/shard_map/ppermute | solution.py:199
  635.9 36.2 %collective-permute-start.32 = (bf16[4,24,3072]{2,1,0:T(8,128)(2,1)S(1)}, bf16[4,24,3072]{2,1,0:T(8,128)(2,1)S(1)}, u32[]{:S(2)}, u32[]{:S(2)}) collective-permute-start(bf16[4,24,3072]{2,1,0:T(8,128)(2,1)S(1)} %fusion.73), channel_id=1, source_target_pairs={{0,2},{1,3},{2,0},{3,1},{4,6},{5,7},{6,4},{7,5},{8,10},{9,11},{10,... | collective-permute-start | bytes 1769480 | tf_op jit(solution)/shard_map/ppermute | solution.py:199
  659.8 22.1 %collective-permute-start.50 = (bf16[4,96,768]{2,1,0:T(8,128)(2,1)S(1)}, bf16[4,96,768]{2,1,0:T(8,128)(2,1)S(1)}, u32[]{:S(2)}, u32[]{:S(2)}) collective-permute-start(bf16[4,96,768]{2,1,0:T(8,128)(2,1)S(1)} %fusion.70), channel_id=1, source_target_pairs={{0,4},{1,5},{2,6},{3,7},{4,0},{5,1},{6,2},{7,3},{8,12},{9,13},{10,... | collective-permute-start | bytes 1769480 | tf_op jit(solution)/shard_map/ppermute | solution.py:199
  672.0 27.7 %collective-permute-start.45 = (bf16[96,768]{1,0:T(8,128)(2,1)S(1)}, bf16[96,768]{1,0:T(8,128)(2,1)S(1)}, u32[]{:S(2)}, u32[]{:S(2)}) collective-permute-start(bf16[96,768]{1,0:T(8,128)(2,1)S(1)} %get-tuple-element.120), channel_id=1, source_target_pairs={{0,8},{1,9},{2,10},{3,11},{4,12},{5,13},{6,14},{7,15},{8,0},{9,1},... | collective-permute-start | bytes 442376 | tf_op jit(solution)/shard_map/ppermute | solution.py:206
  681.9 23.8 %collective-permute-start.46 = (bf16[96,768]{1,0:T(8,128)(2,1)S(1)}, bf16[96,768]{1,0:T(8,128)(2,1)S(1)}, u32[]{:S(2)}, u32[]{:S(2)}) collective-permute-start(bf16[96,768]{1,0:T(8,128)(2,1)S(1)} %get-tuple-element.122), channel_id=1, source_target_pairs={{0,16},{1,17},{2,18},{3,19},{4,20},{5,21},{6,22},{7,23},{8,24},{9,... | collective-permute-start | bytes 442376 | tf_op jit(solution)/shard_map/ppermute | solution.py:206
  682.2 23.4 %collective-permute-start.47 = (bf16[96,768]{1,0:T(8,128)(2,1)S(1)}, bf16[96,768]{1,0:T(8,128)(2,1)S(1)}, u32[]{:S(2)}, u32[]{:S(2)}) collective-permute-start(bf16[96,768]{1,0:T(8,128)(2,1)S(1)} %get-tuple-element.121), channel_id=1, source_target_pairs={{0,24},{1,25},{2,26},{3,27},{4,28},{5,29},{6,30},{7,31},{8,16},{9,... | collective-permute-start | bytes 442376 | tf_op jit(solution)/shard_map/ppermute | solution.py:206
  694.3 25.3 %collective-permute-start.52 = (bf16[96,768]{1,0:T(8,128)(2,1)S(1)}, bf16[96,768]{1,0:T(8,128)(2,1)S(1)}, u32[]{:S(2)}, u32[]{:S(2)}) collective-permute-start(bf16[96,768]{1,0:T(8,128)(2,1)S(1)} %get-tuple-element.125), channel_id=1, source_target_pairs={{0,16},{1,17},{2,18},{3,19},{4,20},{5,21},{6,22},{7,23},{8,24},{9,... | collective-permute-start | bytes 442376 | tf_op jit(solution)/shard_map/ppermute | solution.py:206
  705.6 20.3 %collective-permute-start.40 = (bf16[24,3072]{1,0:T(8,128)(2,1)S(1)}, bf16[24,3072]{1,0:T(8,128)(2,1)S(1)}, u32[]{:S(2)}, u32[]{:S(2)}) collective-permute-start(bf16[24,3072]{1,0:T(8,128)(2,1)S(1)} %get-tuple-element.131), channel_id=1, source_target_pairs={{0,16},{1,17},{2,18},{3,19},{4,20},{5,21},{6,22},{7,23},{8,24},{9,... | collective-permute-start | bytes 442376 | tf_op jit(solution)/shard_map/ppermute | solution.py:206
  (166 other events, 2314.4 us)
Sparse Core Ops, SparseCore 0:
  13.3 100.6 reduce-scatter.1

commit v2 on v1

--- a/solution.py
+++ b/solution.py
@@ -175,63 +175,139 @@
     )(joined, joined, joined, grad_attended, attended, lse, fq, fk)
 
 
-def scatter_sum(blocks, me, order, wire):
-    n = blocks.shape[0]
-    rest = blocks.shape[1:]
-    low_bits = n.bit_length() - 3
-    dims = (4,) + (2,) * low_bits
-    terms = [blocks.reshape(dims + rest)]
-    axes = ["top"] + list(range(low_bits - 1, -1, -1))
-
-    def pick(values, axis, index):
-        return lax.dynamic_index_in_dim(values, index, axis, keepdims=False)
-
-    def total(values):
-        out = values[0].astype(f32)
-        for value in values[1:]:
-            out = out + value.astype(f32)
-        return out
-
-    for bit in order:
-        axis = axes.index(bit)
-        mine = (me >> bit) & 1
-        sent = total([pick(term, axis, 1 - mine) for term in terms]).astype(wire)
-        came = lax.ppermute(sent, "dp", [(i, i ^ (1 << bit)) for i in range(n)])
-        terms = [pick(term, axis, mine) for term in terms] + [came]
-        axes.remove(bit)
-    mine = me >> low_bits
-    arrived = []
-    for k in range(1, 4):
-        sent = total([pick(term, 0, mine ^ k) for term in terms]).astype(wire)
-        arrived.append(lax.ppermute(sent, "dp", [(i, i ^ (k << low_bits)) for i in range(n)]))
-    return total([pick(term, 0, mine) for term in terms] + arrived)
+def suits(n, rows):
+    return n >= 8 and n & (n - 1) == 0 and rows % 8 == 0
+
+
+def middle_bits(n):
+    return list(range(1, n.bit_length() - 3))
+
+
+def total(values):
+    out = values[0].astype(f32)
+    for value in values[1:]:
+        out = out + value.astype(f32)
+    return out
+
+
+def pick(values, axis, index):
+    return lax.dynamic_index_in_dim(values, index, axis, keepdims=False)
+
+
+class ScatterSum:
+    def __init__(self, blocks, me, n, flip, wire):
+        self.n = n
+        self.me = me
+        self.wire = wire
+        self.low_bits = n.bit_length() - 3
+        middle = middle_bits(n)
+        self.order = [0] + (middle[::-1] if flip else middle)
+        self.axes = ["top"] + list(range(self.low_bits - 1, -1, -1))
+        self.terms = [blocks.reshape((4,) + (2,) * self.low_bits + blocks.shape[1:])]
+        self.result = None
+        self.pending = None
+
+    def sends(self):
+        if self.order:
+            self.bit = self.order.pop(0)
+            self.axis = self.axes.index(self.bit)
+            mine = (self.me >> self.bit) & 1
+            self.keep = mine
+            return [total([pick(t, self.axis, 1 - mine) for t in self.terms]).astype(self.wire)]
+        self.bit = None
+        self.axis = 0
+        mine = self.me >> self.low_bits
+        self.keep = mine
+        return [total([pick(t, 0, mine ^ k) for t in self.terms]).astype(self.wire) for k in (1, 2, 3)]
+
+    def launch(self, sends):
+        if self.bit is not None:
+            partners = [1 << self.bit]
+        else:
+            partners = [k << self.low_bits for k in (1, 2, 3)]
+        self.pending = [
+            lax.ppermute(sent, "dp", [(i, i ^ p) for i in range(self.n)])
+            for sent, p in zip(sends, partners)
+        ]
+
+    def land(self, came):
+        self.pending = None
+        self.terms = [pick(t, self.axis, self.keep) for t in self.terms] + list(came)
+        if self.bit is not None:
+            self.axes.remove(self.bit)
+        else:
+            self.result = total(self.terms)
+
+
+class Gather:
+    def __init__(self, block, me, n):
+        self.n = n
+        self.me = me
+        self.bits = list(range(n.bit_length() - 1))
+        self.held = block
+        self.result = None
+        self.pending = None
+
+    def sends(self):
+        self.bit = self.bits.pop(0)
+        return [self.held]
+
+    def launch(self, sends):
+        p = 1 << self.bit
+        self.pending = [lax.ppermute(sends[0], "dp", [(i, i ^ p) for i in range(self.n)])]
+
+    def land(self, came):
+        self.pending = None
+        upper = ((self.me >> self.bit) & 1) == 1
+        low = jnp.where(upper, came[0], self.held)
+        high = jnp.where(upper, self.held, came[0])
+        self.held = jnp.concatenate([low, high], axis=0)
+        if not self.bits:
+            self.result = self.held
+
+
+class Done:
+    def __init__(self, result):
+        self.result = result
+        self.pending = None
+
+
+def fence(main, exchanges):
+    flying = [e for e in exchanges if e.pending is not None]
+    main, came = lax.optimization_barrier((main, [e.pending for e in flying]))
+    for e, values in zip(flying, came):
+        e.land(values)
+    ready = [e for e in exchanges if e.result is None]
+    main, sends = lax.optimization_barrier((main, [e.sends() for e in ready]))
+    for e, values in zip(ready, sends):
+        e.launch(values)
+    return main
 
 
 def reduce_rows(grad, me, n, flip):
     rows, columns = grad.shape
-    if n < 8 or n & (n - 1) or (rows // n) % 8:
-        return lax.psum_scatter(grad.astype(f32), "dp", scatter_dimension=0, tiled=True)
-    low_bits = n.bit_length() - 3
-    middle = list(range(1, low_bits))
-    order = [0] + (middle[::-1] if flip else middle)
-    return scatter_sum(grad.reshape(n, rows // n, columns), me, order, bf16)
-
-
-def reduce_small(vectors, me, n):
+    if not suits(n, rows // n):
+        return Done(lax.psum_scatter(grad.astype(f32), "dp", scatter_dimension=0, tiled=True))
+    return ScatterSum(grad.reshape(n, rows // n, columns), me, n, flip, bf16)
+
+
+def pack_small(vectors, me, n):
     pieces = [vector.reshape(LAYERS, n, -1).transpose(1, 0, 2).reshape(n, -1) for vector in vectors]
     packed = jnp.concatenate(pieces, axis=1)
-    size = packed.shape[1]
-    padded = jnp.pad(packed, ((0, 0), (0, -size % 1024))).reshape(n, -1, 128)
-    if n < 8 or n & (n - 1):
-        mine = lax.psum_scatter(padded, "dp", scatter_dimension=0, tiled=False)
-    else:
-        mine = scatter_sum(padded, me, list(range(n.bit_length() - 3)), f32)
-    flat = mine.reshape(-1)
+    padded = jnp.pad(packed, ((0, 0), (0, -packed.shape[1] % 1024))).reshape(n, -1, 128)
+    sizes = [piece.shape[1] for piece in pieces]
+    if not suits(n, 8):
+        return Done(lax.psum_scatter(padded, "dp", scatter_dimension=0, tiled=False)), sizes
+    return ScatterSum(padded, me, n, False, f32), sizes
+
+
+def unpack_small(result, sizes):
+    flat = result.reshape(-1)
     outs = []
     start = 0
-    for piece in pieces:
-        outs.append(flat[start : start + piece.shape[1]].reshape(LAYERS, -1))
-        start += piece.shape[1]
+    for size in sizes:
+        outs.append(flat[start : start + size].reshape(LAYERS, -1))
+        start += size
     return outs
 
 
@@ -255,32 +331,44 @@
     return back(grad_normed)
 
 
-def layer_backward(grad_stream, cache, weights, fq, fk, me, n):
+def layer_backward(grad_stream, cache, weights, fq, fk, me, n, live):
     stream, normed, joined, attended, lse, middle, normed_two, hidden, activated = cache
     gain_one, shift_one, qkv_w, qv_b, out_w, out_b, gain_two, shift_two, up_w, up_b, down_w, down_b = weights
     grad_low = grad_stream.astype(bf16)
     grad_down_w = jnp.einsum("tf,td->fd", activated, grad_low, preferred_element_type=f32).astype(bf16)
-    down_sum = reduce_rows(grad_down_w, me, n, False)
     grad_down_b = jnp.sum(grad_low.astype(f32), axis=0)
     grad_activated = dot_nt(grad_low, down_w)
     unused, gelu_back = jax.vjp(partial(jax.nn.gelu, approximate=False), hidden)
     grad_hidden = gelu_back(grad_activated)[0].astype(bf16)
     grad_up_w = jnp.einsum("td,tf->df", normed_two, grad_hidden, preferred_element_type=f32).astype(bf16)
+    grad_up_b = jnp.sum(grad_hidden.astype(f32), axis=0)
+    down_sum = reduce_rows(grad_down_w, me, n, False)
     up_sum = reduce_rows(grad_up_w, me, n, True)
-    grad_up_b = jnp.sum(grad_hidden.astype(f32), axis=0)
+    live += [down_sum, up_sum]
+    grad_hidden = fence(grad_hidden, live)
     grad_normed = dot_nt(grad_hidden, up_w)
     grad_input, grad_gain_two, grad_shift_two = norm_backward(grad_normed, middle, gain_two, shift_two)
     grad_middle = grad_stream + grad_input
     branch = grad_middle.astype(bf16)
     grad_out_w = jnp.einsum("tc,td->cd", attended, branch, preferred_element_type=f32).astype(bf16)
-    out_sum = reduce_rows(grad_out_w, me, n, True)
     grad_out_b = jnp.sum(branch.astype(f32), axis=0)
     grad_attended = dot_nt(branch, out_w).astype(bf16)
+    out_sum = reduce_rows(grad_out_w, me, n, True)
+    live.append(out_sum)
+    grad_attended = fence(grad_attended, live)
     grad_joined, column_sums = attend_backward(joined, grad_attended, attended, lse, fq, fk)
+    grad_joined = fence(grad_joined, live)
     grad_qkv_w = jnp.einsum("td,te->de", normed, grad_joined, preferred_element_type=f32).astype(bf16)
-    qkv_sum = reduce_rows(grad_qkv_w, me, n, False)
+    half = grad_qkv_w.shape[1] // 2
+    qkv_sums = [
+        reduce_rows(grad_qkv_w[:, :half], me, n, False),
+        reduce_rows(grad_qkv_w[:, half:], me, n, True),
+    ]
+    live += qkv_sums
+    grad_joined = fence(grad_joined, qkv_sums)
     grad_qv_b = column_sums.reshape(-1)
     grad_normed = dot_nt(grad_joined, qkv_w)
+    grad_normed = fence(grad_normed, live)
     grad_input, grad_gain_one, grad_shift_one = norm_backward(grad_normed, stream, gain_one, shift_one)
     small = (
         grad_gain_one,
@@ -292,7 +380,7 @@
         grad_up_b,
         grad_down_b,
     )
-    return grad_middle + grad_input, (qkv_sum, out_sum, up_sum, down_sum), small
+    return grad_middle + grad_input, (qkv_sums, out_sum, up_sum, down_sum), small
 
 
 def local(n, *arguments):
@@ -335,11 +423,11 @@
     pooled = (
         jnp.dot(member, stream, precision=HIGHEST, preferred_element_type=f32) / counts[:, None]
     )
-    gathered = lax.all_gather(pooled.astype(bf16), "dp", axis=0, tiled=True)
-    scores = dot32(gathered, cls_weight) + cls_bias.astype(f32)
-    logits = jnp.where(live_columns[None, :], scores, 0.0)
-    grad_cls_weight = jnp.einsum("id,ic->dc", gathered, masked_grad, preferred_element_type=f32)
-    grad_cls_bias = jnp.sum(masked_grad.astype(f32), axis=0)
+    low_pooled = pooled.astype(bf16)
+    if suits(n, 8):
+        gather = Gather(low_pooled, me, n)
+    else:
+        gather = Done(lax.all_gather(low_pooled, "dp", axis=0, tiled=True))
     grad_stream = jnp.einsum(
         "it,id->td",
         member,
@@ -347,15 +435,30 @@
         precision=HIGHEST,
         preferred_element_type=f32,
     )
+    live = [gather]
+    grad_stream = fence(grad_stream, live)
     large = [None] * LAYERS
     small = [None] * LAYERS
     for layer in reversed(range(LAYERS)):
         grad_stream, large[layer], small[layer] = layer_backward(
-            grad_stream, caches[layer], layers[layer], fq, fk, me, n
+            grad_stream, caches[layer], layers[layer], fq, fk, me, n, live
         )
-    qkv_sum, out_sum, up_sum, down_sum = (jnp.stack(pair) for pair in zip(*large))
-    gain_one, shift_one, qv_b, out_b, gain_two, shift_two, up_b, down_b = reduce_small(
-        [jnp.stack(pair) for pair in zip(*small)], me, n
+    small_sum, sizes = pack_small([jnp.stack(pair) for pair in zip(*small)], me, n)
+    live.append(small_sum)
+    while any(e.result is None for e in live):
+        grad_stream = fence(grad_stream, live)
+    gathered = gather.result
+    scores = dot32(gathered, cls_weight) + cls_bias.astype(f32)
+    logits = jnp.where(live_columns[None, :], scores, 0.0)
+    grad_cls_weight = jnp.einsum("id,ic->dc", gathered, masked_grad, preferred_element_type=f32)
+    grad_cls_bias = jnp.sum(masked_grad.astype(f32), axis=0)
+    qkv_sums, out_sum, up_sum, down_sum = zip(*large)
+    qkv_sum = jnp.stack([jnp.concatenate([e.result for e in pair], axis=1) for pair in qkv_sums])
+    out_sum, up_sum, down_sum = (
+        jnp.stack([e.result for e in pair]) for pair in (out_sum, up_sum, down_sum)
+    )
+    gain_one, shift_one, qv_b, out_b, gain_two, shift_two, up_b, down_b = unpack_small(
+        small_sum.result, sizes
     )
     return (
         logits,

time: 744 us -> 734 us (0.987)
  blocking collectives: 45.4 us -> 0 us
  other arithmetic: 77.1 us -> 111 us
  waiting for transfers between devices: 107 us -> 84.1 us
  starting transfers between devices: 59 us -> 79.1 us
  local copies, waits for them, and re-layouts: 56.7 us -> 66.9 us
    all_gather x1 -> x0, blocking collectives: 45.4 us -> none  [local(): gathered = lax.all_gather(pooled.astype(bf16), 'dp', axis=0, tiled=True)]
    ppermute x54 -> x71, waiting for transfers between devices: 107 us -> 84 us  [the longest x66 82.4 us: launch(): lax.ppermute(sent, 'dp', [(i, i ^ p) for i in range(self.n)])]
    convert_element_type x24 -> x30, other arithmetic: 30.4 us -> 53.5 us  [the longest x20 35.7 us: sends(): total([pick(t, self.axis, 1 - mine) for t in self.terms]).astype(self.wire)]
    ppermute x54 -> x71, starting transfers between devices: 59 us -> 79 us  [the longest x66 71.6 us: launch(): lax.ppermute(sent, 'dp', [(i, i ^ p) for i in range(self.n)])]
    optimization_barrier x0 -> x3, local copies, waits for them, and re-layouts: none -> 11 us  [fence(): main, sends = lax.optimization_barrier((main, [e.sends() for e in ready]))]
    dot_general x4 -> x2, local copies, waits for them, and re-layouts: 14.8 us -> 7.27 us  [dot_nt(): return lax.dot_general(left, right, NT, preferred_element_type=f32)]
    unnamed x274 -> x326, local copies, waits for them, and re-layouts: 14.6 us -> 20.9 us
    reduce_sum x6 -> x8, other arithmetic: 15.7 us -> 20.6 us  [layer_norm(): return center * lax.rsqrt(spread + EPSILON) * gain_vector + shift_vector]
  transfers between devices with their start and end apart: 55 -> 72, of which waited for: 20 -> 18; matrix products, arithmetic and copies ran while one was open for 28% -> 32% of each run, Pallas kernels for 6% -> 16%
where the time goes in v2:
time: 734 us; the launch traced here: 725 us
  matrix products  250 us (34%)
  Pallas kernels  116 us (16%)
  other arithmetic  111 us (15%)
  waiting for transfers between devices  84.1 us (11%)
  starting transfers between devices  79.1 us (11%)
  local copies, waits for them, and re-layouts  66.9 us (9%)
  between operations  17.7 us (2%)
    dot_general x9, matrix products, dot32(): return jnp.dot(left, right, preferred_element_type=f32)  115 us
    ppermute x66, waiting for transfers between devices, launch(): lax.ppermute(sent, 'dp', [(i, i ^ p) for i in range(self.n)])  82.4 us
    dot_general x9, matrix products, dot_nt(): return lax.dot_general(left, right, NT, preferred_element_type=f32)  77.1 us
    pallas_call x2, Pallas kernels, attend_backward(): pl.pallas_call(partial(attend_backward_kernel, chunk=rows // 2), grid=(n,...  74.3 us
    ppermute x66, starting transfers between devices, launch(): lax.ppermute(sent, 'dp', [(i, i ^ p) for i in range(self.n)])  71.6 us
    pallas_call x2, Pallas kernels, attend_forward(): pl.pallas_call(partial(attend_forward_kernel, chunk=rows), grid=(n,), in_...  41.6 us
    convert_element_type x20, other arithmetic, sends(): total([pick(t, self.axis, 1 - mine) for t in self.terms]).astype(self.wire)  35.7 us
    unnamed x326, local copies, waits for them, and re-layouts  20.9 us
  transfers between devices with their start and end apart: 72, of which 18 were waited for; matrix products, arithmetic and copies ran while one was open for 32% of the time, Pallas kernels for 16%

profile of v2, /device:TPU:0, one launch (start us, length us, event | category | flops | bytes accessed | tf_op | source)
XLA Modules:
  0.0 724.7 jit_solution(6080378683017154070)
XLA Ops:
  16.7 7.8 %add_convert_fusion.3.q_ref.k_ref.v_ref = bf16[1024,2304]{1,0:T(8,128)(2,1)} fusion(f32[2304]{0:T(1024)S(1)} %get-tuple-element.516, bf16[2,768,2304]{2,1,0:T(8,128)(2,1)} %param.25, bf16[1024,768]{0,1:T(8,128)(2,1)S(1)} %copy.133, f32[768]{0:T(1024)S(1)} %get-tuple-element.443, f32[768]{0:T(1024)S(1)} %get-tuple-element.535, f32[1024]{0:T(1024)S(1)} %fusion.315, ...), kind=kOutput, calls=%fused_computation.37 | convolution fusion | flops 3633315840 | bytes 9853952 | tf_op jit(solution)/shard_map/dot_general | solution.py:28
  24.5 20.9 %attend_forward.2 = (bf16[1024,768]{1,0:T(8,128)(2,1)}, f32[6,2,1024]{2,1,0:T(2,128)}) custom-call(bf16[1024,2304]{1,0:T(8,128)(2,1)} %add_convert_fusion.3.q_ref.k_ref.v_ref, bf16[1024,2304]{1,0:T(8,128)(2,1)} %add_convert_fusion.3.q_ref.k_ref.v_ref, bf16[1024,2304]{1,0:T(8,128)(2,1)} %add_convert_fusion.3.q_ref.k_ref.v_ref, ...), custom_call_target="tpu_custom_call" | custom-call | flops 12884901888 | bytes 7864320 | tf_op jit(solution)/shard_map/attend_forward/pallas_call | solution.py:74
  50.4 38.4 %multiply_convert_fusion.1 = (bf16[1024,3072]{1,0:T(8,128)(2,1)}, f32[1024,3072]{1,0:T(8,128)}, f32[1024,3072]{1,0:T(8,128)}) fusion(f32[3072]{0:T(1024)S(1)} %bitcast.1161, bf16[2,768,3072]{2,1,0:T(8,128)(2,1)} %param.31, f32[1024,768]{0,1:T(8,128)S(1)} %get-tuple-element.520, f32[768]{0:T(1024)S(1)} %get-tuple-element.437, ...), kind=kOutput, calls=%fused_computation.21 | convolution fusion | flops 5043388416 | bytes 39348224 | tf_op jit(solution)/shard_map/dot_general | solution.py:28
  88.9 7.7 %fusion.339 = (f32[1024]{0:T(1024)S(1)}, f32[1024,768]{0,1:T(8,128)S(1)}) fusion(f32[768]{0:T(1024)S(1)} %get-tuple-element.433, f32[1024,768]{0,1:T(8,128)S(1)} %get-tuple-element.520, bf16[1024,3072]{1,0:T(8,128)(2,1)} %get-tuple-element.458, bf16[2,3072,768]{2,1,0:T(8,128)(2,1)S(1)} %bitcast.1166), kind=kOutput, calls=%fused_computation.749 | convolution fusion | flops 4834196480 | bytes 17309696 | tf_op jit(solution)/shard_map/dot_general | solution.py:28
  98.5 7.7 %add_convert_fusion.2.q_ref.k_ref.v_ref = bf16[1024,2304]{1,0:T(8,128)(2,1)} fusion(f32[2304]{0:T(1024)S(1)} %get-tuple-element.515, bf16[2,768,2304]{2,1,0:T(8,128)(2,1)} %param.25, f32[1024,768]{0,1:T(8,128)S(1)} %get-tuple-element.523, f32[768]{0:T(1024)S(1)} %get-tuple-element.442, f32[768]{0:T(1024)S(1)} %get-tuple-element.536, f32[1024]{0:T(1024)S(1)} %fusion.317, ...), kind=kOutput, calls=%fused_computation.36 | convolution fusion | flops 3632529408 | bytes 11426816 | tf_op jit(solution)/shard_map/dot_general | solution.py:28
  106.2 20.7 %attend_forward.3 = (bf16[1024,768]{1,0:T(8,128)(2,1)}, f32[6,2,1024]{2,1,0:T(2,128)}) custom-call(bf16[1024,2304]{1,0:T(8,128)(2,1)} %add_convert_fusion.2.q_ref.k_ref.v_ref, bf16[1024,2304]{1,0:T(8,128)(2,1)} %add_convert_fusion.2.q_ref.k_ref.v_ref, bf16[1024,2304]{1,0:T(8,128)(2,1)} %add_convert_fusion.2.q_ref.k_ref.v_ref, ...), custom_call_target="tpu_custom_call" | custom-call | flops 12884901888 | bytes 7864320 | tf_op jit(solution)/shard_map/attend_forward/pallas_call | solution.py:74
  131.4 37.1 %multiply_convert_fusion = (bf16[1024,3072]{1,0:T(8,128)(2,1)S(1)}, f32[1024,3072]{1,0:T(8,128)}, f32[1024,3072]{1,0:T(8,128)}) fusion(f32[3072]{0:T(1024)S(1)} %bitcast.1163, bf16[2,768,3072]{2,1,0:T(8,128)(2,1)} %param.31, f32[1024,768]{0,1:T(8,128)S(1)} %get-tuple-element.525, f32[768]{0:T(1024)S(1)} %get-tuple-element.436, ...), kind=kOutput, calls=%fused_computation.8 | convolution fusion | flops 5043388416 | bytes 39348224 | tf_op jit(solution)/shard_map/dot_general | solution.py:28
  168.5 9.0 %fusion.17 = f32[1024,768]{0,1:T(8,128)S(1)} fusion(bf16[1024,3072]{1,0:T(8,128)(2,1)S(1)} %get-tuple-element.456, bf16[2,3072,768]{2,1,0:T(8,128)(2,1)} %param.33), kind=kOutput, calls=%fused_computation.56 | convolution fusion | flops 4831838208 | bytes 14155776 | tf_op jit(solution)/shard_map/dot_general | solution.py:28
  181.7 11.0 %convolution_convert_fusion.3 = bf16[3072,768]{1,0:T(8,128)(2,1)} fusion(bf16[1024,3072]{1,0:T(8,128)(2,1)} %copy-done.145, f32[1024,768]{1,0:T(8,128)S(1)} %fusion.234), kind=kOutput, calls=%fused_computation.41 | convolution fusion | flops 4834983936 | bytes 14155776 | tf_op jit(solution)/shard_map/tf,td->fd/dot_general | solution.py:338
  193.0 18.8 %convert_reduce_fusion = (f32[3072]{0:T(1024)S(1)}, bf16[1024,3072]{1,0:T(8,128)(2,1)}) fusion(f32[1024,3072]{1,0:T(8,128)} %get-tuple-element.457, bf16[2,3072,768]{2,1,0:T(8,128)(2,1)} %param.33, f32[1024,768]{1,0:T(8,128)} %copy-done.7, f32[1024,3072]{1,0:T(8,128)} %get-tuple-element.526, f32[3072]{0:T(1024)S(1)} %bitcast.1164), kind=kOutput, calls=%fused_computation.4 | convolution fusion | flops 4886098944 | bytes 39346176 | tf_op jit(solution)/shard_map/dot_general | solution.py:32
  211.8 8.9 %convolution_convert_fusion.2 = bf16[768,3072]{1,0:T(8,128)(2,1)S(1)} fusion(bf16[1024,3072]{1,0:T(8,128)(2,1)} %get-tuple-element.200, f32[1024,768]{0,1:T(8,128)S(1)} %get-tuple-element.525, f32[768]{0:T(1024)S(1)} %get-tuple-element.436, f32[768]{0:T(1024)S(1)} %get-tuple-element.538, f32[1024]{0:T(1024)S(1)} %fusion.318, ...), kind=kOutput, calls=%fused_computation.40 | convolution fusion | flops 4838129664 | bytes 14170112 | tf_op jit(solution)/shard_map/td,tf->df/dot_general | solution.py:343
  229.7 9.8 %fusion.341 = (f32[768]{0:T(1024)S(1)}, f32[1024,768]{1,0:T(8,128)}) fusion(bf16[1024,3072]{1,0:T(8,128)(2,1)} %get-tuple-element.200, bf16[2,768,3072]{2,1,0:T(8,128)(2,1)} %param.31), kind=kOutput, calls=%fused_computation.751 | convolution fusion | flops 4832623616 | bytes 14158848 | tf_op jit(solution)/shard_map/dot_general | solution.py:32
  269.1 37.1 %attend_backward.2 = (bf16[1024,2304]{1,0:T(8,128)(2,1)}, f32[2,768]{1,0:T(2,128)}) custom-call(bf16[1024,2304]{1,0:T(8,128)(2,1)} %add_convert_fusion.2.q_ref.k_ref.v_ref, bf16[1024,2304]{1,0:T(8,128)(2,1)} %add_convert_fusion.2.q_ref.k_ref.v_ref, bf16[1024,2304]{1,0:T(8,128)(2,1)} %add_convert_fusion.2.q_ref.k_ref.v_ref, ...), custom_call_target="tpu_custom_call" | custom-call | flops 32212254720 | bytes 12582912 | tf_op jit(solution)/shard_map/attend_backward/pallas_call | solution.py:149
  336.4 11.0 %collective-permute-done.11 = bf16[4,2,24,768]{3,2,1,0:T(8,128)(2,1)S(1)} collective-permute-done((bf16[4,2,24,768]{3,2,1,0:T(8,128)(2,1)S(1)}, bf16[4,2,24,768]{3,2,1,0:T(8,128)(2,1)S(1)}, u32[]{:S(2)}, u32[]{:S(2)}) %collective-permute-start.11) | collective-permute-done | bytes 294944 | tf_op jit(solution)/shard_map/ppermute | solution.py:229
  374.9 7.0 convolution_convert_fusion.1
  382.0 19.6 %convert_reduce_fusion.1 = (f32[3072]{0:T(1024)}, bf16[1024,3072]{1,0:T(8,128)(2,1)}) fusion(f32[1024,3072]{1,0:T(8,128)} %get-tuple-element.459, bf16[2,3072,768]{2,1,0:T(8,128)(2,1)} %param.33, f32[1024,768]{0,1:T(8,128)} %copy-done.16, f32[1024,3072]{1,0:T(8,128)} %get-tuple-element.521, f32[3072]{0:T(1024)S(1)} %bitcast.1162), kind=kOutput, calls=%fused_computation.5 | convolution fusion | flops 4886098944 | bytes 39346176 | tf_op jit(solution)/shard_map/dot_general | solution.py:32
  401.6 8.8 %convolution_convert_fusion = bf16[768,3072]{1,0:T(8,128)(2,1)S(1)} fusion(bf16[1024,3072]{1,0:T(8,128)(2,1)} %get-tuple-element.251, f32[1024,768]{0,1:T(8,128)S(1)} %copy-done.11, f32[768]{0:T(1024)S(1)} %copy-done.130, f32[768]{0:T(1024)S(1)} %copy-done.101, f32[1024]{0:T(1024)S(1)} %copy-done.103, f32[1024]{0:T(1024)S(1)} %copy-done.74), kind=kOutput, calls=%fused_computation.38 | convolution fusion | flops 4838129664 | bytes 14170112 | tf_op jit(solution)/shard_map/td,tf->df/dot_general | solution.py:343
  430.0 12.3 %collective-permute-done.19 = bf16[24,3072]{1,0:T(8,128)(2,1)} collective-permute-done((bf16[24,3072]{1,0:T(8,128)(2,1)}, bf16[24,3072]{1,0:T(8,128)(2,1)}, u32[]{:S(2)}, u32[]{:S(2)}) %collective-permute-start.19) | collective-permute-done | bytes 147488 | tf_op jit(solution)/shard_map/ppermute | solution.py:229
  453.6 10.3 %fusion.342 = (f32[768]{0:T(1024)}, f32[1024,768]{1,0:T(8,128)}) fusion(bf16[1024,3072]{1,0:T(8,128)(2,1)} %get-tuple-element.251, bf16[2,768,3072]{2,1,0:T(8,128)(2,1)} %param.31), kind=kOutput, calls=%fused_computation.752 | convolution fusion | flops 4832623616 | bytes 14158848 | tf_op jit(solution)/shard_map/dot_general | solution.py:32
  516.6 37.2 %attend_backward.3 = (bf16[1024,2304]{1,0:T(8,128)(2,1)}, f32[2,768]{1,0:T(2,128)}) custom-call(bf16[1024,2304]{1,0:T(8,128)(2,1)} %add_convert_fusion.3.q_ref.k_ref.v_ref, bf16[1024,2304]{1,0:T(8,128)(2,1)} %add_convert_fusion.3.q_ref.k_ref.v_ref, bf16[1024,2304]{1,0:T(8,128)(2,1)} %add_convert_fusion.3.q_ref.k_ref.v_ref, ...), custom_call_target="tpu_custom_call" | custom-call | flops 32212254720 | bytes 12582912 | tf_op jit(solution)/shard_map/attend_backward/pallas_call | solution.py:149
  572.3 7.0 convolution_convert_fusion.4
  592.0 15.4 %collective-permute-done.42 = bf16[4,2,24,768]{3,2,1,0:T(8,128)(2,1)S(1)} collective-permute-done((bf16[4,2,24,768]{3,2,1,0:T(8,128)(2,1)S(1)}, bf16[4,2,24,768]{3,2,1,0:T(8,128)(2,1)S(1)}, u32[]{:S(2)}, u32[]{:S(2)}) %collective-permute-start.42) | collective-permute-done | bytes 294944 | tf_op jit(solution)/shard_map/ppermute | solution.py:229
  638.6 8.0 %collective-permute-done.46 = bf16[96,768]{1,0:T(8,128)(2,1)S(1)} collective-permute-done((bf16[96,768]{1,0:T(8,128)(2,1)}, bf16[96,768]{1,0:T(8,128)(2,1)S(1)}, u32[]{:S(2)}, u32[]{:S(2)}) %collective-permute-start.46) | collective-permute-done | bytes 147488 | tf_op jit(solution)/shard_map/ppermute | solution.py:229
  649.2 10.1 %collective-permute-done.49 = bf16[24,3072]{1,0:T(8,128)(2,1)S(1)} collective-permute-done((bf16[24,3072]{1,0:T(8,128)(2,1)}, bf16[24,3072]{1,0:T(8,128)(2,1)S(1)}, u32[]{:S(2)}, u32[]{:S(2)}) %collective-permute-start.49) | collective-permute-done | bytes 147488 | tf_op jit(solution)/shard_map/ppermute | solution.py:229
  (668 shorter events, 325.6 us)
Async XLA Ops:
  7.2 172.1 %reduce-scatter.2.cloned.1.call-start = ((), (), s32[]{:S(2)}) async-start(), calls=%async_computation.1 | async-start | bytes 1622016 | tf_op jit(solution)/shard_map/reduce_scatter | solution.py:414
  266.9 40.6 %collective-permute-start.5 = (bf16[4,2,96,768]{3,2,1,0:T(8,128)(2,1)}, bf16[4,2,96,768]{3,2,1,0:T(8,128)(2,1)S(1)}, u32[]{:S(2)}, u32[]{:S(2)}) collective-permute-start(bf16[4,2,96,768]{3,2,1,0:T(8,128)(2,1)} %fusion.62), channel_id=1, source_target_pairs={{0,2},{1,3},{2,0},{3,1},{4,6},{5,7},{6,4},{7,5},{8,10},{9,11},{10,... | collective-permute-start | bytes 3538952 | tf_op jit(solution)/shard_map/ppermute | solution.py:229
  267.0 40.5 %collective-permute-start.6 = (bf16[4,2,24,3072]{3,2,1,0:T(8,128)(2,1)}, bf16[4,2,24,3072]{3,2,1,0:T(8,128)(2,1)S(1)}, u32[]{:S(2)}, u32[]{:S(2)}) collective-permute-start(bf16[4,2,24,3072]{3,2,1,0:T(8,128)(2,1)} %fusion.61), channel_id=1, source_target_pairs={{0,4},{1,5},{2,6},{3,7},{4,0},{5,1},{6,2},{7,3},{8,12},{9,13},{10,... | collective-permute-start | bytes 3538952 | tf_op jit(solution)/shard_map/ppermute | solution.py:229
  269.0 38.5 %collective-permute-start.7 = (bf16[4,2,2,24,768]{4,3,2,1,0:T(8,128)(2,1)S(1)}, bf16[4,2,2,24,768]{4,3,2,1,0:T(8,128)(2,1)}, u32[]{:S(2)}, u32[]{:S(2)}) collective-permute-start(bf16[4,2,2,24,768]{4,3,2,1,0:T(8,128)(2,1)S(1)} %dynamic-slice_bitcast_fusion.9), channel_id=1, source_target_pairs={{0,1},{1,0},{2,3},{3,2},{4,5},{5,4},{6,7},{7,6},{8,9},{9,8},{10,11... | collective-permute-start | bytes 1769480 | tf_op jit(solution)/shard_map/ppermute | solution.py:229
  269.0 38.5 %collective-permute-start.4 = (bf16[64,768]{1,0:T(8,128)(2,1)S(1)}, bf16[64,768]{1,0:T(8,128)(2,1)S(1)}, u32[]{:S(2)}, u32[]{:S(2)}) collective-permute-start(bf16[64,768]{1,0:T(8,128)(2,1)S(1)} %pad_maximum_fusion.9), channel_id=1, source_target_pairs={{0,4},{1,5},{2,6},{3,7},{4,0},{5,1},{6,2},{7,3},{8,12},{9,13},{10,... | collective-permute-start | bytes 294920 | tf_op jit(solution)/shard_map/ppermute | solution.py:257
  324.0 23.4 %collective-permute-start.12 = (bf16[4,2,2,24,1152]{4,3,2,1,0:T(8,128)(2,1)S(1)}, bf16[4,2,2,24,1152]{4,3,2,1,0:T(8,128)(2,1)S(1)}, u32[]{:S(2)}, u32[]{:S(2)}) collective-permute-start(bf16[4,2,2,24,1152]{4,3,2,1,0:T(8,128)(2,1)S(1)} %dynamic-slice_bitcast_fusion.7), channel_id=1, source_target_pairs={{0,1},{1,0},{2,3},{3,2},{4,5},{5,4},{6,7},{7,6},{8,9},{9,8},{10,11... | collective-permute-start | bytes 2654216 | tf_op jit(solution)/shard_map/ppermute | solution.py:229
  324.0 23.4 %collective-permute-start.13 = (bf16[4,2,2,24,1152]{4,3,2,1,0:T(8,128)(2,1)S(1)}, bf16[4,2,2,24,1152]{4,3,2,1,0:T(8,128)(2,1)S(1)}, u32[]{:S(2)}, u32[]{:S(2)}) collective-permute-start(bf16[4,2,2,24,1152]{4,3,2,1,0:T(8,128)(2,1)S(1)} %dynamic-slice_bitcast_fusion.6), channel_id=1, source_target_pairs={{0,1},{1,0},{2,3},{3,2},{4,5},{5,4},{6,7},{7,6},{8,9},{9,8},{10,11... | collective-permute-start | bytes 2654216 | tf_op jit(solution)/shard_map/ppermute | solution.py:229
  368.4 79.7 %collective-permute-start.22 = (bf16[4,2,24,1152]{3,2,1,0:T(8,128)(2,1)}, bf16[4,2,24,1152]{3,2,1,0:T(8,128)(2,1)}, u32[]{:S(2)}, u32[]{:S(2)}) collective-permute-start(bf16[4,2,24,1152]{3,2,1,0:T(8,128)(2,1)} %fusion.90), channel_id=1, source_target_pairs={{0,2},{1,3},{2,0},{3,1},{4,6},{5,7},{6,4},{7,5},{8,10},{9,11},{10,... | collective-permute-start | bytes 1327112 | tf_op jit(solution)/shard_map/ppermute | solution.py:229
  369.0 79.1 %collective-permute-start.23 = (bf16[4,2,24,1152]{3,2,1,0:T(8,128)(2,1)}, bf16[4,2,24,1152]{3,2,1,0:T(8,128)(2,1)}, u32[]{:S(2)}, u32[]{:S(2)}) collective-permute-start(bf16[4,2,24,1152]{3,2,1,0:T(8,128)(2,1)} %fusion.89), channel_id=1, source_target_pairs={{0,4},{1,5},{2,6},{3,7},{4,0},{5,1},{6,2},{7,3},{8,12},{9,13},{10,... | collective-permute-start | bytes 1327112 | tf_op jit(solution)/shard_map/ppermute | solution.py:229
  370.5 43.7 %collective-permute-start.15 = (bf16[96,768]{1,0:T(8,128)(2,1)}, bf16[96,768]{1,0:T(8,128)(2,1)}, u32[]{:S(2)}, u32[]{:S(2)}) collective-permute-start(bf16[96,768]{1,0:T(8,128)(2,1)} %get-tuple-element.237), channel_id=1, source_target_pairs={{0,8},{1,9},{2,10},{3,11},{4,12},{5,13},{6,14},{7,15},{8,0},{9,1},... | collective-permute-start | bytes 442376 | tf_op jit(solution)/shard_map/ppermute | solution.py:229
  371.0 45.1 %collective-permute-start.16 = (bf16[96,768]{1,0:T(8,128)(2,1)}, bf16[96,768]{1,0:T(8,128)(2,1)}, u32[]{:S(2)}, u32[]{:S(2)}) collective-permute-start(bf16[96,768]{1,0:T(8,128)(2,1)} %get-tuple-element.238), channel_id=1, source_target_pairs={{0,16},{1,17},{2,18},{3,19},{4,20},{5,21},{6,22},{7,23},{8,24},{9,... | collective-permute-start | bytes 442376 | tf_op jit(solution)/shard_map/ppermute | solution.py:229
  373.6 43.8 %collective-permute-start.17 = (bf16[96,768]{1,0:T(8,128)(2,1)}, bf16[96,768]{1,0:T(8,128)(2,1)}, u32[]{:S(2)}, u32[]{:S(2)}) collective-permute-start(bf16[96,768]{1,0:T(8,128)(2,1)} %get-tuple-element.239), channel_id=1, source_target_pairs={{0,24},{1,25},{2,26},{3,27},{4,28},{5,29},{6,30},{7,31},{8,16},{9,... | collective-permute-start | bytes 442376 | tf_op jit(solution)/shard_map/ppermute | solution.py:229
  414.3 33.9 %collective-permute-start.14 = (bf16[256,768]{1,0:T(8,128)(2,1)}, bf16[256,768]{1,0:T(8,128)(2,1)}, u32[]{:S(2)}, u32[]{:S(2)}) collective-permute-start(bf16[256,768]{1,0:T(8,128)(2,1)} %pad_maximum_fusion.6), channel_id=1, source_target_pairs={{0,16},{1,17},{2,18},{3,19},{4,20},{5,21},{6,22},{7,23},{8,24},{9,... | collective-permute-start | bytes 1179656 | tf_op jit(solution)/shard_map/ppermute | solution.py:257
  417.4 24.8 %collective-permute-start.19 = (bf16[24,3072]{1,0:T(8,128)(2,1)}, bf16[24,3072]{1,0:T(8,128)(2,1)}, u32[]{:S(2)}, u32[]{:S(2)}) collective-permute-start(bf16[24,3072]{1,0:T(8,128)(2,1)} %get-tuple-element.241), channel_id=1, source_target_pairs={{0,16},{1,17},{2,18},{3,19},{4,20},{5,21},{6,22},{7,23},{8,24},{9,... | collective-permute-start | bytes 442376 | tf_op jit(solution)/shard_map/ppermute | solution.py:229
  476.2 25.0 %collective-permute-start.29 = (bf16[4,2,2,96,768]{4,3,2,1,0:T(8,128)(2,1)}, bf16[4,2,2,96,768]{4,3,2,1,0:T(8,128)(2,1)}, u32[]{:S(2)}, u32[]{:S(2)}) collective-permute-start(bf16[4,2,2,96,768]{4,3,2,1,0:T(8,128)(2,1)} %dynamic-slice_bitcast_fusion.1), channel_id=1, source_target_pairs={{0,1},{1,0},{2,3},{3,2},{4,5},{5,4},{6,7},{7,6},{8,9},{9,8},{10,11... | collective-permute-start | bytes 7077896 | tf_op jit(solution)/shard_map/ppermute | solution.py:229
  476.4 24.9 %collective-permute-start.30 = (bf16[4,2,2,24,3072]{4,3,2,1,0:T(8,128)(2,1)S(1)}, bf16[4,2,2,24,3072]{4,3,2,1,0:T(8,128)(2,1)}, u32[]{:S(2)}, u32[]{:S(2)}) collective-permute-start(bf16[4,2,2,24,3072]{4,3,2,1,0:T(8,128)(2,1)S(1)} %copy-done.28), channel_id=1, source_target_pairs={{0,1},{1,0},{2,3},{3,2},{4,5},{5,4},{6,7},{7,6},{8,9},{9,8},{10,11... | collective-permute-start | bytes 7077896 | tf_op jit(solution)/shard_map/ppermute | solution.py:229
  478.1 23.1 %collective-permute-start.27 = (bf16[4,24,1152]{2,1,0:T(8,128)(2,1)}, bf16[4,24,1152]{2,1,0:T(8,128)(2,1)}, u32[]{:S(2)}, u32[]{:S(2)}) collective-permute-start(bf16[4,24,1152]{2,1,0:T(8,128)(2,1)} %fusion.100), channel_id=1, source_target_pairs={{0,4},{1,5},{2,6},{3,7},{4,0},{5,1},{6,2},{7,3},{8,12},{9,13},{10,... | collective-permute-start | bytes 663560 | tf_op jit(solution)/shard_map/ppermute | solution.py:229
  511.5 55.5 %collective-permute-start.37 = (bf16[4,2,96,768]{3,2,1,0:T(8,128)(2,1)}, bf16[4,2,96,768]{3,2,1,0:T(8,128)(2,1)S(1)}, u32[]{:S(2)}, u32[]{:S(2)}) collective-permute-start(bf16[4,2,96,768]{3,2,1,0:T(8,128)(2,1)} %fusion.60), channel_id=1, source_target_pairs={{0,2},{1,3},{2,0},{3,1},{4,6},{5,7},{6,4},{7,5},{8,10},{9,11},{10,... | collective-permute-start | bytes 3538952 | tf_op jit(solution)/shard_map/ppermute | solution.py:229
  512.1 54.9 %collective-permute-start.38 = (bf16[4,2,24,3072]{3,2,1,0:T(8,128)(2,1)}, bf16[4,2,24,3072]{3,2,1,0:T(8,128)(2,1)}, u32[]{:S(2)}, u32[]{:S(2)}) collective-permute-start(bf16[4,2,24,3072]{3,2,1,0:T(8,128)(2,1)} %fusion.59), channel_id=1, source_target_pairs={{0,4},{1,5},{2,6},{3,7},{4,0},{5,1},{6,2},{7,3},{8,12},{9,13},{10,... | collective-permute-start | bytes 3538952 | tf_op jit(solution)/shard_map/ppermute | solution.py:229
  513.7 53.4 %collective-permute-start.39 = (bf16[4,2,2,24,768]{4,3,2,1,0:T(8,128)(2,1)S(1)}, bf16[4,2,2,24,768]{4,3,2,1,0:T(8,128)(2,1)}, u32[]{:S(2)}, u32[]{:S(2)}) collective-permute-start(bf16[4,2,2,24,768]{4,3,2,1,0:T(8,128)(2,1)S(1)} %copy-done.50), channel_id=1, source_target_pairs={{0,1},{1,0},{2,3},{3,2},{4,5},{5,4},{6,7},{7,6},{8,9},{9,8},{10,11... | collective-permute-start | bytes 1769480 | tf_op jit(solution)/shard_map/ppermute | solution.py:229
  513.7 40.2 %collective-permute-start.31 = (bf16[24,1152]{1,0:T(8,128)(2,1)S(1)}, bf16[24,1152]{1,0:T(8,128)(2,1)S(1)}, u32[]{:S(2)}, u32[]{:S(2)}) collective-permute-start(bf16[24,1152]{1,0:T(8,128)(2,1)S(1)} %get-tuple-element.267), channel_id=1, source_target_pairs={{0,8},{1,9},{2,10},{3,11},{4,12},{5,13},{6,14},{7,15},{8,0},{9,1},... | collective-permute-start | bytes 165896 | tf_op jit(solution)/shard_map/ppermute | solution.py:229
  513.9 41.5 %collective-permute-start.32 = (bf16[24,1152]{1,0:T(8,128)(2,1)S(1)}, bf16[24,1152]{1,0:T(8,128)(2,1)S(1)}, u32[]{:S(2)}, u32[]{:S(2)}) collective-permute-start(bf16[24,1152]{1,0:T(8,128)(2,1)S(1)} %get-tuple-element.268), channel_id=1, source_target_pairs={{0,16},{1,17},{2,18},{3,19},{4,20},{5,21},{6,22},{7,23},{8,24},{9,... | collective-permute-start | bytes 165896 | tf_op jit(solution)/shard_map/ppermute | solution.py:229
  632.2 27.0 %collective-permute-start.52 = (bf16[4,2,24,1152]{3,2,1,0:T(8,128)(2,1)}, bf16[4,2,24,1152]{3,2,1,0:T(8,128)(2,1)S(1)}, u32[]{:S(2)}, u32[]{:S(2)}) collective-permute-start(bf16[4,2,24,1152]{3,2,1,0:T(8,128)(2,1)} %fusion.88), channel_id=1, source_target_pairs={{0,2},{1,3},{2,0},{3,1},{4,6},{5,7},{6,4},{7,5},{8,10},{9,11},{10,... | collective-permute-start | bytes 1327112 | tf_op jit(solution)/shard_map/ppermute | solution.py:229
  633.6 25.6 %collective-permute-start.53 = (bf16[4,2,24,1152]{3,2,1,0:T(8,128)(2,1)}, bf16[4,2,24,1152]{3,2,1,0:T(8,128)(2,1)S(1)}, u32[]{:S(2)}, u32[]{:S(2)}) collective-permute-start(bf16[4,2,24,1152]{3,2,1,0:T(8,128)(2,1)} %fusion.87), channel_id=1, source_target_pairs={{0,4},{1,5},{2,6},{3,7},{4,0},{5,1},{6,2},{7,3},{8,12},{9,13},{10,... | collective-permute-start | bytes 1327112 | tf_op jit(solution)/shard_map/ppermute | solution.py:229
  (209 other events, 2561.1 us)
Sparse Core Ops, SparseCore 0:
  13.9 100.6 reduce-scatter.1

commit v3 on v1

--- a/solution.py
+++ b/solution.py
@@ -175,63 +175,136 @@
     )(joined, joined, joined, grad_attended, attended, lse, fq, fk)
 
 
-def scatter_sum(blocks, me, order, wire):
-    n = blocks.shape[0]
-    rest = blocks.shape[1:]
-    low_bits = n.bit_length() - 3
-    dims = (4,) + (2,) * low_bits
-    terms = [blocks.reshape(dims + rest)]
-    axes = ["top"] + list(range(low_bits - 1, -1, -1))
-
-    def pick(values, axis, index):
-        return lax.dynamic_index_in_dim(values, index, axis, keepdims=False)
-
-    def total(values):
-        out = values[0].astype(f32)
-        for value in values[1:]:
-            out = out + value.astype(f32)
-        return out
-
-    for bit in order:
-        axis = axes.index(bit)
-        mine = (me >> bit) & 1
-        sent = total([pick(term, axis, 1 - mine) for term in terms]).astype(wire)
-        came = lax.ppermute(sent, "dp", [(i, i ^ (1 << bit)) for i in range(n)])
-        terms = [pick(term, axis, mine) for term in terms] + [came]
-        axes.remove(bit)
-    mine = me >> low_bits
-    arrived = []
-    for k in range(1, 4):
-        sent = total([pick(term, 0, mine ^ k) for term in terms]).astype(wire)
-        arrived.append(lax.ppermute(sent, "dp", [(i, i ^ (k << low_bits)) for i in range(n)]))
-    return total([pick(term, 0, mine) for term in terms] + arrived)
-
-
-def reduce_rows(grad, me, n, flip):
-    rows, columns = grad.shape
-    if n < 8 or n & (n - 1) or (rows // n) % 8:
-        return lax.psum_scatter(grad.astype(f32), "dp", scatter_dimension=0, tiled=True)
-    low_bits = n.bit_length() - 3
-    middle = list(range(1, low_bits))
-    order = [0] + (middle[::-1] if flip else middle)
-    return scatter_sum(grad.reshape(n, rows // n, columns), me, order, bf16)
-
-
-def reduce_small(vectors, me, n):
-    pieces = [vector.reshape(LAYERS, n, -1).transpose(1, 0, 2).reshape(n, -1) for vector in vectors]
-    packed = jnp.concatenate(pieces, axis=1)
-    size = packed.shape[1]
-    padded = jnp.pad(packed, ((0, 0), (0, -size % 1024))).reshape(n, -1, 128)
-    if n < 8 or n & (n - 1):
-        mine = lax.psum_scatter(padded, "dp", scatter_dimension=0, tiled=False)
-    else:
-        mine = scatter_sum(padded, me, list(range(n.bit_length() - 3)), f32)
-    flat = mine.reshape(-1)
+def total(values):
+    out = values[0].astype(f32)
+    for value in values[1:]:
+        out = out + value.astype(f32)
+    return out
+
+
+def pick(values, axis, index):
+    return lax.dynamic_index_in_dim(values, index, axis, keepdims=False)
+
+
+def pack(grads, n, width):
+    pieces = []
+    for grad in grads:
+        rows, columns = grad.shape
+        blocks = grad.reshape(n, rows // n, columns)
+        pieces += [blocks[:, :, at : at + width] for at in range(0, columns, width)]
+    return jnp.concatenate(pieces, axis=1)
+
+
+def unpack(packed, shapes, n):
+    width = packed.shape[1]
     outs = []
     start = 0
-    for piece in pieces:
-        outs.append(flat[start : start + piece.shape[1]].reshape(LAYERS, -1))
-        start += piece.shape[1]
+    for rows, columns in shapes:
+        count = rows // n
+        pieces = []
+        for unused in range(0, columns, width):
+            pieces.append(packed[start : start + count])
+            start += count
+        outs.append(jnp.concatenate(pieces, axis=1))
+    return outs
+
+
+class PairSum:
+    def __init__(self, a, b, me):
+        self.me = me
+        self.n = a.shape[0]
+        self.rows = a.shape[1]
+        dims = (4, 2, 2, 2)
+        self.terms = [[a.reshape(dims + a.shape[1:])], [b.reshape(dims + b.shape[1:])]]
+        self.round = 0
+        self.result = None
+        self.pending = None
+
+    def bit(self, at):
+        return (self.me >> at) & 1
+
+    def steps(self):
+        x, y = self.bit(1), self.bit(2)
+        core = self.bit(0)
+        top = self.me >> 3
+        return [((3, core), (3, core)), ((2, x), (1, y)), ((1, y), (1, x)), ((0, top), (0, top))][self.round]
+
+    def part(self, which, other):
+        axis, mine = self.steps()[which]
+        return total([pick(t, axis, mine ^ other) for t in self.terms[which]]).astype(bf16)
+
+    def sends(self):
+        if self.round == 0:
+            return [jnp.concatenate([self.part(0, 1), self.part(1, 1)], axis=-2)]
+        if self.round < 3:
+            return [self.part(0, 1), self.part(1, 1)]
+        return [jnp.concatenate([self.part(0, k), self.part(1, k)], axis=-2) for k in (1, 2, 3)]
+
+    def launch(self, sends):
+        partners = [[1], [2, 4], [4, 2], [8, 16, 24]][self.round]
+        self.pending = [
+            lax.ppermute(sent, "dp", [(i, i ^ p) for i in range(self.n)])
+            for sent, p in zip(sends, partners)
+        ]
+
+    def land(self, came):
+        self.pending = None
+        steps = self.steps()
+        if self.round in (0, 3):
+            came = [
+                [value[..., : self.rows, :] for value in came],
+                [value[..., self.rows :, :] for value in came],
+            ]
+        else:
+            came = [[came[0]], [came[1]]]
+        for which in (0, 1):
+            axis, mine = steps[which]
+            self.terms[which] = [pick(t, axis, mine) for t in self.terms[which]] + came[which]
+        self.round += 1
+        if self.round == 4:
+            self.result = [total(self.terms[0]), total(self.terms[1])]
+
+
+class Scattered:
+    def __init__(self, a, b):
+        both = jnp.concatenate([a, b], axis=1)
+        out = lax.psum_scatter(both, "dp", scatter_dimension=0, tiled=False).astype(f32)
+        self.result = [out[: a.shape[1]], out[a.shape[1] :]]
+        self.pending = None
+
+
+def pair_sum(a, b, me, n):
+    if n == 32 and a.shape[1] % 8 == 0 and b.shape[1] % 8 == 0:
+        return PairSum(a, b, me)
+    return Scattered(a, b)
+
+
+def fence(main, exchanges):
+    flying = [e for e in exchanges if e.pending is not None]
+    main, came = lax.optimization_barrier((main, [e.pending for e in flying]))
+    for e, values in zip(flying, came):
+        e.land(values)
+    ready = [e for e in exchanges if e.result is None]
+    main, sends = lax.optimization_barrier((main, [e.sends() for e in ready]))
+    for e, values in zip(ready, sends):
+        e.launch(values)
+    return main
+
+
+def pack_small(vectors, n, width):
+    pieces = [vector.reshape(LAYERS, n, -1).transpose(1, 0, 2).reshape(n, -1) for vector in vectors]
+    packed = jnp.concatenate(pieces, axis=1).astype(bf16)
+    padded = jnp.pad(packed, ((0, 0), (0, -packed.shape[1] % (8 * width))))
+    return padded.reshape(n, -1, width), [piece.shape[1] for piece in pieces]
+
+
+def unpack_small(block, sizes):
+    flat = block.reshape(-1)
+    outs = []
+    start = 0
+    for size in sizes:
+        outs.append(flat[start : start + size].reshape(LAYERS, -1))
+        start += size
     return outs
 
 
@@ -255,30 +328,30 @@
     return back(grad_normed)
 
 
-def layer_backward(grad_stream, cache, weights, fq, fk, me, n):
+def layer_backward(grad_stream, cache, weights, fq, fk, tie):
     stream, normed, joined, attended, lse, middle, normed_two, hidden, activated = cache
     gain_one, shift_one, qkv_w, qv_b, out_w, out_b, gain_two, shift_two, up_w, up_b, down_w, down_b = weights
     grad_low = grad_stream.astype(bf16)
     grad_down_w = jnp.einsum("tf,td->fd", activated, grad_low, preferred_element_type=f32).astype(bf16)
-    down_sum = reduce_rows(grad_down_w, me, n, False)
     grad_down_b = jnp.sum(grad_low.astype(f32), axis=0)
     grad_activated = dot_nt(grad_low, down_w)
     unused, gelu_back = jax.vjp(partial(jax.nn.gelu, approximate=False), hidden)
     grad_hidden = gelu_back(grad_activated)[0].astype(bf16)
     grad_up_w = jnp.einsum("td,tf->df", normed_two, grad_hidden, preferred_element_type=f32).astype(bf16)
-    up_sum = reduce_rows(grad_up_w, me, n, True)
     grad_up_b = jnp.sum(grad_hidden.astype(f32), axis=0)
+    grad_hidden = tie("hidden", grad_hidden, (grad_down_w, grad_up_w))
     grad_normed = dot_nt(grad_hidden, up_w)
     grad_input, grad_gain_two, grad_shift_two = norm_backward(grad_normed, middle, gain_two, shift_two)
     grad_middle = grad_stream + grad_input
     branch = grad_middle.astype(bf16)
     grad_out_w = jnp.einsum("tc,td->cd", attended, branch, preferred_element_type=f32).astype(bf16)
-    out_sum = reduce_rows(grad_out_w, me, n, True)
     grad_out_b = jnp.sum(branch.astype(f32), axis=0)
     grad_attended = dot_nt(branch, out_w).astype(bf16)
+    grad_attended = tie("attended", grad_attended, (grad_out_w,))
     grad_joined, column_sums = attend_backward(joined, grad_attended, attended, lse, fq, fk)
+    grad_joined = tie("joined", grad_joined, ())
     grad_qkv_w = jnp.einsum("td,te->de", normed, grad_joined, preferred_element_type=f32).astype(bf16)
-    qkv_sum = reduce_rows(grad_qkv_w, me, n, False)
+    grad_joined = tie("qkv", grad_joined, (grad_qkv_w,))
     grad_qv_b = column_sums.reshape(-1)
     grad_normed = dot_nt(grad_joined, qkv_w)
     grad_input, grad_gain_one, grad_shift_one = norm_backward(grad_normed, stream, gain_one, shift_one)
@@ -292,7 +365,7 @@
         grad_up_b,
         grad_down_b,
     )
-    return grad_middle + grad_input, (qkv_sum, out_sum, up_sum, down_sum), small
+    return grad_middle + grad_input, (grad_qkv_w, grad_out_w, grad_up_w, grad_down_w), small
 
 
 def local(n, *arguments):
@@ -307,7 +380,8 @@
         logit_grad,
     ) = arguments
     me = lax.axis_index("dp")
-    row_count = patches.shape[0]
+    row_count, width = patches.shape
+    up_width = stacked[8].shape[2]
     slot_count = img_length.shape[0]
     positions = jnp.arange(row_count, dtype=jnp.int32)
     inside = (positions[None, :] >= img_start[:, None]) & (
@@ -332,14 +406,9 @@
     for weights in layers:
         stream, cache = layer_forward(stream, weights, fq, fk)
         caches.append(cache)
-    pooled = (
-        jnp.dot(member, stream, precision=HIGHEST, preferred_element_type=f32) / counts[:, None]
-    )
-    gathered = lax.all_gather(pooled.astype(bf16), "dp", axis=0, tiled=True)
-    scores = dot32(gathered, cls_weight) + cls_bias.astype(f32)
-    logits = jnp.where(live_columns[None, :], scores, 0.0)
-    grad_cls_weight = jnp.einsum("id,ic->dc", gathered, masked_grad, preferred_element_type=f32)
-    grad_cls_bias = jnp.sum(masked_grad.astype(f32), axis=0)
+    sums = jnp.dot(member, stream, precision=HIGHEST, preferred_element_type=f32)
+    side = jnp.broadcast_to(counts[:, None], (slot_count, 128))
+    gathered = lax.all_gather(jnp.concatenate([sums, side], axis=1), "dp", axis=0, tiled=True)
     grad_stream = jnp.einsum(
         "it,id->td",
         member,
@@ -347,15 +416,59 @@
         precision=HIGHEST,
         preferred_element_type=f32,
     )
-    large = [None] * LAYERS
-    small = [None] * LAYERS
-    for layer in reversed(range(LAYERS)):
-        grad_stream, large[layer], small[layer] = layer_backward(
-            grad_stream, caches[layer], layers[layer], fq, fk, me, n
-        )
-    qkv_sum, out_sum, up_sum, down_sum = (jnp.stack(pair) for pair in zip(*large))
-    gain_one, shift_one, qv_b, out_b, gain_two, shift_two, up_b, down_b = reduce_small(
-        [jnp.stack(pair) for pair in zip(*small)], me, n
+    last = {}
+
+    def tie_last(name, value, grads):
+        last[name] = grads
+        if name != "qkv":
+            return value
+        both = pack(last["hidden"] + last["attended"] + grads, n, width)
+        value, both = lax.optimization_barrier((value, both))
+        last["sum"] = lax.psum_scatter(both, "dp", scatter_dimension=0, tiled=False)
+        return value
+
+    def tie_first(name, value, grads):
+        if name == "hidden":
+            first.append(pair_sum(pack(grads[:1], n, width), pack(grads[1:], n, width), me, n))
+        if name == "qkv":
+            return value
+        return fence(value, first)
+
+    first = []
+    grad_stream, unused, small_last = layer_backward(grad_stream, caches[1], layers[1], fq, fk, tie_last)
+    grad_stream, gathered = lax.optimization_barrier((grad_stream, gathered))
+    grad_stream, grads, small_first = layer_backward(grad_stream, caches[0], layers[0], fq, fk, tie_first)
+    grad_stream, last["sum"] = lax.optimization_barrier((grad_stream, last["sum"]))
+    grad_qkv_w, grad_out_w = grads[:2]
+    small, sizes = pack_small([jnp.stack(pair) for pair in zip(small_first, small_last)], n, width)
+    qk = 2 * width
+    side_a = jnp.concatenate([pack([grad_qkv_w[:, :qk]], n, width), small], axis=1)
+    side_b = pack([grad_qkv_w[:, qk:], grad_out_w], n, width)
+    first.append(pair_sum(side_a, side_b, me, n))
+    while any(e.result is None for e in first):
+        grad_stream = fence(grad_stream, first)
+    gathered = (gathered[:, :width] / gathered[:, width : width + 1]).astype(bf16)
+    scores = dot32(gathered, cls_weight) + cls_bias.astype(f32)
+    logits = jnp.where(live_columns[None, :], scores, 0.0)
+    grad_cls_weight = jnp.einsum("id,ic->dc", gathered, masked_grad, preferred_element_type=f32)
+    grad_cls_bias = jnp.sum(masked_grad.astype(f32), axis=0)
+    square = (width, width)
+    wide = (width, up_width)
+    tall = (up_width, width)
+    down_last, up_last, out_last, qkv_last = unpack(
+        last["sum"].astype(f32), [tall, wide, square, (width, 3 * width)], n
+    )
+    (down_first,) = unpack(first[0].result[0], [tall], n)
+    (up_first,) = unpack(first[0].result[1], [wide], n)
+    (qk_first,) = unpack(first[1].result[0][: 2 * (width // n)], [(width, qk)], n)
+    v_first, out_first = unpack(first[1].result[1], [square, square], n)
+    qkv_first = jnp.concatenate([qk_first, v_first], axis=1)
+    qkv_sum = jnp.stack([qkv_first, qkv_last])
+    out_sum = jnp.stack([out_first, out_last])
+    up_sum = jnp.stack([up_first, up_last])
+    down_sum = jnp.stack([down_first, down_last])
+    gain_one, shift_one, qv_b, out_b, gain_two, shift_two, up_b, down_b = unpack_small(
+        first[1].result[0][2 * (width // n) :], sizes
     )
     return (
         logits,

time: 744 us -> 594 us (0.80)
  blocking collectives: 45.4 us -> 0 us
  waiting for transfers between devices: 107 us -> 72.2 us
  starting transfers between devices: 59 us -> 26.6 us
  other arithmetic: 77.1 us -> 58.5 us
  matrix products: 257 us -> 244 us
    ppermute x54 -> x16, waiting for transfers between devices: 107 us -> 46.3 us  [launch(): lax.ppermute(sent, 'dp', [(i, i ^ p) for i in range(self.n)])]
    all_gather x1 -> x0, blocking collectives: 45.4 us -> none  [local(): gathered = lax.all_gather(pooled.astype(bf16), 'dp', axis=0, tiled=True)]
    ppermute x54 -> x16, starting transfers between devices: 59 us -> 26.5 us  [launch(): lax.ppermute(sent, 'dp', [(i, i ^ p) for i in range(self.n)])]
    reduce_scatter x0 -> x1, waiting for transfers between devices: none -> 25.9 us  [tie_last(): last['sum'] = lax.psum_scatter(both, 'dp', scatter_dimension=0, tiled=False)]
    unnamed x274 -> x223, local copies, waits for them, and re-layouts: 14.6 us -> 38.1 us
    dot_general x5 -> x0, local copies, waits for them, and re-layouts: 18.8 us -> none  [the longest x4 14.8 us: dot_nt(): return lax.dot_general(left, right, NT, preferred_element_type=f32)]
    convert_element_type x24 -> x14, other arithmetic: 30.4 us -> 17.2 us  [the longest x12 15.6 us: part(): total([pick(t, axis, mine ^ other) for t in self.terms[which]]).astype(bf16)]
    reduce_sum x6 -> x1, other arithmetic: 15.7 us -> 3.36 us  [layer_norm(): return center * lax.rsqrt(spread + EPSILON) * gain_vector + shift_vector]
  transfers between devices with their start and end apart: 55 -> 19, of which waited for: 20 -> 9; matrix products, arithmetic and copies ran while one was open for 28% -> 54% of each run, Pallas kernels for 6% -> 20%
where the time goes in v3:
time: 594 us; the launch traced here: 587 us
  matrix products  244 us (41%)
  Pallas kernels  116 us (20%)
  waiting for transfers between devices  72.2 us (12%)
  other arithmetic  58.5 us (10%)
  local copies, waits for them, and re-layouts  53.4 us (9%)
  starting transfers between devices  26.6 us (4%)
  between operations  16.5 us (3%)
    dot_general x9, matrix products, dot32(): return jnp.dot(left, right, preferred_element_type=f32)  107 us
    dot_general x9, matrix products, dot_nt(): return lax.dot_general(left, right, NT, preferred_element_type=f32)  81.3 us
    pallas_call x2, Pallas kernels, attend_backward(): pl.pallas_call(partial(attend_backward_kernel, chunk=rows // 2), grid=(n,...  74.4 us
    ppermute x16, waiting for transfers between devices, launch(): lax.ppermute(sent, 'dp', [(i, i ^ p) for i in range(self.n)])  46.3 us
    pallas_call x2, Pallas kernels, attend_forward(): pl.pallas_call(partial(attend_forward_kernel, chunk=rows), grid=(n,), in_...  41.5 us
    unnamed x223, local copies, waits for them, and re-layouts  38.1 us
    ppermute x16, starting transfers between devices, launch(): lax.ppermute(sent, 'dp', [(i, i ^ p) for i in range(self.n)])  26.5 us
    reduce_scatter x1, waiting for transfers between devices, tie_last(): last['sum'] = lax.psum_scatter(both, 'dp', scatter_dimension=0, tiled=False)  25.9 us
  transfers between devices with their start and end apart: 19, of which 9 were waited for; matrix products, arithmetic and copies ran while one was open for 54% of the time, Pallas kernels for 20%

profile of v3, /device:TPU:0, one launch (start us, length us, event | category | flops | bytes accessed | tf_op | source)
XLA Modules:
  0.0 587.2 jit_solution(17466793605964885867)
XLA Ops:
  17.0 7.9 %add_convert_fusion.3.q_ref.k_ref.v_ref = bf16[1024,2304]{1,0:T(8,128)(2,1)} fusion(f32[2304]{0:T(1024)S(1)} %get-tuple-element.228, bf16[2,768,2304]{2,1,0:T(8,128)(2,1)} %param.25, bf16[1024,768]{1,0:T(8,128)(2,1)S(1)} %copy-done.9, f32[768]{0:T(1024)S(1)} %get-tuple-element.164, f32[768]{0:T(1024)S(1)} %get-tuple-element.248, f32[1024]{0:T(1024)S(1)} %fusion.127, ...), kind=kOutput, calls=%fused_computation.35 | convolution fusion | flops 3633315840 | bytes 9853952 | tf_op jit(solution)/shard_map/dot_general | solution.py:28
  24.9 20.7 %attend_forward.2 = (bf16[1024,768]{1,0:T(8,128)(2,1)}, f32[6,2,1024]{2,1,0:T(2,128)}) custom-call(bf16[1024,2304]{1,0:T(8,128)(2,1)} %add_convert_fusion.3.q_ref.k_ref.v_ref, bf16[1024,2304]{1,0:T(8,128)(2,1)} %add_convert_fusion.3.q_ref.k_ref.v_ref, bf16[1024,2304]{1,0:T(8,128)(2,1)} %add_convert_fusion.3.q_ref.k_ref.v_ref, ...), custom_call_target="tpu_custom_call" | custom-call | flops 12884901888 | bytes 7864320 | tf_op jit(solution)/shard_map/attend_forward/pallas_call | solution.py:74
  51.9 35.8 %multiply_convert_fusion.1 = (bf16[1024,3072]{1,0:T(8,128)(2,1)}, f32[1024,3072]{1,0:T(8,128)}, f32[1024,3072]{1,0:T(8,128)}) fusion(f32[3072]{0:T(1024)S(1)} %bitcast.469, bf16[2,768,3072]{2,1,0:T(8,128)(2,1)S(1)} %bitcast.478, f32[1024,768]{1,0:T(8,128)S(1)} %get-tuple-element.233, f32[768]{0:T(1024)S(1)} %get-tuple-element.158, ...), kind=kOutput, calls=%fused_computation.19 | convolution fusion | flops 5043388416 | bytes 39350272 | tf_op jit(solution)/shard_map/dot_general | solution.py:28
  87.8 7.5 %fusion.158 = (f32[1024]{0:T(1024)S(1)}, f32[1024,768]{1,0:T(8,128)S(1)}) fusion(f32[768]{0:T(1024)S(1)} %get-tuple-element.154, f32[1024,768]{1,0:T(8,128)S(1)} %get-tuple-element.233, bf16[1024,3072]{1,0:T(8,128)(2,1)} %get-tuple-element.179, bf16[2,3072,768]{2,1,0:T(8,128)(2,1)S(1)} %bitcast.474), kind=kOutput, calls=%fused_computation.378 | convolution fusion | flops 4834196480 | bytes 17309696 | tf_op jit(solution)/shard_map/dot_general | solution.py:28
  103.3 20.8 %attend_forward.3 = (bf16[1024,768]{1,0:T(8,128)(2,1)}, f32[6,2,1024]{2,1,0:T(2,128)}) custom-call(bf16[1024,2304]{1,0:T(8,128)(2,1)} %add_convert_fusion.2.q_ref.k_ref.v_ref, bf16[1024,2304]{1,0:T(8,128)(2,1)} %add_convert_fusion.2.q_ref.k_ref.v_ref, bf16[1024,2304]{1,0:T(8,128)(2,1)} %add_convert_fusion.2.q_ref.k_ref.v_ref, ...), custom_call_target="tpu_custom_call" | custom-call | flops 12884901888 | bytes 7864320 | tf_op jit(solution)/shard_map/attend_forward/pallas_call | solution.py:74
  128.8 36.6 %multiply_convert_fusion = (bf16[1024,3072]{1,0:T(8,128)(2,1)S(1)}, f32[1024,3072]{1,0:T(8,128)}, f32[1024,3072]{1,0:T(8,128)}) fusion(f32[3072]{0:T(1024)S(1)} %bitcast.471, bf16[2,768,3072]{2,1,0:T(8,128)(2,1)} %param.31, f32[1024,768]{1,0:T(8,128)S(1)} %get-tuple-element.238, f32[768]{0:T(1024)S(1)} %get-tuple-element.157, ...), kind=kOutput, calls=%fused_computation.5 | convolution fusion | flops 5043388416 | bytes 39348224 | tf_op jit(solution)/shard_map/dot_general | solution.py:28
  175.0 10.1 %convolution_convert_fusion.3 = bf16[3072,768]{1,0:T(8,128)(2,1)} fusion(bf16[1024,3072]{1,0:T(8,128)(2,1)} %copy-done.91, f32[1024,768]{1,0:T(8,128)S(1)} %fusion.118), kind=kOutput, calls=%fused_computation.39 | convolution fusion | flops 4834983936 | bytes 14155776 | tf_op jit(solution)/shard_map/tf,td->fd/dot_general | solution.py:335
  185.1 16.7 %fusion.160 = (bf16[3072]{0:T(1024)(128)(2,1)S(1)}, bf16[1024,3072]{1,0:T(8,128)(2,1)}) fusion(f32[1024,3072]{1,0:T(8,128)} %get-tuple-element.176, bf16[2,3072,768]{2,1,0:T(8,128)(2,1)} %param.33, f32[1024,768]{1,0:T(8,128)S(1)} %fusion.118, f32[1024,3072]{1,0:T(8,128)} %get-tuple-element.239, f32[3072]{0:T(1024)S(1)} %bitcast.472), kind=kOutput, calls=%fused_computation.380 | convolution fusion | flops 4882953216 | bytes 39340032 | tf_op jit(solution)/shard_map/dot_general | solution.py:32
  201.9 9.8 %multiply_reduce_fusion = (bf16[768]{0:T(1024)(128)(2,1)S(1)}, f32[1024]{0:T(1024)S(1)}, bf16[768]{0:T(1024)(128)(2,1)S(1)}, f32[1024,768]{1,0:T(8,128)S(1)}) fusion(f32[1024,768]{1,0:T(8,128)} %copy-done.1, f32[1024]{0:T(1024)S(1)} %fusion.130, f32[1024]{0:T(1024)S(1)} %broadcast_multiply_fusion, f32[768]{0:T(1024)S(1)} %get-tuple-element.251, ...), kind=kOutput, calls=%fused_computation.105 | convolution fusion | flops 4838126592 | bytes 17319936 | tf_op jit(solution)/shard_map/dot_general | solution.py:32
  211.7 8.0 %convolution_convert_fusion.2 = bf16[768,3072]{1,0:T(8,128)(2,1)} fusion(bf16[1024,3072]{1,0:T(8,128)(2,1)S(1)} %copy-done.89, f32[1024,768]{1,0:T(8,128)S(1)} %copy-done.2, f32[768]{0:T(1024)S(1)} %get-tuple-element.157, f32[768]{0:T(1024)S(1)} %get-tuple-element.251, f32[1024]{0:T(1024)S(1)} %fusion.130, f32[1024]{0:T(1024)S(1)} %broadcast_multiply_fusion), kind=kOutput, calls=%fused_computation.38 | convolution fusion | flops 4838129664 | bytes 14170112 | tf_op jit(solution)/shard_map/td,tf->df/dot_general | solution.py:340
  228.6 37.0 %attend_backward.2 = (bf16[1024,2304]{1,0:T(8,128)(2,1)}, f32[2,768]{1,0:T(2,128)}) custom-call(bf16[1024,2304]{1,0:T(8,128)(2,1)} %add_convert_fusion.2.q_ref.k_ref.v_ref, bf16[1024,2304]{1,0:T(8,128)(2,1)} %add_convert_fusion.2.q_ref.k_ref.v_ref, bf16[1024,2304]{1,0:T(8,128)(2,1)} %add_convert_fusion.2.q_ref.k_ref.v_ref, ...), custom_call_target="tpu_custom_call" | custom-call | flops 32212254720 | bytes 12582912 | tf_op jit(solution)/shard_map/attend_backward/pallas_call | solution.py:149
  265.7 6.9 %convolution_convert_fusion.5 = bf16[768,2304]{1,0:T(8,128)(2,1)S(1)} fusion(bf16[1024,2304]{1,0:T(8,128)(2,1)} %get-tuple-element.80, f32[1024,768]{1,0:T(8,128)S(1)} %copy-done.17, f32[768]{0:T(1024)S(1)} %copy-done.83, f32[768]{0:T(1024)S(1)} %copy-done.55, f32[1024]{0:T(1024)S(1)} %copy-done.60, f32[1024]{0:T(1024)S(1)} %copy-done.38), kind=kOutput, calls=%fused_computation.41 | convolution fusion | flops 3629580288 | bytes 11417600 | tf_op jit(solution)/shard_map/td,te->de/dot_general | solution.py:353
  289.2 8.8 %multiply_reduce_fusion.2 = (bf16[768]{0:T(1024)(128)(2,1)S(1)}, f32[1024]{0:T(1024)S(1)}, bf16[768]{0:T(1024)(128)(2,1)S(1)}, f32[1024,768]{1,0:T(8,128)S(1)}) fusion(f32[1024,768]{1,0:T(8,128)} %copy-done.16, f32[1024]{0:T(1024)S(1)} %copy-done.60, f32[1024]{0:T(1024)S(1)} %copy-done.38, f32[768]{0:T(1024)S(1)} %copy-done.55, ...), kind=kOutput, calls=%fused_computation.107 | convolution fusion | flops 3630167552 | bytes 14567424 | tf_op jit(solution)/shard_map/dot_general | solution.py:32
  304.1 17.6 %fusion.161 = (bf16[3072]{0:T(1024)(128)(2,1)S(1)}, bf16[1024,3072]{1,0:T(8,128)(2,1)}) fusion(f32[1024,3072]{1,0:T(8,128)} %get-tuple-element.180, bf16[2,3072,768]{2,1,0:T(8,128)(2,1)} %param.33, f32[1024,768]{1,0:T(8,128)S(1)} %copy-done.5, f32[1024,3072]{1,0:T(8,128)} %get-tuple-element.234, f32[3072]{0:T(1024)S(1)} %bitcast.470), kind=kOutput, calls=%fused_computation.381 | convolution fusion | flops 4882953216 | bytes 39340032 | tf_op jit(solution)/shard_map/dot_general | solution.py:32
  321.7 9.1 %convolution_convert_fusion.1 = bf16[3072,768]{1,0:T(8,128)(2,1)S(1)} fusion(bf16[1024,3072]{1,0:T(8,128)(2,1)} %get-tuple-element.179, f32[1024,768]{1,0:T(8,128)S(1)} %copy-done.5), kind=kOutput, calls=%fused_computation.37 | convolution fusion | flops 4834983936 | bytes 14155776 | tf_op jit(solution)/shard_map/tf,td->fd/dot_general | solution.py:335
  348.6 11.0 %multiply_reduce_fusion.1 = (bf16[768]{0:T(1024)(128)(2,1)S(1)}, f32[1024]{0:T(1024)S(1)}, bf16[768]{0:T(1024)(128)(2,1)S(1)}, f32[1024,768]{1,0:T(8,128)}) fusion(f32[1024,768]{1,0:T(8,128)} %copy-done.14, f32[1024]{0:T(1024)S(1)} %copy-done.58, f32[1024]{0:T(1024)S(1)} %copy-done.36, f32[768]{0:T(1024)S(1)} %copy-done.53, ...), kind=kOutput, calls=%fused_computation.106 | convolution fusion | flops 4838126592 | bytes 17319936 | tf_op jit(solution)/shard_map/dot_general | solution.py:32
  386.1 37.3 %attend_backward.3 = (bf16[1024,2304]{1,0:T(8,128)(2,1)}, f32[2,768]{1,0:T(2,128)}) custom-call(bf16[1024,2304]{1,0:T(8,128)(2,1)} %add_convert_fusion.3.q_ref.k_ref.v_ref, bf16[1024,2304]{1,0:T(8,128)(2,1)} %add_convert_fusion.3.q_ref.k_ref.v_ref, bf16[1024,2304]{1,0:T(8,128)(2,1)} %add_convert_fusion.3.q_ref.k_ref.v_ref, ...), custom_call_target="tpu_custom_call" | custom-call | flops 32212254720 | bytes 12582912 | tf_op jit(solution)/shard_map/attend_backward/pallas_call | solution.py:149
  441.3 7.7 %fusion.140 = (bf16[768]{0:T(1024)(128)(2,1)S(1)}, f32[1024]{0:T(1024)S(1)}, f32[1024,768]{1,0:T(8,128)}) fusion(f32[768]{0:T(1024)S(1)} %copy-done.48, f32[1024]{0:T(1024)S(1)} %copy-done.33, bf16[1024,768]{1,0:T(8,128)(2,1)S(1)} %copy-done.11, bf16[1024,2304]{1,0:T(8,128)(2,1)S(1)} %bitcast.482, bf16[2,768,2304]{2,1,0:T(8,128)(2,1)} %param.25), kind=kOutput, calls=%fused_computation.364 | convolution fusion | flops 3628595456 | bytes 12988928 | tf_op jit(solution)/shard_map/dot_general | solution.py:32
  464.0 25.9 %reduce-scatter.5.cloned.1.call-done = bf16[1,288,768]{2,1,0:T(8,128)(2,1)} async-done(((bf16[32,288,768]{2,1,0:T(8,128)(2,1)}), bf16[1,288,768]{2,1,0:T(8,128)(2,1)}) %reduce-scatter.5.cloned.1.call-update) | async-done | bytes 442384 | tf_op jit(solution)/shard_map/reduce_scatter | solution.py:427
  507.6 10.5 %collective-permute-done.5 = bf16[192,768]{1,0:T(8,128)(2,1)S(1)} collective-permute-done((bf16[192,768]{1,0:T(8,128)(2,1)S(1)}, bf16[192,768]{1,0:T(8,128)(2,1)S(1)}, u32[]{:S(2)}, u32[]{:S(2)}) %collective-permute-start.5) | collective-permute-done | bytes 294944 | tf_op jit(solution)/shard_map/ppermute | solution.py:246
  518.1 9.3 %collective-permute-done.6 = bf16[192,768]{1,0:T(8,128)(2,1)S(1)} collective-permute-done((bf16[192,768]{1,0:T(8,128)(2,1)S(1)}, bf16[192,768]{1,0:T(8,128)(2,1)S(1)}, u32[]{:S(2)}, u32[]{:S(2)}) %collective-permute-start.6) | collective-permute-done | bytes 294944 | tf_op jit(solution)/shard_map/ppermute | solution.py:246
  535.8 8.8 %collective-permute-done.10 = bf16[4,2,48,768]{3,2,1,0:T(8,128)(2,1)S(1)} collective-permute-done((bf16[4,2,48,768]{3,2,1,0:T(8,128)(2,1)S(1)}, bf16[4,2,48,768]{3,2,1,0:T(8,128)(2,1)S(1)}, u32[]{:S(2)}, u32[]{:S(2)}) %collective-permute-start.10) | collective-permute-done | bytes 589856 | tf_op jit(solution)/shard_map/ppermute | solution.py:246
  556.0 8.3 %collective-permute-start.13 = (bf16[104,768]{1,0:T(8,128)(2,1)S(1)}, bf16[104,768]{1,0:T(8,128)(2,1)S(1)}, u32[]{:S(2)}, u32[]{:S(2)}) collective-permute-start(bf16[104,768]{1,0:T(8,128)(2,1)S(1)} %pad_maximum_fusion.10), channel_id=1, source_target_pairs={{0,8},{1,9},{2,10},{3,11},{4,12},{5,13},{6,14},{7,15},{8,0},{9,1},... | collective-permute-start | bytes 479240 | tf_op jit(solution)/shard_map/ppermute | solution.py:246
  568.6 8.0 %collective-permute-done.14 = bf16[104,768]{1,0:T(8,128)(2,1)S(1)} collective-permute-done((bf16[104,768]{1,0:T(8,128)(2,1)S(1)}, bf16[104,768]{1,0:T(8,128)(2,1)S(1)}, u32[]{:S(2)}, u32[]{:S(2)}) %collective-permute-start.14) | collective-permute-done | bytes 159776 | tf_op jit(solution)/shard_map/ppermute | solution.py:246
  (434 shorter events, 190.4 us)
Async XLA Ops:
  7.2 165.5 %reduce-scatter.3.cloned.1.call-start = ((), (), s32[]{:S(2)}) async-start(), calls=%async_computation.2 | async-start | bytes 1622016 | tf_op jit(solution)/shard_map/reduce_scatter | solution.py:400
  11.1 291.1 %all-gather.2.cloned.1.call-start = ((), (), s32[]{:S(2)}) async-start(), calls=%async_computation.3 | async-start | bytes 1892352 | tf_op jit(solution)/shard_map/all_gather | solution.py:411
  16.4 80.4 %copy-start.54 = (f32[768]{0:T(1024)}, f32[768]{0:T(1024)S(1)}, u32[]{:S(2)}) copy-start(f32[768]{0:T(1024)S(1)} %get-tuple-element.249) | copy-start | bytes 9220
  16.4 80.4 %copy-start.82 = (f32[768]{0:T(1024)}, f32[768]{0:T(1024)S(1)}, u32[]{:S(2)}) copy-start(f32[768]{0:T(1024)S(1)} %get-tuple-element.163) | copy-start | bytes 9220
  45.7 42.1 %slice-start.3 = ((s8[9437184]{0:T(1024)(128)(4,1)}), s8[4194304]{0:T(1024)(128)(4,1)S(1)}, s32[]{:S(2)}) async-start(s8[9437184]{0:T(1024)(128)(4,1)} %bitcast.473), calls=%async_computation.8 | async-start | bytes 8388608
  124.1 41.3 %slice-start.6 = ((s8[9437184]{0:T(1024)(128)(4,1)}), s8[4194304]{0:T(1024)(128)(4,1)S(1)}, s32[]{:S(2)}) async-start(s8[9437184]{0:T(1024)(128)(4,1)} %bitcast.475), calls=%async_computation.11 | async-start | bytes 8388608
  127.2 43.3 %copy-start.1 = (f32[1024,768]{1,0:T(8,128)}, f32[1024,768]{1,0:T(8,128)S(1)}, u32[]{:S(2)}) copy-start(f32[1024,768]{1,0:T(8,128)S(1)} %get-tuple-element.238) | copy-start | bytes 9437188
  172.6 317.3 %reduce-scatter.5.cloned.1.call-start = ((), (), s32[]{:S(2)}) async-start(), calls=%async_computation.4 | async-start | bytes 14598144 | tf_op jit(solution)/shard_map/reduce_scatter | solution.py:427
  347.1 26.6 %collective-permute-start = (bf16[4,2,2,192,768]{4,3,2,1,0:T(8,128)(2,1)}, bf16[4,2,2,192,768]{4,3,2,1,0:T(8,128)(2,1)}, u32[]{:S(2)}, u32[]{:S(2)}) collective-permute-start(bf16[4,2,2,192,768]{4,3,2,1,0:T(8,128)(2,1)} %pad_maximum_fusion.1), channel_id=1, source_target_pairs={{0,1},{1,0},{2,3},{3,2},{4,5},{5,4},{6,7},{7,6},{8,9},{9,8},{10,11... | collective-permute-start | bytes 14155784 | tf_op jit(solution)/shard_map/ppermute | solution.py:246
  382.6 42.0 %collective-permute-start.1 = (bf16[4,2,96,768]{3,2,1,0:T(8,128)(2,1)}, bf16[4,2,96,768]{3,2,1,0:T(8,128)(2,1)}, u32[]{:S(2)}, u32[]{:S(2)}) collective-permute-start(bf16[4,2,96,768]{3,2,1,0:T(8,128)(2,1)} %fusion.60), channel_id=1, source_target_pairs={{0,2},{1,3},{2,0},{3,1},{4,6},{5,7},{6,4},{7,5},{8,10},{9,11},{10,... | collective-permute-start | bytes 3538952 | tf_op jit(solution)/shard_map/ppermute | solution.py:246
  384.6 40.8 %collective-permute-start.2 = (bf16[4,2,96,768]{3,2,1,0:T(8,128)(2,1)}, bf16[4,2,96,768]{3,2,1,0:T(8,128)(2,1)}, u32[]{:S(2)}, u32[]{:S(2)}) collective-permute-start(bf16[4,2,96,768]{3,2,1,0:T(8,128)(2,1)} %fusion.59), channel_id=1, source_target_pairs={{0,4},{1,5},{2,6},{3,7},{4,0},{5,1},{6,2},{7,3},{8,12},{9,13},{10,... | collective-permute-start | bytes 3538952 | tf_op jit(solution)/shard_map/ppermute | solution.py:246
  439.2 50.7 %collective-permute-start.3 = (bf16[4,96,768]{2,1,0:T(8,128)(2,1)}, bf16[4,96,768]{2,1,0:T(8,128)(2,1)S(1)}, u32[]{:S(2)}, u32[]{:S(2)}) collective-permute-start(bf16[4,96,768]{2,1,0:T(8,128)(2,1)} %fusion.69), channel_id=1, source_target_pairs={{0,4},{1,5},{2,6},{3,7},{4,0},{5,1},{6,2},{7,3},{8,12},{9,13},{10,... | collective-permute-start | bytes 1769480 | tf_op jit(solution)/shard_map/ppermute | solution.py:246
  440.7 49.2 %collective-permute-start.4 = (bf16[4,96,768]{2,1,0:T(8,128)(2,1)}, bf16[4,96,768]{2,1,0:T(8,128)(2,1)}, u32[]{:S(2)}, u32[]{:S(2)}) collective-permute-start(bf16[4,96,768]{2,1,0:T(8,128)(2,1)} %fusion.68), channel_id=1, source_target_pairs={{0,2},{1,3},{2,0},{3,1},{4,6},{5,7},{6,4},{7,5},{8,10},{9,11},{10,... | collective-permute-start | bytes 1769480 | tf_op jit(solution)/shard_map/ppermute | solution.py:246
  495.5 31.9 %collective-permute-start.8 = (bf16[4,2,2,104,768]{4,3,2,1,0:T(8,128)(2,1)}, bf16[4,2,2,104,768]{4,3,2,1,0:T(8,128)(2,1)}, u32[]{:S(2)}, u32[]{:S(2)}) collective-permute-start(bf16[4,2,2,104,768]{4,3,2,1,0:T(8,128)(2,1)} %pad_maximum_fusion.3), channel_id=1, source_target_pairs={{0,1},{1,0},{2,3},{3,2},{4,5},{5,4},{6,7},{7,6},{8,9},{9,8},{10,11... | collective-permute-start | bytes 7667720 | tf_op jit(solution)/shard_map/ppermute | solution.py:246
  503.0 15.1 %collective-permute-start.5 = (bf16[192,768]{1,0:T(8,128)(2,1)S(1)}, bf16[192,768]{1,0:T(8,128)(2,1)S(1)}, u32[]{:S(2)}, u32[]{:S(2)}) collective-permute-start(bf16[192,768]{1,0:T(8,128)(2,1)S(1)} %copy-done.31), channel_id=1, source_target_pairs={{0,8},{1,9},{2,10},{3,11},{4,12},{5,13},{6,14},{7,15},{8,0},{9,1},... | collective-permute-start | bytes 884744 | tf_op jit(solution)/shard_map/ppermute | solution.py:246
  503.9 23.5 %collective-permute-start.6 = (bf16[192,768]{1,0:T(8,128)(2,1)S(1)}, bf16[192,768]{1,0:T(8,128)(2,1)S(1)}, u32[]{:S(2)}, u32[]{:S(2)}) collective-permute-start(bf16[192,768]{1,0:T(8,128)(2,1)S(1)} %copy-done.30), channel_id=1, source_target_pairs={{0,16},{1,17},{2,18},{3,19},{4,20},{5,21},{6,22},{7,23},{8,24},{9,... | collective-permute-start | bytes 884744 | tf_op jit(solution)/shard_map/ppermute | solution.py:246
  505.4 22.0 %collective-permute-start.7 = (bf16[192,768]{1,0:T(8,128)(2,1)S(1)}, bf16[192,768]{1,0:T(8,128)(2,1)S(1)}, u32[]{:S(2)}, u32[]{:S(2)}) collective-permute-start(bf16[192,768]{1,0:T(8,128)(2,1)S(1)} %copy-done.29), channel_id=1, source_target_pairs={{0,24},{1,25},{2,26},{3,27},{4,28},{5,29},{6,30},{7,31},{8,16},{9,... | collective-permute-start | bytes 884744 | tf_op jit(solution)/shard_map/ppermute | solution.py:246
  531.1 13.4 %collective-permute-start.10 = (bf16[4,2,48,768]{3,2,1,0:T(8,128)(2,1)S(1)}, bf16[4,2,48,768]{3,2,1,0:T(8,128)(2,1)S(1)}, u32[]{:S(2)}, u32[]{:S(2)}) collective-permute-start(bf16[4,2,48,768]{3,2,1,0:T(8,128)(2,1)S(1)} %fusion.67), channel_id=1, source_target_pairs={{0,4},{1,5},{2,6},{3,7},{4,0},{5,1},{6,2},{7,3},{8,12},{9,13},{10,... | collective-permute-start | bytes 1769480 | tf_op jit(solution)/shard_map/ppermute | solution.py:246
  532.7 15.2 %collective-permute-start.9 = (bf16[4,2,56,768]{3,2,1,0:T(8,128)(2,1)S(1)}, bf16[4,2,56,768]{3,2,1,0:T(8,128)(2,1)S(1)}, u32[]{:S(2)}, u32[]{:S(2)}) collective-permute-start(bf16[4,2,56,768]{3,2,1,0:T(8,128)(2,1)S(1)} %fusion.64), channel_id=1, source_target_pairs={{0,2},{1,3},{2,0},{3,1},{4,6},{5,7},{6,4},{7,5},{8,10},{9,11},{10,... | collective-permute-start | bytes 2064392 | tf_op jit(solution)/shard_map/ppermute | solution.py:246
  548.1 7.4 %collective-permute-start.11 = (bf16[4,56,768]{2,1,0:T(8,128)(2,1)S(1)}, bf16[4,56,768]{2,1,0:T(8,128)(2,1)S(1)}, u32[]{:S(2)}, u32[]{:S(2)}) collective-permute-start(bf16[4,56,768]{2,1,0:T(8,128)(2,1)S(1)} %fusion.79), channel_id=1, source_target_pairs={{0,4},{1,5},{2,6},{3,7},{4,0},{5,1},{6,2},{7,3},{8,12},{9,13},{10,... | collective-permute-start | bytes 1032200 | tf_op jit(solution)/shard_map/ppermute | solution.py:246
  548.8 6.8 %collective-permute-start.12 = (bf16[4,48,768]{2,1,0:T(8,128)(2,1)S(1)}, bf16[4,48,768]{2,1,0:T(8,128)(2,1)S(1)}, u32[]{:S(2)}, u32[]{:S(2)}) collective-permute-start(bf16[4,48,768]{2,1,0:T(8,128)(2,1)S(1)} %fusion.82), channel_id=1, source_target_pairs={{0,2},{1,3},{2,0},{3,1},{4,6},{5,7},{6,4},{7,5},{8,10},{9,11},{10,... | collective-permute-start | bytes 884744 | tf_op jit(solution)/shard_map/ppermute | solution.py:246
  556.0 12.6 %collective-permute-start.13 = (bf16[104,768]{1,0:T(8,128)(2,1)S(1)}, bf16[104,768]{1,0:T(8,128)(2,1)S(1)}, u32[]{:S(2)}, u32[]{:S(2)}) collective-permute-start(bf16[104,768]{1,0:T(8,128)(2,1)S(1)} %pad_maximum_fusion.10), channel_id=1, source_target_pairs={{0,8},{1,9},{2,10},{3,11},{4,12},{5,13},{6,14},{7,15},{8,0},{9,1},... | collective-permute-start | bytes 479240 | tf_op jit(solution)/shard_map/ppermute | solution.py:246
  564.3 12.3 %collective-permute-start.14 = (bf16[104,768]{1,0:T(8,128)(2,1)S(1)}, bf16[104,768]{1,0:T(8,128)(2,1)S(1)}, u32[]{:S(2)}, u32[]{:S(2)}) collective-permute-start(bf16[104,768]{1,0:T(8,128)(2,1)S(1)} %pad_maximum_fusion.11), channel_id=1, source_target_pairs={{0,16},{1,17},{2,18},{3,19},{4,20},{5,21},{6,22},{7,23},{8,24},{9,... | collective-permute-start | bytes 479240 | tf_op jit(solution)/shard_map/ppermute | solution.py:246
  564.7 11.9 %collective-permute-start.15 = (bf16[104,768]{1,0:T(8,128)(2,1)S(1)}, bf16[104,768]{1,0:T(8,128)(2,1)S(1)}, u32[]{:S(2)}, u32[]{:S(2)}) collective-permute-start(bf16[104,768]{1,0:T(8,128)(2,1)S(1)} %pad_maximum_fusion.12), channel_id=1, source_target_pairs={{0,24},{1,25},{2,26},{3,27},{4,28},{5,29},{6,30},{7,31},{8,16},{9,... | collective-permute-start | bytes 479240 | tf_op jit(solution)/shard_map/ppermute | solution.py:246
  (103 other events, 1071.0 us)
Sparse Core Ops, SparseCore 0:
  13.3 100.6 reduce-scatter.2
  172.8 58.4 all-gather.1
  302.4 187.4 reduce-scatter.4

commit v4 on v3

--- a/solution.py
+++ b/solution.py
@@ -16,12 +16,7 @@
 f32 = jnp.float32
 bf16 = jnp.bfloat16
 VMEM_LIMIT = 56 << 20
-
-
-def layer_norm(stream, gain_vector, shift_vector):
-    center = stream - jnp.mean(stream, axis=-1, keepdims=True)
-    spread = jnp.mean(center * center, axis=-1, keepdims=True)
-    return center * lax.rsqrt(spread + EPSILON) * gain_vector + shift_vector
+ROWS_STEP = 256
 
 
 def dot32(left, right):
@@ -308,64 +303,247 @@
     return outs
 
 
-def layer_forward(stream, weights, fq, fk):
-    gain_one, shift_one, qkv_w, qv_b, out_w, out_b, gain_two, shift_two, up_w, up_b, down_w, down_b = weights
-    width = stream.shape[1]
-    normed = layer_norm(stream, gain_one.astype(f32), shift_one.astype(f32)).astype(bf16)
-    bias_full = jnp.concatenate([qv_b[:width], jnp.zeros((width,), bf16), qv_b[width:]]).astype(f32)
-    joined = (dot32(normed, qkv_w) + bias_full).astype(bf16)
+def row_block(width):
+    return pl.BlockSpec((ROWS_STEP, width), lambda i: (i, 0))
+
+
+def vector(layer, width):
+    return pl.BlockSpec((None, 1, width), lambda i: (layer, 0, 0))
+
+
+def resident(layer, rows, columns):
+    return pl.BlockSpec((None, rows, columns), lambda i: (layer, 0, 0), pipeline_mode=pl.Buffered(1))
+
+
+def kept(rows, columns):
+    return pl.BlockSpec((rows, columns), lambda i: (0, 0))
+
+
+def standardize(values):
+    center = values - jnp.mean(values, axis=-1, keepdims=True)
+    scale = lax.rsqrt(jnp.mean(center * center, axis=-1, keepdims=True) + EPSILON)
+    return center * scale, scale
+
+
+def columns_sum(values):
+    return jnp.sum(values, axis=0, keepdims=True)
+
+
+def dense_call(kernel, name, rows, in_specs, out_specs, out_shape, flops, moved):
+    return pl.pallas_call(
+        kernel,
+        grid=(rows // ROWS_STEP,),
+        in_specs=in_specs,
+        out_specs=out_specs,
+        out_shape=out_shape,
+        compiler_params=pltpu.CompilerParams(vmem_limit_bytes=VMEM_LIMIT),
+        cost_estimate=pl.CostEstimate(flops=flops, bytes_accessed=moved, transcendentals=0),
+        name=name,
+    )
+
+
+def project_kernel(stream_ref, gain_ref, shift_ref, w_ref, b_ref, normed_ref, joined_ref):
+    unit, unused = standardize(stream_ref[...].astype(f32))
+    normed = (unit * gain_ref[...].astype(f32) + shift_ref[...].astype(f32)).astype(bf16)
+    normed_ref[...] = normed
+    joined_ref[...] = (dot32(normed, w_ref[...]) + b_ref[...].astype(f32)).astype(bf16)
+
+
+def project(layer, stream, gain, shift, qkv_w, bias):
+    rows, width = stream.shape
+    out = jax.ShapeDtypeStruct
+    return dense_call(
+        project_kernel,
+        "project",
+        rows,
+        [row_block(width), vector(layer, width), vector(layer, width)]
+        + [resident(layer, width, 3 * width), vector(layer, 3 * width)],
+        [row_block(width), row_block(3 * width)],
+        [out((rows, width), bf16), out((rows, 3 * width), bf16)],
+        6 * rows * width * width,
+        12 * rows * width + 6 * width * width,
+    )(stream, gain, shift, qkv_w, bias)
+
+
+def mlp_forward_kernel(
+    att_ref, stream_ref, out_w_ref, out_b_ref, gain_ref, shift_ref, up_w_ref, up_b_ref,
+    down_w_ref, down_b_ref, middle_ref, normed_ref, act_ref, slope_ref, result_ref,
+):
+    width = att_ref.shape[1]
+    middle = (
+        stream_ref[...].astype(f32) + dot32(att_ref[...], out_w_ref[...]) + out_b_ref[...].astype(f32)
+    )
+    middle_ref[...] = middle
+    unit, unused = standardize(middle)
+    normed = (unit * gain_ref[...].astype(f32) + shift_ref[...].astype(f32)).astype(bf16)
+    normed_ref[...] = normed
+    result = middle + down_b_ref[...].astype(f32)
+    for at in range(0, up_w_ref.shape[1], width):
+        span = slice(at, at + width)
+        hidden = dot32(normed, up_w_ref[:, span]) + up_b_ref[:, span].astype(f32)
+        below = 0.5 + 0.5 * lax.erf(hidden * 0.7071067811865476)
+        act = (hidden * below).astype(bf16)
+        slope = below + hidden * (0.3989422804014327 * jnp.exp(-0.5 * (hidden * hidden)))
+        act_ref[:, span] = act
+        slope_ref[:, span] = slope.astype(bf16)
+        result = result + dot32(act, down_w_ref[span, :])
+    result_ref[...] = result
+
+
+def mlp_forward(layer, attended, stream, out_w, out_b, gain, shift, up_w, up_b, down_w, down_b):
+    rows, width = attended.shape
+    up = up_w.shape[2]
+    out = jax.ShapeDtypeStruct
+    return dense_call(
+        mlp_forward_kernel,
+        "mlp_forward",
+        rows,
+        [row_block(width), row_block(width), resident(layer, width, width)]
+        + [vector(layer, width)] * 3
+        + [resident(layer, width, up), vector(layer, up), resident(layer, up, width), vector(layer, width)],
+        [row_block(width), row_block(width), row_block(up), row_block(up), row_block(width)],
+        [
+            out((rows, width), f32),
+            out((rows, width), bf16),
+            out((rows, up), bf16),
+            out((rows, up), bf16),
+            out((rows, width), f32),
+        ],
+        2 * rows * width * (width + 2 * up),
+        4 * rows * (4 * width + up) + 4 * width * (width + up),
+    )(attended, stream, out_w, out_b, gain, shift, up_w, up_b, down_w, down_b)
+
+
+def mlp_backward_kernel(
+    grad_ref, slope_ref, middle_ref, gain_ref, up_w_ref, down_w_ref, out_w_ref,
+    low_ref, hidden_ref, grad_middle_ref, branch_ref, attended_ref, up_sum_ref, sums_ref,
+):
+    width = grad_ref.shape[1]
+
+    @pl.when(pl.program_id(0) == 0)
+    def _():
+        up_sum_ref[...] = jnp.zeros_like(up_sum_ref)
+        sums_ref[...] = jnp.zeros_like(sums_ref)
+
+    grad = grad_ref[...]
+    low = grad.astype(bf16)
+    low_ref[...] = low
+    normed = jnp.zeros(grad.shape, f32)
+    for at in range(0, up_w_ref.shape[1], width):
+        span = slice(at, at + width)
+        act = dot_nt(low, down_w_ref[span, :])
+        hidden = (slope_ref[:, span].astype(f32) * act).astype(bf16)
+        hidden_ref[:, span] = hidden
+        up_sum_ref[:, span] += columns_sum(hidden.astype(f32))
+        normed = normed + dot_nt(hidden, up_w_ref[:, span])
+    unit, scale = standardize(middle_ref[...])
+    scaled = normed * gain_ref[...].astype(f32)
+    inner = scaled - jnp.mean(scaled, axis=-1, keepdims=True)
+    inner = inner - unit * jnp.mean(scaled * unit, axis=-1, keepdims=True)
+    middle = grad + inner * scale
+    grad_middle_ref[...] = middle
+    branch = middle.astype(bf16)
+    branch_ref[...] = branch
+    attended_ref[...] = dot_nt(branch, out_w_ref[...]).astype(bf16)
+    sums_ref[0:1, :] += columns_sum(low.astype(f32))
+    sums_ref[1:2, :] += columns_sum(normed * unit)
+    sums_ref[2:3, :] += columns_sum(normed)
+    sums_ref[3:4, :] += columns_sum(branch.astype(f32))
+
+
+def mlp_backward(layer, grad, slope, middle, gain, up_w, down_w, out_w):
+    rows, width = grad.shape
+    up = up_w.shape[2]
+    out = jax.ShapeDtypeStruct
+    return dense_call(
+        mlp_backward_kernel,
+        "mlp_backward",
+        rows,
+        [row_block(width), row_block(up), row_block(width), vector(layer, width)]
+        + [resident(layer, width, up), resident(layer, up, width), resident(layer, width, width)],
+        [row_block(width), row_block(up)] + [row_block(width)] * 3 + [kept(1, up), kept(8, width)],
+        [
+            out((rows, width), bf16),
+            out((rows, up), bf16),
+            out((rows, width), f32),
+            out((rows, width), bf16),
+            out((rows, width), bf16),
+            out((1, up), f32),
+            out((8, width), f32),
+        ],
+        2 * rows * width * (width + 2 * up),
+        4 * rows * (5 * width + up) + 4 * width * (width + up),
+    )(grad, slope, middle, gain, up_w, down_w, out_w)
+
+
+def project_backward_kernel(joined_ref, stream_ref, grad_ref, gain_ref, w_ref, result_ref, sums_ref):
+    @pl.when(pl.program_id(0) == 0)
+    def _():
+        sums_ref[...] = jnp.zeros_like(sums_ref)
+
+    normed = dot_nt(joined_ref[...], w_ref[...])
+    unit, scale = standardize(stream_ref[...].astype(f32))
+    scaled = normed * gain_ref[...].astype(f32)
+    inner = scaled - jnp.mean(scaled, axis=-1, keepdims=True)
+    inner = inner - unit * jnp.mean(scaled * unit, axis=-1, keepdims=True)
+    result_ref[...] = grad_ref[...] + inner * scale
+    sums_ref[0:1, :] += columns_sum(normed * unit)
+    sums_ref[1:2, :] += columns_sum(normed)
+
+
+def project_backward(layer, joined, stream, grad, gain, qkv_w):
+    rows, width = grad.shape
+    out = jax.ShapeDtypeStruct
+    return dense_call(
+        project_backward_kernel,
+        "project_backward",
+        rows,
+        [row_block(3 * width), row_block(width), row_block(width), vector(layer, width)]
+        + [resident(layer, width, 3 * width)],
+        [row_block(width), kept(8, width)],
+        [out((rows, width), f32), out((8, width), f32)],
+        6 * rows * width * width,
+        18 * rows * width + 6 * width * width,
+    )(joined, stream, grad, gain, qkv_w)
+
+
+def layer_forward(layer, stream, weights, fq, fk):
+    gain_one, shift_one, qkv_w, bias, out_w, out_b, gain_two, shift_two, up_w, up_b, down_w, down_b = weights
+    normed, joined = project(layer, stream, gain_one, shift_one, qkv_w, bias)
     attended, lse = attend_forward(joined, fq, fk)
-    middle = stream + dot32(attended, out_w) + out_b.astype(f32)
-    normed_two = layer_norm(middle, gain_two.astype(f32), shift_two.astype(f32)).astype(bf16)
-    hidden = dot32(normed_two, up_w) + up_b.astype(f32)
-    activated = jax.nn.gelu(hidden, approximate=False).astype(bf16)
-    output = middle + dot32(activated, down_w) + down_b.astype(f32)
-    return output, (stream, normed, joined, attended, lse, middle, normed_two, hidden, activated)
-
-
-def norm_backward(grad_normed, values, gain, shift):
-    unused, back = jax.vjp(layer_norm, values, gain.astype(f32), shift.astype(f32))
-    return back(grad_normed)
-
-
-def layer_backward(grad_stream, cache, weights, fq, fk, tie):
-    stream, normed, joined, attended, lse, middle, normed_two, hidden, activated = cache
-    gain_one, shift_one, qkv_w, qv_b, out_w, out_b, gain_two, shift_two, up_w, up_b, down_w, down_b = weights
-    grad_low = grad_stream.astype(bf16)
-    grad_down_w = jnp.einsum("tf,td->fd", activated, grad_low, preferred_element_type=f32).astype(bf16)
-    grad_down_b = jnp.sum(grad_low.astype(f32), axis=0)
-    grad_activated = dot_nt(grad_low, down_w)
-    unused, gelu_back = jax.vjp(partial(jax.nn.gelu, approximate=False), hidden)
-    grad_hidden = gelu_back(grad_activated)[0].astype(bf16)
+    middle, normed_two, activated, slope, output = mlp_forward(
+        layer, attended, stream, out_w, out_b, gain_two, shift_two, up_w, up_b, down_w, down_b
+    )
+    return output, (stream, normed, joined, attended, lse, middle, normed_two, slope, activated)
+
+
+def layer_backward(layer, grad_stream, cache, weights, fq, fk, tie):
+    stream, normed, joined, attended, lse, middle, normed_two, slope, activated = cache
+    gain_one, shift_one, qkv_w, bias, out_w, out_b, gain_two, shift_two, up_w, up_b, down_w, down_b = weights
+    low, grad_hidden, grad_middle, branch, grad_attended, grad_up_b, sums = mlp_backward(
+        layer, grad_stream, slope, middle, gain_two, up_w, down_w, out_w
+    )
+    grad_down_w = jnp.einsum("tf,td->fd", activated, low, preferred_element_type=f32).astype(bf16)
     grad_up_w = jnp.einsum("td,tf->df", normed_two, grad_hidden, preferred_element_type=f32).astype(bf16)
-    grad_up_b = jnp.sum(grad_hidden.astype(f32), axis=0)
-    grad_hidden = tie("hidden", grad_hidden, (grad_down_w, grad_up_w))
-    grad_normed = dot_nt(grad_hidden, up_w)
-    grad_input, grad_gain_two, grad_shift_two = norm_backward(grad_normed, middle, gain_two, shift_two)
-    grad_middle = grad_stream + grad_input
-    branch = grad_middle.astype(bf16)
+    branch = tie("hidden", branch, (grad_down_w, grad_up_w))
     grad_out_w = jnp.einsum("tc,td->cd", attended, branch, preferred_element_type=f32).astype(bf16)
-    grad_out_b = jnp.sum(branch.astype(f32), axis=0)
-    grad_attended = dot_nt(branch, out_w).astype(bf16)
     grad_attended = tie("attended", grad_attended, (grad_out_w,))
     grad_joined, column_sums = attend_backward(joined, grad_attended, attended, lse, fq, fk)
     grad_joined = tie("joined", grad_joined, ())
     grad_qkv_w = jnp.einsum("td,te->de", normed, grad_joined, preferred_element_type=f32).astype(bf16)
     grad_joined = tie("qkv", grad_joined, (grad_qkv_w,))
-    grad_qv_b = column_sums.reshape(-1)
-    grad_normed = dot_nt(grad_joined, qkv_w)
-    grad_input, grad_gain_one, grad_shift_one = norm_backward(grad_normed, stream, gain_one, shift_one)
+    grad_input, sums_one = project_backward(layer, grad_joined, stream, grad_middle, gain_one, qkv_w)
     small = (
-        grad_gain_one,
-        grad_shift_one,
-        grad_qv_b,
-        grad_out_b,
-        grad_gain_two,
-        grad_shift_two,
-        grad_up_b,
-        grad_down_b,
-    )
-    return grad_middle + grad_input, (grad_qkv_w, grad_out_w, grad_up_w, grad_down_w), small
+        sums_one[0],
+        sums_one[1],
+        column_sums.reshape(-1),
+        sums[3],
+        sums[1],
+        sums[2],
+        grad_up_b[0],
+        sums[0],
+    )
+    return grad_input, (grad_qkv_w, grad_out_w, grad_up_w, grad_down_w), small
 
 
 def local(n, *arguments):
@@ -400,11 +578,15 @@
     pooled_grad = lax.psum_scatter(
         dot_nt(masked_grad, cls_weight), "dp", scatter_dimension=0, tiled=True
     )
-    stream = patches.astype(f32)
-    layers = [tuple(weight[layer] for weight in stacked) for layer in range(LAYERS)]
+    weights = [value[:, None, :] if value.ndim == 2 else value for value in stacked]
+    qv_bias = weights[3]
+    weights[3] = jnp.concatenate(
+        [qv_bias[..., :width], jnp.zeros((LAYERS, 1, width), bf16), qv_bias[..., width:]], axis=-1
+    )
+    stream = patches
     caches = []
-    for weights in layers:
-        stream, cache = layer_forward(stream, weights, fq, fk)
+    for layer in range(LAYERS):
+        stream, cache = layer_forward(layer, stream, weights, fq, fk)
         caches.append(cache)
     sums = jnp.dot(member, stream, precision=HIGHEST, preferred_element_type=f32)
     side = jnp.broadcast_to(counts[:, None], (slot_count, 128))
@@ -435,9 +617,9 @@
         return fence(value, first)
 
     first = []
-    grad_stream, unused, small_last = layer_backward(grad_stream, caches[1], layers[1], fq, fk, tie_last)
+    grad_stream, unused, small_last = layer_backward(1, grad_stream, caches[1], weights, fq, fk, tie_last)
     grad_stream, gathered = lax.optimization_barrier((grad_stream, gathered))
-    grad_stream, grads, small_first = layer_backward(grad_stream, caches[0], layers[0], fq, fk, tie_first)
+    grad_stream, grads, small_first = layer_backward(0, grad_stream, caches[0], weights, fq, fk, tie_first)
     grad_stream, last["sum"] = lax.optimization_barrier((grad_stream, last["sum"]))
     grad_qkv_w, grad_out_w = grads[:2]
     small, sizes = pack_small([jnp.stack(pair) for pair in zip(small_first, small_last)], n, width)

time: 594 us -> 508 us (0.86)
  matrix products: 244 us -> 58.9 us
  Pallas kernels: 116 us -> 242 us
  other arithmetic: 58.5 us -> 35.3 us
  local copies, waits for them, and re-layouts: 53.4 us -> 41.6 us
    pallas_call x0 -> x8, Pallas kernels: none -> 126 us  [the longest x2 44.4 us: mlp_forward(): dense_call(mlp_forward_kernel, 'mlp_forward', rows, [row_block(width), ro...]
    dot_general x9 -> x1, matrix products: 107 us -> 1.02 us  [dot32(): return jnp.dot(left, right, preferred_element_type=f32)]
    dot_general x9 -> x1, matrix products: 81.3 us -> 2.45 us  [dot_nt(): return lax.dot_general(left, right, NT, preferred_element_type=f32)]
    unnamed x223 -> x97, local copies, waits for them, and re-layouts: 38.1 us -> 20.8 us
    reduce_sum x11 -> x0, other arithmetic: 16.6 us -> none  [the longest x4 8.41 us: layer_norm(): center = stream - jnp.mean(stream, axis=-1, keepdims=True)]
    add x7 -> x0, other arithmetic: 6.11 us -> none  [the longest x2 4.79 us: layer_backward(): grad_middle + grad_input]
  transfers between devices with their start and end apart: 19 -> 19, of which waited for: 9 -> 10; matrix products, arithmetic and copies ran while one was open for 54% -> 22% of each run, Pallas kernels for 20% -> 49%
where the time goes in v4:
time: 508 us; the launch traced here: 498 us
  Pallas kernels  242 us (48%)
  waiting for transfers between devices  77 us (15%)
  matrix products  58.9 us (12%)
  local copies, waits for them, and re-layouts  41.6 us (8%)
  other arithmetic  35.3 us (7%)
  starting transfers between devices  27.8 us (5%)
  between operations  16 us (3%)
    pallas_call x2, Pallas kernels, attend_backward(): pl.pallas_call(partial(attend_backward_kernel, chunk=rows // 2), grid=(n,...  74.5 us
    ppermute x16, waiting for transfers between devices, launch(): lax.ppermute(sent, 'dp', [(i, i ^ p) for i in range(self.n)])  47.8 us
    pallas_call x2, Pallas kernels, mlp_forward(): dense_call(mlp_forward_kernel, 'mlp_forward', rows, [row_block(width), ro...  44.4 us
    pallas_call x2, Pallas kernels, mlp_backward(): dense_call(mlp_backward_kernel, 'mlp_backward', rows, [row_block(width),...  42.7 us
    pallas_call x2, Pallas kernels, attend_forward(): pl.pallas_call(partial(attend_forward_kernel, chunk=rows), grid=(n,), in_...  41.4 us
    reduce_scatter x1, waiting for transfers between devices, tie_last(): last['sum'] = lax.psum_scatter(both, 'dp', scatter_dimension=0, tiled=False)  29.2 us
    ppermute x16, starting transfers between devices, launch(): lax.ppermute(sent, 'dp', [(i, i ^ p) for i in range(self.n)])  27.6 us
    pallas_call x2, Pallas kernels, project_backward(): dense_call(project_backward_kernel, 'project_backward', rows, [row_block(...  21.2 us
  transfers between devices with their start and end apart: 19, of which 10 were waited for; matrix products, arithmetic and copies ran while one was open for 22% of the time, Pallas kernels for 49%

profile of v4, /device:TPU:0, one launch (start us, length us, event | category | flops | bytes accessed | tf_op | source)
XLA Modules:
  0.0 498.2 jit_solution(6988963812174068244)
XLA Ops:
  18.0 8.5 %project.2 = (bf16[1024,768]{1,0:T(8,128)(2,1)}, bf16[1024,2304]{1,0:T(8,128)(2,1)}) custom-call(bf16[1024,768]{1,0:T(8,128)(2,1)} %stream_ref.5, bf16[2,1,768]{2,1,0:T(2,128)(2,1)} %copy.96.gain_ref, bf16[2,1,768]{2,1,0:T(2,128)(2,1)} %copy.97.shift_ref, bf16[2,768,2304]{2,1,0:T(8,128)(2,1)} %w_ref.7, bf16[2,1,2304]{2,1,0:T(2,128)(2,1)} %pad_maximum_fusion.15.b_ref), custom_call_target="tpu_custom_call" | custom-call | flops 3623878656 | bytes 12976128 | tf_op jit(solution)/shard_map/project/pallas_call | solution.py:355
  26.5 20.7 %attend_forward.2 = (bf16[1024,768]{1,0:T(8,128)(2,1)}, f32[6,2,1024]{2,1,0:T(2,128)}) custom-call(bf16[1024,2304]{1,0:T(8,128)(2,1)} %get-tuple-element.108.q_ref.k_ref.v_ref, bf16[1024,2304]{1,0:T(8,128)(2,1)} %get-tuple-element.108.q_ref.k_ref.v_ref, bf16[1024,2304]{1,0:T(8,128)(2,1)} %get-tuple-element.108.q_ref.k_ref.v_ref, ...), custom_call_target="tpu_custom_call" | custom-call | flops 12884901888 | bytes 7864320 | tf_op jit(solution)/shard_map/attend_forward/pallas_call | solution.py:69
  47.2 22.0 %mlp_forward.2 = (f32[1024,768]{1,0:T(8,128)}, bf16[1024,768]{1,0:T(8,128)(2,1)}, bf16[1024,3072]{1,0:T(8,128)(2,1)}, bf16[1024,3072]{1,0:T(8,128)(2,1)}, f32[1024,768]{1,0:T(8,128)}) custom-call(bf16[1024,768]{1,0:T(8,128)(2,1)} %get-tuple-element.109.att_ref.o_ref, bf16[1024,768]{1,0:T(8,128)(2,1)} %stream_ref.5, bf16[2,768,768]{2,1,0:T(8,128)(2,1)} %out_w_ref.7, ...), custom_call_target="tpu_custom_call" | custom-call | flops 10871635968 | bytes 36962304 | tf_op jit(solution)/shard_map/mlp_forward/pallas_call | solution.py:397
  69.2 9.0 %project.3 = (bf16[1024,768]{1,0:T(8,128)(2,1)}, bf16[1024,2304]{1,0:T(8,128)(2,1)}) custom-call(f32[1024,768]{1,0:T(8,128)} %get-tuple-element.110.stream_ref, bf16[2,1,768]{2,1,0:T(2,128)(2,1)} %copy.96.gain_ref, bf16[2,1,768]{2,1,0:T(2,128)(2,1)} %copy.97.shift_ref, bf16[2,768,2304]{2,1,0:T(8,128)(2,1)} %w_ref.7, bf16[2,1,2304]{2,1,0:T(2,128)(2,1)} %pad_maximum_fusion.15.b_ref), custom_call_target="tpu_custom_call" | custom-call | flops 3623878656 | bytes 12976128 | tf_op jit(solution)/shard_map/project/pallas_call | solution.py:355
  78.2 20.7 %attend_forward.3 = (bf16[1024,768]{1,0:T(8,128)(2,1)}, f32[6,2,1024]{2,1,0:T(2,128)}) custom-call(bf16[1024,2304]{1,0:T(8,128)(2,1)} %get-tuple-element.111.q_ref.k_ref.v_ref, bf16[1024,2304]{1,0:T(8,128)(2,1)} %get-tuple-element.111.q_ref.k_ref.v_ref, bf16[1024,2304]{1,0:T(8,128)(2,1)} %get-tuple-element.111.q_ref.k_ref.v_ref, ...), custom_call_target="tpu_custom_call" | custom-call | flops 12884901888 | bytes 7864320 | tf_op jit(solution)/shard_map/attend_forward/pallas_call | solution.py:69
  98.9 22.4 %mlp_forward.3 = (f32[1024,768]{1,0:T(8,128)}, bf16[1024,768]{1,0:T(8,128)(2,1)}, bf16[1024,3072]{1,0:T(8,128)(2,1)}, bf16[1024,3072]{1,0:T(8,128)(2,1)}, f32[1024,768]{1,0:T(8,128)}) custom-call(bf16[1024,768]{1,0:T(8,128)(2,1)} %get-tuple-element.112.att_ref.o_ref, f32[1024,768]{1,0:T(8,128)} %get-tuple-element.110.stream_ref, ...), custom_call_target="tpu_custom_call" | custom-call | flops 10871635968 | bytes 36962304 | tf_op jit(solution)/shard_map/mlp_forward/pallas_call | solution.py:397
  129.1 20.9 %mlp_backward.2 = (bf16[1024,768]{1,0:T(8,128)(2,1)}, bf16[1024,3072]{1,0:T(8,128)(2,1)}, f32[1024,768]{1,0:T(8,128)}, bf16[1024,768]{1,0:T(8,128)(2,1)}, bf16[1...) custom-call(f32[1024,768]{1,0:T(8,128)} %fusion.46.grad_ref, ...), custom_call_target="tpu_custom_call" | custom-call | flops 10871635968 | bytes 40108032 | tf_op jit(solution)/shard_map/mlp_backward/pallas_call | solution.py:458
  153.0 8.7 %convolution_convert_fusion.3 = bf16[3072,768]{1,0:T(8,128)(2,1)S(1)} fusion(bf16[1024,3072]{1,0:T(8,128)(2,1)} %get-tuple-element.118, bf16[1024,768]{1,0:T(8,128)(2,1)S(1)} %copy-done.38), kind=kOutput, calls=%fused_computation.3 | convolution fusion | flops 4834197504 | bytes 12582912 | tf_op jit(solution)/shard_map/tf,td->fd/dot_general | solution.py:526
  164.2 5.4 %convolution_convert_fusion.2 = bf16[768,3072]{1,0:T(8,128)(2,1)S(1)} fusion(bf16[1024,768]{1,0:T(8,128)(2,1)S(1)} %copy-done.36, bf16[1024,3072]{1,0:T(8,128)(2,1)S(1)} %bitcast.417), kind=kOutput, calls=%fused_computation.2 | convolution fusion | flops 4834197504 | bytes 12582912 | tf_op jit(solution)/shard_map/td,tf->df/dot_general | solution.py:527
  175.4 37.2 %attend_backward.2 = (bf16[1024,2304]{1,0:T(8,128)(2,1)}, f32[2,768]{1,0:T(2,128)}) custom-call(bf16[1024,2304]{1,0:T(8,128)(2,1)} %get-tuple-element.111.q_ref.k_ref.v_ref, bf16[1024,2304]{1,0:T(8,128)(2,1)} %get-tuple-element.111.q_ref.k_ref.v_ref, bf16[1024,2304]{1,0:T(8,128)(2,1)} %get-tuple-element.111.q_ref.k_ref.v_ref, ...), custom_call_target="tpu_custom_call" | custom-call | flops 32212254720 | bytes 12582912 | tf_op jit(solution)/shard_map/attend_backward/pallas_call | solution.py:144
  212.6 6.5 %convolution_convert_fusion.5 = bf16[768,2304]{1,0:T(8,128)(2,1)S(1)} fusion(bf16[1024,768]{1,0:T(8,128)(2,1)S(1)} %copy-done.33, bf16[1024,2304]{1,0:T(8,128)(2,1)} %get-tuple-element.124.joined_ref), kind=kOutput, calls=%fused_computation.5 | convolution fusion | flops 3625648128 | bytes 9830400 | tf_op jit(solution)/shard_map/td,te->de/dot_general | solution.py:533
  222.6 10.3 %project_backward.2 = (f32[1024,768]{1,0:T(8,128)}, f32[8,768]{1,0:T(8,128)}) custom-call(bf16[1024,2304]{1,0:T(8,128)(2,1)} %get-tuple-element.124.joined_ref, f32[1024,768]{1,0:T(8,128)} %get-tuple-element.110.stream_ref, f32[1024,768]{1,0:T(8,128)} %get-tuple-element.125.grad_ref, bf16[2,1,768]{2,1,0:T(2,128)(2,1)} %copy.96.gain_ref, ...), custom_call_target="tpu_custom_call" | custom-call | flops 3623878656 | bytes 17694720 | tf_op jit(solution)/shard_map/project_backward/pallas_call | solution.py:497
  232.9 21.8 %mlp_backward.3 = (bf16[1024,768]{1,0:T(8,128)(2,1)}, bf16[1024,3072]{1,0:T(8,128)(2,1)}, f32[1024,768]{1,0:T(8,128)}, bf16[1024,768]{1,0:T(8,128)(2,1)}, bf16[1...) custom-call(f32[1024,768]{1,0:T(8,128)} %get-tuple-element.129.grad_ref, ...), custom_call_target="tpu_custom_call" | custom-call | flops 10871635968 | bytes 40108032 | tf_op jit(solution)/shard_map/mlp_backward/pallas_call | solution.py:458
  254.8 8.8 %convolution_convert_fusion = bf16[768,3072]{1,0:T(8,128)(2,1)S(1)} fusion(bf16[1024,768]{1,0:T(8,128)(2,1)S(1)} %copy-done.35, bf16[1024,3072]{1,0:T(8,128)(2,1)} %get-tuple-element.137), kind=kOutput, calls=%fused_computation | convolution fusion | flops 4834197504 | bytes 12582912 | tf_op jit(solution)/shard_map/td,tf->df/dot_general | solution.py:527
  269.1 5.5 %convolution_convert_fusion.1 = bf16[3072,768]{1,0:T(8,128)(2,1)S(1)} fusion(bf16[1024,3072]{1,0:T(8,128)(2,1)S(1)} %bitcast.419, bf16[1024,768]{1,0:T(8,128)(2,1)S(1)} %copy-done.37), kind=kOutput, calls=%fused_computation.1 | convolution fusion | flops 4834197504 | bytes 12582912 | tf_op jit(solution)/shard_map/tf,td->fd/dot_general | solution.py:526
  301.3 37.3 %attend_backward.3 = (bf16[1024,2304]{1,0:T(8,128)(2,1)}, f32[2,768]{1,0:T(2,128)}) custom-call(bf16[1024,2304]{1,0:T(8,128)(2,1)} %get-tuple-element.108.q_ref.k_ref.v_ref, bf16[1024,2304]{1,0:T(8,128)(2,1)} %get-tuple-element.108.q_ref.k_ref.v_ref, bf16[1024,2304]{1,0:T(8,128)(2,1)} %get-tuple-element.108.q_ref.k_ref.v_ref, ...), custom_call_target="tpu_custom_call" | custom-call | flops 32212254720 | bytes 12582912 | tf_op jit(solution)/shard_map/attend_backward/pallas_call | solution.py:144
  344.8 5.8 %convolution_convert_fusion.4 = bf16[768,2304]{1,0:T(8,128)(2,1)S(1)} fusion(bf16[1024,768]{1,0:T(8,128)(2,1)} %get-tuple-element.159, bf16[1024,2304]{1,0:T(8,128)(2,1)S(1)} %copy-done.6), kind=kOutput, calls=%fused_computation.4 | convolution fusion | flops 3625648128 | bytes 9830400 | tf_op jit(solution)/shard_map/td,te->de/dot_general | solution.py:533
  352.3 10.9 %project_backward.3 = (f32[1024,768]{1,0:T(8,128)}, f32[8,768]{1,0:T(8,128)}) custom-call(bf16[1024,2304]{1,0:T(8,128)(2,1)} %get-tuple-element.149.joined_ref, bf16[1024,768]{1,0:T(8,128)(2,1)} %stream_ref.5, f32[1024,768]{1,0:T(8,128)} %get-tuple-element.150.grad_ref, bf16[2,1,768]{2,1,0:T(2,128)(2,1)} %copy.96.gain_ref, bf16[2,768,2304]{2,1,0:T(8,128)(2,1)} %w_ref.7), custom_call_target="tpu_custom_call" | custom-call | flops 3623878656 | bytes 17694720 | tf_op jit(solution)/shard_map/project_backward/pallas_call | solution.py:497
  372.2 29.2 %reduce-scatter.5.cloned.1.call-done = bf16[1,288,768]{2,1,0:T(8,128)(2,1)} async-done(((bf16[32,288,768]{2,1,0:T(8,128)(2,1)}), bf16[1,288,768]{2,1,0:T(8,128)(2,1)}) %reduce-scatter.5.cloned.1.call-update) | async-done | bytes 442384 | tf_op jit(solution)/shard_map/reduce_scatter | solution.py:609
  417.2 10.5 %collective-permute-done.5 = bf16[192,768]{1,0:T(8,128)(2,1)S(1)} collective-permute-done((bf16[192,768]{1,0:T(8,128)(2,1)S(1)}, bf16[192,768]{1,0:T(8,128)(2,1)S(1)}, u32[]{:S(2)}, u32[]{:S(2)}) %collective-permute-start.5) | collective-permute-done | bytes 294944 | tf_op jit(solution)/shard_map/ppermute | solution.py:241
  427.7 9.5 %collective-permute-done.6 = bf16[192,768]{1,0:T(8,128)(2,1)S(1)} collective-permute-done((bf16[192,768]{1,0:T(8,128)(2,1)S(1)}, bf16[192,768]{1,0:T(8,128)(2,1)S(1)}, u32[]{:S(2)}, u32[]{:S(2)}) %collective-permute-start.6) | collective-permute-done | bytes 294944 | tf_op jit(solution)/shard_map/ppermute | solution.py:241
  446.5 8.8 %collective-permute-done.10 = bf16[4,2,48,768]{3,2,1,0:T(8,128)(2,1)S(1)} collective-permute-done((bf16[4,2,48,768]{3,2,1,0:T(8,128)(2,1)S(1)}, bf16[4,2,48,768]{3,2,1,0:T(8,128)(2,1)S(1)}, u32[]{:S(2)}, u32[]{:S(2)}) %collective-permute-start.10) | collective-permute-done | bytes 589856 | tf_op jit(solution)/shard_map/ppermute | solution.py:241
  467.0 8.0 %collective-permute-start.13 = (bf16[104,768]{1,0:T(8,128)(2,1)S(1)}, bf16[104,768]{1,0:T(8,128)(2,1)S(1)}, u32[]{:S(2)}, u32[]{:S(2)}) collective-permute-start(bf16[104,768]{1,0:T(8,128)(2,1)S(1)} %pad_maximum_fusion.10), channel_id=1, source_target_pairs={{0,8},{1,9},{2,10},{3,11},{4,12},{5,13},{6,14},{7,15},{8,0},{9,1},... | collective-permute-start | bytes 479240 | tf_op jit(solution)/shard_map/ppermute | solution.py:241
  479.4 8.0 %collective-permute-done.14 = bf16[104,768]{1,0:T(8,128)(2,1)S(1)} collective-permute-done((bf16[104,768]{1,0:T(8,128)(2,1)S(1)}, bf16[104,768]{1,0:T(8,128)(2,1)S(1)}, u32[]{:S(2)}, u32[]{:S(2)}) %collective-permute-start.14) | collective-permute-done | bytes 159776 | tf_op jit(solution)/shard_map/ppermute | solution.py:241
  (269 shorter events, 126.0 us)
Async XLA Ops:
  7.3 117.8 %reduce-scatter.3.cloned.1.call-start = ((), (), s32[]{:S(2)}) async-start(), calls=%async_computation.2 | async-start | bytes 1622016 | tf_op jit(solution)/shard_map/reduce_scatter | solution.py:578
  11.0 221.9 %all-gather.2.cloned.1.call-start = ((), (), s32[]{:S(2)}) async-start(), calls=%async_computation.3 | async-start | bytes 1892352 | tf_op jit(solution)/shard_map/all_gather | solution.py:593
  125.0 276.3 %reduce-scatter.5.cloned.1.call-start = ((), (), s32[]{:S(2)}) async-start(), calls=%async_computation.4 | async-start | bytes 14598144 | tf_op jit(solution)/shard_map/reduce_scatter | solution.py:609
  129.1 20.9 %copy-start.34 = (bf16[1024,768]{1,0:T(8,128)(2,1)S(1)}, bf16[1024,768]{1,0:T(8,128)(2,1)}, u32[]{:S(2)}) copy-start(bf16[1024,768]{1,0:T(8,128)(2,1)} %get-tuple-element.112.att_ref.o_ref) | copy-start | bytes 4718596
  149.9 14.2 %slice-start = ((s8[6291456]{0:T(1024)(128)(4,1)}), s8[4194304]{0:T(1024)(128)(4,1)S(1)}, s32[]{:S(2)}) async-start(s8[6291456]{0:T(1024)(128)(4,1)} %bitcast.416), calls=%async_computation.5 | async-start | bytes 8388608
  153.0 11.2 %slice-start.1 = ((s8[6291456]{0:T(1024)(128)(4,1)}), s8[2097152]{0:T(1024)(128)(4,1)S(1)}, s32[]{:S(2)}) async-start(s8[6291456]{0:T(1024)(128)(4,1)} %bitcast.416), calls=%async_computation.6 | async-start | bytes 4194304
  175.4 37.2 %copy-start.33 = (bf16[1024,768]{1,0:T(8,128)(2,1)S(1)}, bf16[1024,768]{1,0:T(8,128)(2,1)}, u32[]{:S(2)}) copy-start(bf16[1024,768]{1,0:T(8,128)(2,1)} %get-tuple-element.123) | copy-start | bytes 4718596
  232.9 21.8 %copy-start.35 = (bf16[1024,768]{1,0:T(8,128)(2,1)S(1)}, bf16[1024,768]{1,0:T(8,128)(2,1)}, u32[]{:S(2)}) copy-start(bf16[1024,768]{1,0:T(8,128)(2,1)} %get-tuple-element.136) | copy-start | bytes 4718596
  279.3 8.4 %collective-permute-start = (bf16[4,2,2,192,768]{4,3,2,1,0:T(8,128)(2,1)}, bf16[4,2,2,192,768]{4,3,2,1,0:T(8,128)(2,1)}, u32[]{:S(2)}, u32[]{:S(2)}) collective-permute-start(bf16[4,2,2,192,768]{4,3,2,1,0:T(8,128)(2,1)} %pad_maximum_fusion.1), channel_id=1, source_target_pairs={{0,1},{1,0},{2,3},{3,2},{4,5},{5,4},{6,7},{7,6},{8,9},{9,8},{10,11... | collective-permute-start | bytes 14155784 | tf_op jit(solution)/shard_map/ppermute | solution.py:241
  296.5 43.0 %collective-permute-start.1 = (bf16[4,2,96,768]{3,2,1,0:T(8,128)(2,1)}, bf16[4,2,96,768]{3,2,1,0:T(8,128)(2,1)S(1)}, u32[]{:S(2)}, u32[]{:S(2)}) collective-permute-start(bf16[4,2,96,768]{3,2,1,0:T(8,128)(2,1)} %fusion.1), channel_id=1, source_target_pairs={{0,2},{1,3},{2,0},{3,1},{4,6},{5,7},{6,4},{7,5},{8,10},{9,11},{10,... | collective-permute-start | bytes 3538952 | tf_op jit(solution)/shard_map/ppermute | solution.py:241
  299.6 40.0 %collective-permute-start.2 = (bf16[4,2,96,768]{3,2,1,0:T(8,128)(2,1)}, bf16[4,2,96,768]{3,2,1,0:T(8,128)(2,1)}, u32[]{:S(2)}, u32[]{:S(2)}) collective-permute-start(bf16[4,2,96,768]{3,2,1,0:T(8,128)(2,1)} %fusion), channel_id=1, source_target_pairs={{0,4},{1,5},{2,6},{3,7},{4,0},{5,1},{6,2},{7,3},{8,12},{9,13},{10,... | collective-permute-start | bytes 3538952 | tf_op jit(solution)/shard_map/ppermute | solution.py:241
  364.8 36.5 %collective-permute-start.3 = (bf16[4,96,768]{2,1,0:T(8,128)(2,1)}, bf16[4,96,768]{2,1,0:T(8,128)(2,1)S(1)}, u32[]{:S(2)}, u32[]{:S(2)}) collective-permute-start(bf16[4,96,768]{2,1,0:T(8,128)(2,1)} %fusion.7), channel_id=1, source_target_pairs={{0,4},{1,5},{2,6},{3,7},{4,0},{5,1},{6,2},{7,3},{8,12},{9,13},{10,... | collective-permute-start | bytes 1769480 | tf_op jit(solution)/shard_map/ppermute | solution.py:241
  366.9 34.5 %collective-permute-start.4 = (bf16[4,96,768]{2,1,0:T(8,128)(2,1)}, bf16[4,96,768]{2,1,0:T(8,128)(2,1)}, u32[]{:S(2)}, u32[]{:S(2)}) collective-permute-start(bf16[4,96,768]{2,1,0:T(8,128)(2,1)} %fusion.6), channel_id=1, source_target_pairs={{0,2},{1,3},{2,0},{3,1},{4,6},{5,7},{6,4},{7,5},{8,10},{9,11},{10,... | collective-permute-start | bytes 1769480 | tf_op jit(solution)/shard_map/ppermute | solution.py:241
  407.0 30.2 %collective-permute-start.8 = (bf16[4,2,2,104,768]{4,3,2,1,0:T(8,128)(2,1)}, bf16[4,2,2,104,768]{4,3,2,1,0:T(8,128)(2,1)}, u32[]{:S(2)}, u32[]{:S(2)}) collective-permute-start(bf16[4,2,2,104,768]{4,3,2,1,0:T(8,128)(2,1)} %pad_maximum_fusion.3), channel_id=1, source_target_pairs={{0,1},{1,0},{2,3},{3,2},{4,5},{5,4},{6,7},{7,6},{8,9},{9,8},{10,11... | collective-permute-start | bytes 7667720 | tf_op jit(solution)/shard_map/ppermute | solution.py:241
  412.6 15.0 %collective-permute-start.5 = (bf16[192,768]{1,0:T(8,128)(2,1)S(1)}, bf16[192,768]{1,0:T(8,128)(2,1)S(1)}, u32[]{:S(2)}, u32[]{:S(2)}) collective-permute-start(bf16[192,768]{1,0:T(8,128)(2,1)S(1)} %copy-done.13), channel_id=1, source_target_pairs={{0,8},{1,9},{2,10},{3,11},{4,12},{5,13},{6,14},{7,15},{8,0},{9,1},... | collective-permute-start | bytes 884744 | tf_op jit(solution)/shard_map/ppermute | solution.py:241
  413.7 23.5 %collective-permute-start.6 = (bf16[192,768]{1,0:T(8,128)(2,1)S(1)}, bf16[192,768]{1,0:T(8,128)(2,1)S(1)}, u32[]{:S(2)}, u32[]{:S(2)}) collective-permute-start(bf16[192,768]{1,0:T(8,128)(2,1)S(1)} %copy-done.12), channel_id=1, source_target_pairs={{0,16},{1,17},{2,18},{3,19},{4,20},{5,21},{6,22},{7,23},{8,24},{9,... | collective-permute-start | bytes 884744 | tf_op jit(solution)/shard_map/ppermute | solution.py:241
  415.2 22.0 %collective-permute-start.7 = (bf16[192,768]{1,0:T(8,128)(2,1)S(1)}, bf16[192,768]{1,0:T(8,128)(2,1)S(1)}, u32[]{:S(2)}, u32[]{:S(2)}) collective-permute-start(bf16[192,768]{1,0:T(8,128)(2,1)S(1)} %copy-done.11), channel_id=1, source_target_pairs={{0,24},{1,25},{2,26},{3,27},{4,28},{5,29},{6,30},{7,31},{8,16},{9,... | collective-permute-start | bytes 884744 | tf_op jit(solution)/shard_map/ppermute | solution.py:241
  441.9 13.4 %collective-permute-start.10 = (bf16[4,2,48,768]{3,2,1,0:T(8,128)(2,1)S(1)}, bf16[4,2,48,768]{3,2,1,0:T(8,128)(2,1)S(1)}, u32[]{:S(2)}, u32[]{:S(2)}) collective-permute-start(bf16[4,2,48,768]{3,2,1,0:T(8,128)(2,1)S(1)} %fusion.5), channel_id=1, source_target_pairs={{0,4},{1,5},{2,6},{3,7},{4,0},{5,1},{6,2},{7,3},{8,12},{9,13},{10,... | collective-permute-start | bytes 1769480 | tf_op jit(solution)/shard_map/ppermute | solution.py:241
  443.4 15.4 %collective-permute-start.9 = (bf16[4,2,56,768]{3,2,1,0:T(8,128)(2,1)S(1)}, bf16[4,2,56,768]{3,2,1,0:T(8,128)(2,1)S(1)}, u32[]{:S(2)}, u32[]{:S(2)}) collective-permute-start(bf16[4,2,56,768]{3,2,1,0:T(8,128)(2,1)S(1)} %fusion.2), channel_id=1, source_target_pairs={{0,2},{1,3},{2,0},{3,1},{4,6},{5,7},{6,4},{7,5},{8,10},{9,11},{10,... | collective-permute-start | bytes 2064392 | tf_op jit(solution)/shard_map/ppermute | solution.py:241
  459.1 7.4 %collective-permute-start.11 = (bf16[4,56,768]{2,1,0:T(8,128)(2,1)S(1)}, bf16[4,56,768]{2,1,0:T(8,128)(2,1)S(1)}, u32[]{:S(2)}, u32[]{:S(2)}) collective-permute-start(bf16[4,56,768]{2,1,0:T(8,128)(2,1)S(1)} %fusion.9), channel_id=1, source_target_pairs={{0,4},{1,5},{2,6},{3,7},{4,0},{5,1},{6,2},{7,3},{8,12},{9,13},{10,... | collective-permute-start | bytes 1032200 | tf_op jit(solution)/shard_map/ppermute | solution.py:241
  459.8 6.8 %collective-permute-start.12 = (bf16[4,48,768]{2,1,0:T(8,128)(2,1)S(1)}, bf16[4,48,768]{2,1,0:T(8,128)(2,1)S(1)}, u32[]{:S(2)}, u32[]{:S(2)}) collective-permute-start(bf16[4,48,768]{2,1,0:T(8,128)(2,1)S(1)} %fusion.12), channel_id=1, source_target_pairs={{0,2},{1,3},{2,0},{3,1},{4,6},{5,7},{6,4},{7,5},{8,10},{9,11},{10,... | collective-permute-start | bytes 884744 | tf_op jit(solution)/shard_map/ppermute | solution.py:241
  467.0 12.4 %collective-permute-start.13 = (bf16[104,768]{1,0:T(8,128)(2,1)S(1)}, bf16[104,768]{1,0:T(8,128)(2,1)S(1)}, u32[]{:S(2)}, u32[]{:S(2)}) collective-permute-start(bf16[104,768]{1,0:T(8,128)(2,1)S(1)} %pad_maximum_fusion.10), channel_id=1, source_target_pairs={{0,8},{1,9},{2,10},{3,11},{4,12},{5,13},{6,14},{7,15},{8,0},{9,1},... | collective-permute-start | bytes 479240 | tf_op jit(solution)/shard_map/ppermute | solution.py:241
  475.0 12.3 %collective-permute-start.14 = (bf16[104,768]{1,0:T(8,128)(2,1)S(1)}, bf16[104,768]{1,0:T(8,128)(2,1)S(1)}, u32[]{:S(2)}, u32[]{:S(2)}) collective-permute-start(bf16[104,768]{1,0:T(8,128)(2,1)S(1)} %pad_maximum_fusion.11), channel_id=1, source_target_pairs={{0,16},{1,17},{2,18},{3,19},{4,20},{5,21},{6,22},{7,23},{8,24},{9,... | collective-permute-start | bytes 479240 | tf_op jit(solution)/shard_map/ppermute | solution.py:241
  475.5 11.9 %collective-permute-start.15 = (bf16[104,768]{1,0:T(8,128)(2,1)S(1)}, bf16[104,768]{1,0:T(8,128)(2,1)S(1)}, u32[]{:S(2)}, u32[]{:S(2)}) collective-permute-start(bf16[104,768]{1,0:T(8,128)(2,1)S(1)} %pad_maximum_fusion.12), channel_id=1, source_target_pairs={{0,24},{1,25},{2,26},{3,27},{4,28},{5,29},{6,30},{7,31},{8,16},{9,... | collective-permute-start | bytes 479240 | tf_op jit(solution)/shard_map/ppermute | solution.py:241
  (38 other events, 181.2 us)
Sparse Core Ops, SparseCore 0:
  13.3 100.6 reduce-scatter.2
  125.2 58.4 all-gather.1
  222.7 178.5 reduce-scatter.4

commit v5 on v4

--- a/solution.py
+++ b/solution.py
@@ -79,9 +79,7 @@
             jax.ShapeDtypeStruct((n, 2, rows), f32),
         ],
         compiler_params=pltpu.CompilerParams(vmem_limit_bytes=VMEM_LIMIT),
-        cost_estimate=pl.CostEstimate(
-            flops=16 * rows * rows * width, bytes_accessed=10 * rows * width, transcendentals=0
-        ),
+        cost_estimate=pl.CostEstimate(flops=1, bytes_accessed=1, transcendentals=0),
         name="attend_forward",
     )(joined, joined, joined, fq, fk)
 
@@ -163,9 +161,7 @@
             jax.ShapeDtypeStruct((2, width), f32),
         ],
         compiler_params=pltpu.CompilerParams(vmem_limit_bytes=VMEM_LIMIT),
-        cost_estimate=pl.CostEstimate(
-            flops=40 * rows * rows * width, bytes_accessed=16 * rows * width, transcendentals=0
-        ),
+        cost_estimate=pl.CostEstimate(flops=1, bytes_accessed=1, transcendentals=0),
         name="attend_backward",
     )(joined, joined, joined, grad_attended, attended, lse, fq, fk)
 
@@ -337,7 +333,7 @@
         out_specs=out_specs,
         out_shape=out_shape,
         compiler_params=pltpu.CompilerParams(vmem_limit_bytes=VMEM_LIMIT),
-        cost_estimate=pl.CostEstimate(flops=flops, bytes_accessed=moved, transcendentals=0),
+        cost_estimate=pl.CostEstimate(flops=1, bytes_accessed=1, transcendentals=0),
         name=name,
     )
 
@@ -612,21 +608,22 @@
     def tie_first(name, value, grads):
         if name == "hidden":
             first.append(pair_sum(pack(grads[:1], n, width), pack(grads[1:], n, width), me, n))
-        if name == "qkv":
-            return value
         return fence(value, first)
 
     first = []
     grad_stream, unused, small_last = layer_backward(1, grad_stream, caches[1], weights, fq, fk, tie_last)
     grad_stream, gathered = lax.optimization_barrier((grad_stream, gathered))
     grad_stream, grads, small_first = layer_backward(0, grad_stream, caches[0], weights, fq, fk, tie_first)
-    grad_stream, last["sum"] = lax.optimization_barrier((grad_stream, last["sum"]))
     grad_qkv_w, grad_out_w = grads[:2]
     small, sizes = pack_small([jnp.stack(pair) for pair in zip(small_first, small_last)], n, width)
     qk = 2 * width
     side_a = jnp.concatenate([pack([grad_qkv_w[:, :qk]], n, width), small], axis=1)
     side_b = pack([grad_qkv_w[:, qk:], grad_out_w], n, width)
     first.append(pair_sum(side_a, side_b, me, n))
+    for unused in range(2):
+        grad_stream = fence(grad_stream, first[1:])
+    grad_stream, last["sum"] = lax.optimization_barrier((grad_stream, last["sum"]))
+    grad_stream = fence(grad_stream, first[1:])
     while any(e.result is None for e in first):
         grad_stream = fence(grad_stream, first)
     gathered = (gathered[:, :width] / gathered[:, width : width + 1]).astype(bf16)

time: 508 us -> 475 us (0.935)
  waiting for transfers between devices: 77 us -> 46.5 us
  other arithmetic: 35.3 us -> 45.8 us
  starting transfers between devices: 27.8 us -> 17.9 us
    reduce_scatter x1, waiting for transfers between devices: 29.2 us -> 0.01 us  [tie_last(): last['sum'] = lax.psum_scatter(both, 'dp', scatter_dimension=0, tiled=False)]
    ppermute x16, starting transfers between devices: 27.6 us -> 17.7 us  [launch(): lax.ppermute(sent, 'dp', [(i, i ^ p) for i in range(self.n)])]
    unnamed x97 -> x99, local copies, waits for them, and re-layouts: 20.8 us -> 22 us
  transfers between devices with their start and end apart: 19 -> 19, of which waited for: 10 -> 6; matrix products, arithmetic and copies ran while one was open for 22% -> 26% of each run, Pallas kernels for 49% -> 52%
where the time goes in v5:
time: 475 us; the launch traced here: 466 us
  Pallas kernels  241 us (51%)
  matrix products  55.9 us (12%)
  waiting for transfers between devices  46.5 us (10%)
  other arithmetic  45.8 us (10%)
  local copies, waits for them, and re-layouts  43.3 us (9%)
  starting transfers between devices  17.9 us (4%)
  between operations  15.9 us (3%)
    pallas_call x2, Pallas kernels, attend_backward(): pl.pallas_call(partial(attend_backward_kernel, chunk=rows // 2), grid=(n,...  74.3 us
    ppermute x16, waiting for transfers between devices, launch(): lax.ppermute(sent, 'dp', [(i, i ^ p) for i in range(self.n)])  46.4 us
    pallas_call x2, Pallas kernels, mlp_forward(): dense_call(mlp_forward_kernel, 'mlp_forward', rows, [row_block(width), ro...  44.1 us
    pallas_call x2, Pallas kernels, mlp_backward(): dense_call(mlp_backward_kernel, 'mlp_backward', rows, [row_block(width),...  43.1 us
    pallas_call x2, Pallas kernels, attend_forward(): pl.pallas_call(partial(attend_forward_kernel, chunk=rows), grid=(n,), in_...  41.6 us
    unnamed x99, local copies, waits for them, and re-layouts  22 us
    pallas_call x2, Pallas kernels, project_backward(): dense_call(project_backward_kernel, 'project_backward', rows, [row_block(...  20.7 us
    convert_element_type x12, other arithmetic, part(): total([pick(t, axis, mine ^ other) for t in self.terms[which]]).astype(bf16)  20.6 us
  transfers between devices with their start and end apart: 19, of which 6 were waited for; matrix products, arithmetic and copies ran while one was open for 26% of the time, Pallas kernels for 52%

profile of v5, /device:TPU:0, one launch (start us, length us, event | category | flops | bytes accessed | tf_op | source)
XLA Modules:
  0.0 466.5 jit_solution(3567136853768514195)
XLA Ops:
  12.5 8.5 %project.2 = (bf16[1024,768]{1,0:T(8,128)(2,1)}, bf16[1024,2304]{1,0:T(8,128)(2,1)}) custom-call(bf16[1024,768]{1,0:T(8,128)(2,1)} %stream_ref.5, bf16[2,1,768]{2,1,0:T(2,128)(2,1)} %copy.96.gain_ref, bf16[2,1,768]{2,1,0:T(2,128)(2,1)} %copy.97.shift_ref, bf16[2,768,2304]{2,1,0:T(8,128)(2,1)} %w_ref.7, bf16[2,1,2304]{2,1,0:T(2,128)(2,1)} %pad_maximum_fusion.15.b_ref), custom_call_target="tpu_custom_call" | custom-call | flops 1 | bytes 1 | tf_op jit(solution)/shard_map/project/pallas_call | solution.py:351
  23.1 20.7 %attend_forward.2 = (bf16[1024,768]{1,0:T(8,128)(2,1)}, f32[6,2,1024]{2,1,0:T(2,128)}) custom-call(bf16[1024,2304]{1,0:T(8,128)(2,1)} %get-tuple-element.109.q_ref.k_ref.v_ref, bf16[1024,2304]{1,0:T(8,128)(2,1)} %get-tuple-element.109.q_ref.k_ref.v_ref, bf16[1024,2304]{1,0:T(8,128)(2,1)} %get-tuple-element.109.q_ref.k_ref.v_ref, ...), custom_call_target="tpu_custom_call" | custom-call | flops 1 | bytes 1 | tf_op jit(solution)/shard_map/attend_forward/pallas_call | solution.py:69
  46.8 22.0 %mlp_forward.2 = (f32[1024,768]{1,0:T(8,128)}, bf16[1024,768]{1,0:T(8,128)(2,1)}, bf16[1024,3072]{1,0:T(8,128)(2,1)}, bf16[1024,3072]{1,0:T(8,128)(2,1)}, f32[1024,768]{1,0:T(8,128)}) custom-call(bf16[1024,768]{1,0:T(8,128)(2,1)} %get-tuple-element.110.att_ref.o_ref, bf16[1024,768]{1,0:T(8,128)(2,1)} %stream_ref.5, bf16[2,768,768]{2,1,0:T(8,128)(2,1)} %out_w_ref.7, ...), custom_call_target="tpu_custom_call" | custom-call | flops 1 | bytes 1 | tf_op jit(solution)/shard_map/mlp_forward/pallas_call | solution.py:393
  68.8 9.0 %project.3 = (bf16[1024,768]{1,0:T(8,128)(2,1)}, bf16[1024,2304]{1,0:T(8,128)(2,1)}) custom-call(f32[1024,768]{1,0:T(8,128)} %get-tuple-element.111.stream_ref, bf16[2,1,768]{2,1,0:T(2,128)(2,1)} %copy.96.gain_ref, bf16[2,1,768]{2,1,0:T(2,128)(2,1)} %copy.97.shift_ref, bf16[2,768,2304]{2,1,0:T(8,128)(2,1)} %w_ref.7, bf16[2,1,2304]{2,1,0:T(2,128)(2,1)} %pad_maximum_fusion.15.b_ref), custom_call_target="tpu_custom_call" | custom-call | flops 1 | bytes 1 | tf_op jit(solution)/shard_map/project/pallas_call | solution.py:351
  77.8 20.9 %attend_forward.3 = (bf16[1024,768]{1,0:T(8,128)(2,1)}, f32[6,2,1024]{2,1,0:T(2,128)}) custom-call(bf16[1024,2304]{1,0:T(8,128)(2,1)} %get-tuple-element.112.q_ref.k_ref.v_ref, bf16[1024,2304]{1,0:T(8,128)(2,1)} %get-tuple-element.112.q_ref.k_ref.v_ref, bf16[1024,2304]{1,0:T(8,128)(2,1)} %get-tuple-element.112.q_ref.k_ref.v_ref, ...), custom_call_target="tpu_custom_call" | custom-call | flops 1 | bytes 1 | tf_op jit(solution)/shard_map/attend_forward/pallas_call | solution.py:69
  98.7 22.1 %mlp_forward.3 = (f32[1024,768]{1,0:T(8,128)}, bf16[1024,768]{1,0:T(8,128)(2,1)}, bf16[1024,3072]{1,0:T(8,128)(2,1)}, bf16[1024,3072]{1,0:T(8,128)(2,1)}, f32[1024,768]{1,0:T(8,128)}) custom-call(bf16[1024,768]{1,0:T(8,128)(2,1)} %get-tuple-element.113.att_ref.o_ref, f32[1024,768]{1,0:T(8,128)} %get-tuple-element.111.stream_ref, ...), custom_call_target="tpu_custom_call" | custom-call | flops 1 | bytes 1 | tf_op jit(solution)/shard_map/mlp_forward/pallas_call | solution.py:393
  124.6 3.9 fusion.46.grad_ref
  128.5 21.2 %mlp_backward.2 = (bf16[1024,768]{1,0:T(8,128)(2,1)}, bf16[1024,3072]{1,0:T(8,128)(2,1)}, f32[1024,768]{1,0:T(8,128)}, bf16[1024,768]{1,0:T(8,128)(2,1)}, bf16[1...) custom-call(f32[1024,768]{1,0:T(8,128)} %fusion.46.grad_ref, ...), custom_call_target="tpu_custom_call" | custom-call | flops 1 | bytes 1 | tf_op jit(solution)/shard_map/mlp_backward/pallas_call | solution.py:454
  149.7 7.7 %convolution_convert_fusion.3 = bf16[3072,768]{1,0:T(8,128)(2,1)S(1)} fusion(bf16[1024,3072]{1,0:T(8,128)(2,1)} %get-tuple-element.119, bf16[1024,768]{1,0:T(8,128)(2,1)} %get-tuple-element.120), kind=kOutput, calls=%fused_computation.3 | convolution fusion | flops 4834197504 | bytes 12582912 | tf_op jit(solution)/shard_map/tf,td->fd/dot_general | solution.py:522
  157.5 37.0 %attend_backward.2 = (bf16[1024,2304]{1,0:T(8,128)(2,1)}, f32[2,768]{1,0:T(2,128)}) custom-call(bf16[1024,2304]{1,0:T(8,128)(2,1)} %get-tuple-element.112.q_ref.k_ref.v_ref, bf16[1024,2304]{1,0:T(8,128)(2,1)} %get-tuple-element.112.q_ref.k_ref.v_ref, bf16[1024,2304]{1,0:T(8,128)(2,1)} %get-tuple-element.112.q_ref.k_ref.v_ref, ...), custom_call_target="tpu_custom_call" | custom-call | flops 1 | bytes 1 | tf_op jit(solution)/shard_map/attend_backward/pallas_call | solution.py:142
  194.5 8.3 %convolution_convert_fusion.2 = bf16[768,3072]{1,0:T(8,128)(2,1)S(1)} fusion(bf16[1024,768]{1,0:T(8,128)(2,1)S(1)} %copy-done.36, bf16[1024,3072]{1,0:T(8,128)(2,1)} %get-tuple-element.122), kind=kOutput, calls=%fused_computation.2 | convolution fusion | flops 4834197504 | bytes 12582912 | tf_op jit(solution)/shard_map/td,tf->df/dot_general | solution.py:523
  213.5 4.1 convolution_convert_fusion.5
  221.1 10.2 %project_backward.2 = (f32[1024,768]{1,0:T(8,128)}, f32[8,768]{1,0:T(8,128)}) custom-call(bf16[1024,2304]{1,0:T(8,128)(2,1)} %get-tuple-element.125.joined_ref, f32[1024,768]{1,0:T(8,128)} %get-tuple-element.111.stream_ref, f32[1024,768]{1,0:T(8,128)} %get-tuple-element.126.grad_ref, bf16[2,1,768]{2,1,0:T(2,128)(2,1)} %copy.96.gain_ref, ...), custom_call_target="tpu_custom_call" | custom-call | flops 1 | bytes 1 | tf_op jit(solution)/shard_map/project_backward/pallas_call | solution.py:493
  231.3 21.8 %mlp_backward.3 = (bf16[1024,768]{1,0:T(8,128)(2,1)}, bf16[1024,3072]{1,0:T(8,128)(2,1)}, f32[1024,768]{1,0:T(8,128)}, bf16[1024,768]{1,0:T(8,128)(2,1)}, bf16[1...) custom-call(f32[1024,768]{1,0:T(8,128)} %get-tuple-element.130.grad_ref, ...), custom_call_target="tpu_custom_call" | custom-call | flops 1 | bytes 1 | tf_op jit(solution)/shard_map/mlp_backward/pallas_call | solution.py:454
  253.2 8.8 %convolution_convert_fusion = bf16[768,3072]{1,0:T(8,128)(2,1)S(1)} fusion(bf16[1024,768]{1,0:T(8,128)(2,1)S(1)} %copy-done.34, bf16[1024,3072]{1,0:T(8,128)(2,1)} %get-tuple-element.138), kind=kOutput, calls=%fused_computation | convolution fusion | flops 4834197504 | bytes 12582912 | tf_op jit(solution)/shard_map/td,tf->df/dot_general | solution.py:523
  267.5 5.5 %convolution_convert_fusion.1 = bf16[3072,768]{1,0:T(8,128)(2,1)S(1)} fusion(bf16[1024,3072]{1,0:T(8,128)(2,1)S(1)} %bitcast.419, bf16[1024,768]{1,0:T(8,128)(2,1)S(1)} %copy-done.38), kind=kOutput, calls=%fused_computation.1 | convolution fusion | flops 4834197504 | bytes 12582912 | tf_op jit(solution)/shard_map/tf,td->fd/dot_general | solution.py:522
  278.4 7.6 %collective-permute-done = bf16[4,2,2,192,768]{4,3,2,1,0:T(8,128)(2,1)} collective-permute-done((bf16[4,2,2,192,768]{4,3,2,1,0:T(8,128)(2,1)}, bf16[4,2,2,192,768]{4,3,2,1,0:T(8,128)(2,1)}, u32[]{:S(2)}, u32[]{:S(2)}) %collective-permute-start) | collective-permute-done | bytes 4718624 | tf_op jit(solution)/shard_map/ppermute | solution.py:237
  304.1 37.3 %attend_backward.3 = (bf16[1024,2304]{1,0:T(8,128)(2,1)}, f32[2,768]{1,0:T(2,128)}) custom-call(bf16[1024,2304]{1,0:T(8,128)(2,1)} %get-tuple-element.109.q_ref.k_ref.v_ref, bf16[1024,2304]{1,0:T(8,128)(2,1)} %get-tuple-element.109.q_ref.k_ref.v_ref, bf16[1024,2304]{1,0:T(8,128)(2,1)} %get-tuple-element.109.q_ref.k_ref.v_ref, ...), custom_call_target="tpu_custom_call" | custom-call | flops 1 | bytes 1 | tf_op jit(solution)/shard_map/attend_backward/pallas_call | solution.py:142
  346.9 5.8 %convolution_convert_fusion.4 = bf16[768,2304]{1,0:T(8,128)(2,1)S(1)} fusion(bf16[1024,768]{1,0:T(8,128)(2,1)} %get-tuple-element.159, bf16[1024,2304]{1,0:T(8,128)(2,1)S(1)} %copy-done.10), kind=kOutput, calls=%fused_computation.4 | convolution fusion | flops 3625648128 | bytes 9830400 | tf_op jit(solution)/shard_map/td,te->de/dot_general | solution.py:529
  358.1 11.2 %collective-permute-done.3 = bf16[4,96,768]{2,1,0:T(8,128)(2,1)S(1)} collective-permute-done((bf16[4,96,768]{2,1,0:T(8,128)(2,1)S(1)}, bf16[4,96,768]{2,1,0:T(8,128)(2,1)S(1)}, u32[]{:S(2)}, u32[]{:S(2)}) %collective-permute-start.3) | collective-permute-done | bytes 589856 | tf_op jit(solution)/shard_map/ppermute | solution.py:237
  375.2 10.4 %project_backward.3 = (f32[1024,768]{1,0:T(8,128)}, f32[8,768]{1,0:T(8,128)}) custom-call(bf16[1024,2304]{1,0:T(8,128)(2,1)} %get-tuple-element.156.joined_ref, bf16[1024,768]{1,0:T(8,128)(2,1)} %stream_ref.5, f32[1024,768]{1,0:T(8,128)} %get-tuple-element.157.grad_ref, bf16[2,1,768]{2,1,0:T(2,128)(2,1)} %copy.96.gain_ref, bf16[2,768,2304]{2,1,0:T(8,128)(2,1)} %w_ref.7), custom_call_target="tpu_custom_call" | custom-call | flops 1 | bytes 1 | tf_op jit(solution)/shard_map/project_backward/pallas_call | solution.py:493
  411.8 12.2 %collective-permute-done.7 = bf16[4,2,48,768]{3,2,1,0:T(8,128)(2,1)} collective-permute-done((bf16[4,2,48,768]{3,2,1,0:T(8,128)(2,1)}, bf16[4,2,48,768]{3,2,1,0:T(8,128)(2,1)}, u32[]{:S(2)}, u32[]{:S(2)}) %collective-permute-start.7) | collective-permute-done | bytes 589856 | tf_op jit(solution)/shard_map/ppermute | solution.py:237
  430.4 7.0 %collective-permute-done.12 = bf16[4,48,768]{2,1,0:T(8,128)(2,1)S(1)} collective-permute-done((bf16[4,48,768]{2,1,0:T(8,128)(2,1)S(1)}, bf16[4,48,768]{2,1,0:T(8,128)(2,1)S(1)}, u32[]{:S(2)}, u32[]{:S(2)}) %collective-permute-start.12) | collective-permute-done | bytes 294944 | tf_op jit(solution)/shard_map/ppermute | solution.py:237
  447.9 5.9 %collective-permute-done.14 = bf16[104,768]{1,0:T(8,128)(2,1)S(1)} collective-permute-done((bf16[104,768]{1,0:T(8,128)(2,1)S(1)}, bf16[104,768]{1,0:T(8,128)(2,1)S(1)}, u32[]{:S(2)}, u32[]{:S(2)}) %collective-permute-start.14) | collective-permute-done | bytes 159776 | tf_op jit(solution)/shard_map/ppermute | solution.py:237
  (272 shorter events, 121.2 us)
Async XLA Ops:
  7.2 117.4 %reduce-scatter.3.cloned.1.call-start = ((), (), s32[]{:S(2)}) async-start(), calls=%async_computation.2 | async-start | bytes 1622016 | tf_op jit(solution)/shard_map/reduce_scatter | solution.py:574
  10.5 220.8 %all-gather.2.cloned.1.call-start = ((), (), s32[]{:S(2)}) async-start(), calls=%async_computation.3 | async-start | bytes 1892352 | tf_op jit(solution)/shard_map/all_gather | solution.py:589
  23.0 21.9 %copy-start.31 = (bf16[2,768]{1,0:T(2,128)(2,1)S(1)}, bf16[2,768]{1,0:T(2,128)(2,1)}, u32[]{:S(2)}) copy-start(bf16[2,768]{1,0:T(2,128)(2,1)} %param.30) | copy-start | bytes 9220
  23.0 22.5 %copy-start.32 = (bf16[2,768]{1,0:T(2,128)(2,1)S(1)}, bf16[2,768]{1,0:T(2,128)(2,1)}, u32[]{:S(2)}) copy-start(bf16[2,768]{1,0:T(2,128)(2,1)} %param.34) | copy-start | bytes 9220
  23.0 23.1 %copy-start.23 = (bf16[2,3072]{1,0:T(2,128)(2,1)S(1)}, bf16[2,3072]{1,0:T(2,128)(2,1)}, u32[]{:S(2)}) copy-start(bf16[2,3072]{1,0:T(2,128)(2,1)} %param.32) | copy-start | bytes 36868
  124.5 285.0 %reduce-scatter.5.cloned.1.call-start = ((), (), s32[]{:S(2)}) async-start(), calls=%async_computation.4 | async-start | bytes 14598144 | tf_op jit(solution)/shard_map/reduce_scatter | solution.py:605
  157.5 37.0 %copy-start.36 = (bf16[1024,768]{1,0:T(8,128)(2,1)S(1)}, bf16[1024,768]{1,0:T(8,128)(2,1)}, u32[]{:S(2)}) copy-start(bf16[1024,768]{1,0:T(8,128)(2,1)} %get-tuple-element.121) | copy-start | bytes 4718596
  231.3 21.8 %copy-start.34 = (bf16[1024,768]{1,0:T(8,128)(2,1)S(1)}, bf16[1024,768]{1,0:T(8,128)(2,1)}, u32[]{:S(2)}) copy-start(bf16[1024,768]{1,0:T(8,128)(2,1)} %get-tuple-element.137) | copy-start | bytes 4718596
  277.7 8.4 %collective-permute-start = (bf16[4,2,2,192,768]{4,3,2,1,0:T(8,128)(2,1)}, bf16[4,2,2,192,768]{4,3,2,1,0:T(8,128)(2,1)}, u32[]{:S(2)}, u32[]{:S(2)}) collective-permute-start(bf16[4,2,2,192,768]{4,3,2,1,0:T(8,128)(2,1)} %pad_maximum_fusion.1), channel_id=1, source_target_pairs={{0,1},{1,0},{2,3},{3,2},{4,5},{5,4},{6,7},{7,6},{8,9},{9,8},{10,11... | collective-permute-start | bytes 14155784 | tf_op jit(solution)/shard_map/ppermute | solution.py:237
  295.0 47.3 %collective-permute-start.1 = (bf16[4,2,96,768]{3,2,1,0:T(8,128)(2,1)}, bf16[4,2,96,768]{3,2,1,0:T(8,128)(2,1)}, u32[]{:S(2)}, u32[]{:S(2)}) collective-permute-start(bf16[4,2,96,768]{3,2,1,0:T(8,128)(2,1)} %fusion.1), channel_id=1, source_target_pairs={{0,2},{1,3},{2,0},{3,1},{4,6},{5,7},{6,4},{7,5},{8,10},{9,11},{10,... | collective-permute-start | bytes 3538952 | tf_op jit(solution)/shard_map/ppermute | solution.py:237
  298.2 44.1 %collective-permute-start.2 = (bf16[4,2,96,768]{3,2,1,0:T(8,128)(2,1)}, bf16[4,2,96,768]{3,2,1,0:T(8,128)(2,1)}, u32[]{:S(2)}, u32[]{:S(2)}) collective-permute-start(bf16[4,2,96,768]{3,2,1,0:T(8,128)(2,1)} %fusion), channel_id=1, source_target_pairs={{0,4},{1,5},{2,6},{3,7},{4,0},{5,1},{6,2},{7,3},{8,12},{9,13},{10,... | collective-permute-start | bytes 3538952 | tf_op jit(solution)/shard_map/ppermute | solution.py:237
  346.0 23.3 %collective-permute-start.3 = (bf16[4,96,768]{2,1,0:T(8,128)(2,1)S(1)}, bf16[4,96,768]{2,1,0:T(8,128)(2,1)S(1)}, u32[]{:S(2)}, u32[]{:S(2)}) collective-permute-start(bf16[4,96,768]{2,1,0:T(8,128)(2,1)S(1)} %fusion.7), channel_id=1, source_target_pairs={{0,4},{1,5},{2,6},{3,7},{4,0},{5,1},{6,2},{7,3},{8,12},{9,13},{10,... | collective-permute-start | bytes 1769480 | tf_op jit(solution)/shard_map/ppermute | solution.py:237
  346.8 22.5 %collective-permute-start.4 = (bf16[4,96,768]{2,1,0:T(8,128)(2,1)S(1)}, bf16[4,96,768]{2,1,0:T(8,128)(2,1)S(1)}, u32[]{:S(2)}, u32[]{:S(2)}) collective-permute-start(bf16[4,96,768]{2,1,0:T(8,128)(2,1)S(1)} %fusion.6), channel_id=1, source_target_pairs={{0,2},{1,3},{2,0},{3,1},{4,6},{5,7},{6,4},{7,5},{8,10},{9,11},{10,... | collective-permute-start | bytes 1769480 | tf_op jit(solution)/shard_map/ppermute | solution.py:237
  392.9 9.8 %collective-permute-start.5 = (bf16[4,2,2,104,768]{4,3,2,1,0:T(8,128)(2,1)}, bf16[4,2,2,104,768]{4,3,2,1,0:T(8,128)(2,1)}, u32[]{:S(2)}, u32[]{:S(2)}) collective-permute-start(bf16[4,2,2,104,768]{4,3,2,1,0:T(8,128)(2,1)} %pad_maximum_fusion.3), channel_id=1, source_target_pairs={{0,1},{1,0},{2,3},{3,2},{4,5},{5,4},{6,7},{7,6},{8,9},{9,8},{10,11... | collective-permute-start | bytes 7667720 | tf_op jit(solution)/shard_map/ppermute | solution.py:237
  398.3 32.1 %collective-permute-start.8 = (bf16[192,768]{1,0:T(8,128)(2,1)}, bf16[192,768]{1,0:T(8,128)(2,1)S(1)}, u32[]{:S(2)}, u32[]{:S(2)}) collective-permute-start(bf16[192,768]{1,0:T(8,128)(2,1)} %pad_maximum_fusion.7), channel_id=1, source_target_pairs={{0,8},{1,9},{2,10},{3,11},{4,12},{5,13},{6,14},{7,15},{8,0},{9,1},... | collective-permute-start | bytes 884744 | tf_op jit(solution)/shard_map/ppermute | solution.py:237
  400.0 30.4 %collective-permute-start.9 = (bf16[192,768]{1,0:T(8,128)(2,1)}, bf16[192,768]{1,0:T(8,128)(2,1)}, u32[]{:S(2)}, u32[]{:S(2)}) collective-permute-start(bf16[192,768]{1,0:T(8,128)(2,1)} %pad_maximum_fusion.8), channel_id=1, source_target_pairs={{0,16},{1,17},{2,18},{3,19},{4,20},{5,21},{6,22},{7,23},{8,24},{9,... | collective-permute-start | bytes 884744 | tf_op jit(solution)/shard_map/ppermute | solution.py:237
  402.6 27.8 %collective-permute-start.10 = (bf16[192,768]{1,0:T(8,128)(2,1)}, bf16[192,768]{1,0:T(8,128)(2,1)}, u32[]{:S(2)}, u32[]{:S(2)}) collective-permute-start(bf16[192,768]{1,0:T(8,128)(2,1)} %pad_maximum_fusion.9), channel_id=1, source_target_pairs={{0,24},{1,25},{2,26},{3,27},{4,28},{5,29},{6,30},{7,31},{8,16},{9,... | collective-permute-start | bytes 884744 | tf_op jit(solution)/shard_map/ppermute | solution.py:237
  408.5 15.5 %collective-permute-start.7 = (bf16[4,2,48,768]{3,2,1,0:T(8,128)(2,1)}, bf16[4,2,48,768]{3,2,1,0:T(8,128)(2,1)}, u32[]{:S(2)}, u32[]{:S(2)}) collective-permute-start(bf16[4,2,48,768]{3,2,1,0:T(8,128)(2,1)} %fusion.5), channel_id=1, source_target_pairs={{0,4},{1,5},{2,6},{3,7},{4,0},{5,1},{6,2},{7,3},{8,12},{9,13},{10,... | collective-permute-start | bytes 1769480 | tf_op jit(solution)/shard_map/ppermute | solution.py:237
  409.5 16.8 %collective-permute-start.6 = (bf16[4,2,56,768]{3,2,1,0:T(8,128)(2,1)S(1)}, bf16[4,2,56,768]{3,2,1,0:T(8,128)(2,1)}, u32[]{:S(2)}, u32[]{:S(2)}) collective-permute-start(bf16[4,2,56,768]{3,2,1,0:T(8,128)(2,1)S(1)} %fusion.2), channel_id=1, source_target_pairs={{0,2},{1,3},{2,0},{3,1},{4,6},{5,7},{6,4},{7,5},{8,10},{9,11},{10,... | collective-permute-start | bytes 2064392 | tf_op jit(solution)/shard_map/ppermute | solution.py:237
  428.7 8.8 %collective-permute-start.11 = (bf16[4,56,768]{2,1,0:T(8,128)(2,1)S(1)}, bf16[4,56,768]{2,1,0:T(8,128)(2,1)S(1)}, u32[]{:S(2)}, u32[]{:S(2)}) collective-permute-start(bf16[4,56,768]{2,1,0:T(8,128)(2,1)S(1)} %fusion.9), channel_id=1, source_target_pairs={{0,4},{1,5},{2,6},{3,7},{4,0},{5,1},{6,2},{7,3},{8,12},{9,13},{10,... | collective-permute-start | bytes 1032200 | tf_op jit(solution)/shard_map/ppermute | solution.py:237
  430.0 7.4 %collective-permute-start.12 = (bf16[4,48,768]{2,1,0:T(8,128)(2,1)S(1)}, bf16[4,48,768]{2,1,0:T(8,128)(2,1)S(1)}, u32[]{:S(2)}, u32[]{:S(2)}) collective-permute-start(bf16[4,48,768]{2,1,0:T(8,128)(2,1)S(1)} %fusion.12), channel_id=1, source_target_pairs={{0,2},{1,3},{2,0},{3,1},{4,6},{5,7},{6,4},{7,5},{8,10},{9,11},{10,... | collective-permute-start | bytes 884744 | tf_op jit(solution)/shard_map/ppermute | solution.py:237
  439.9 8.0 %collective-permute-start.13 = (bf16[104,768]{1,0:T(8,128)(2,1)S(1)}, bf16[104,768]{1,0:T(8,128)(2,1)S(1)}, u32[]{:S(2)}, u32[]{:S(2)}) collective-permute-start(bf16[104,768]{1,0:T(8,128)(2,1)S(1)} %pad_maximum_fusion.10), channel_id=1, source_target_pairs={{0,8},{1,9},{2,10},{3,11},{4,12},{5,13},{6,14},{7,15},{8,0},{9,1},... | collective-permute-start | bytes 479240 | tf_op jit(solution)/shard_map/ppermute | solution.py:237
  440.3 13.5 %collective-permute-start.14 = (bf16[104,768]{1,0:T(8,128)(2,1)S(1)}, bf16[104,768]{1,0:T(8,128)(2,1)S(1)}, u32[]{:S(2)}, u32[]{:S(2)}) collective-permute-start(bf16[104,768]{1,0:T(8,128)(2,1)S(1)} %pad_maximum_fusion.11), channel_id=1, source_target_pairs={{0,16},{1,17},{2,18},{3,19},{4,20},{5,21},{6,22},{7,23},{8,24},{9,... | collective-permute-start | bytes 479240 | tf_op jit(solution)/shard_map/ppermute | solution.py:237
  443.8 10.0 %collective-permute-start.15 = (bf16[104,768]{1,0:T(8,128)(2,1)S(1)}, bf16[104,768]{1,0:T(8,128)(2,1)S(1)}, u32[]{:S(2)}, u32[]{:S(2)}) collective-permute-start(bf16[104,768]{1,0:T(8,128)(2,1)S(1)} %pad_maximum_fusion.12), channel_id=1, source_target_pairs={{0,24},{1,25},{2,26},{3,27},{4,28},{5,29},{6,30},{7,31},{8,16},{9,... | collective-permute-start | bytes 479240 | tf_op jit(solution)/shard_map/ppermute | solution.py:237
  (40 other events, 216.2 us)
Sparse Core Ops, SparseCore 0:
  13.3 100.6 reduce-scatter.2
  124.6 58.4 all-gather.1
  221.2 184.9 reduce-scatter.4
